TPU v7x, 32 devices: a whole 2x2x4 slice. The times are simulated.
32 devices in a mesh: shard: 16 (over z, y, x), rep: 2 (over core).
Axes of the slice: x: 2, y: 2, z: 4, core: 2. Of those that a mesh axis runs over, the one named last changes fastest.
Arguments:
- tokens: bfloat16 [65536, 768], P(('shard', 'rep')), may hold values from -6 to 6
- grad_out: bfloat16 [65536, 768], P(('shard', 'rep')), may hold values from -6 to 6
- first_gain: bfloat16 [768], P('shard'), may hold values from 0.5 to 1.5
- first_shift: bfloat16 [768], P('shard'), may hold values from -3 to 3
- query_proj: bfloat16 [768, 768], P('shard'), may hold values from -0.21875 to 0.21875
- query_bias: bfloat16 [768], P('shard'), may hold values from -3 to 3
- key_proj: bfloat16 [768, 768], P('shard'), may hold values from -0.21875 to 0.21875
- value_proj: bfloat16 [768, 768], P('shard'), may hold values from -0.21875 to 0.21875
- value_bias: bfloat16 [768], P('shard'), may hold values from -3 to 3
- output_proj: bfloat16 [768, 768], P('shard'), may hold values from -0.875 to 0.875
- output_bias: bfloat16 [768], P('shard'), may hold values from -3 to 3
- second_gain: bfloat16 [768], P('shard'), may hold values from 0.5 to 1.5
- second_shift: bfloat16 [768], P('shard'), may hold values from -3 to 3
- hidden_proj: bfloat16 [768, 3072], P('shard'), may hold values from -0.21875 to 0.21875
- hidden_bias: bfloat16 [3072], P('shard'), may hold values from -3 to 3
- final_proj: bfloat16 [3072, 768], P('shard'), may hold values from -0.109375 to 0.109375
- final_bias: bfloat16 [768], P('shard'), may hold values from -3 to 3
- threshold: float32 [12], replicated, may hold values from 0.5 to 3
Outputs:
- layer_output: bfloat16 [65536, 768], P(('shard', 'rep'))
- grad_tokens: bfloat16 [65536, 768], P(('shard', 'rep'))
- grad_first_gain: float32 [768], P('shard')
- grad_first_shift: float32 [768], P('shard')
- grad_query_proj: float32 [768, 768], P('shard')
- grad_query_bias: float32 [768], P('shard')
- grad_key_proj: float32 [768, 768], P('shard')
- grad_value_proj: float32 [768, 768], P('shard')
- grad_value_bias: float32 [768], P('shard')
- grad_output_proj: float32 [768, 768], P('shard')
- grad_output_bias: float32 [768], P('shard')
- grad_second_gain: float32 [768], P('shard')
- grad_second_shift: float32 [768], P('shard')
- grad_hidden_proj: float32 [768, 3072], P('shard')
- grad_hidden_bias: float32 [3072], P('shard')
- grad_final_proj: float32 [3072, 768], P('shard')
- grad_final_bias: float32 [768], P('shard')
- head_max: float32 [12], replicated
- clip_factor: float32 [12], replicated
- clipped_query: float32 [768, 768], P('shard')
- clipped_query_bias: float32 [768], P('shard')
- clipped_key: float32 [768, 768], P('shard')
All inputs are finite; a program needn't handle non-finite values.
Results may differ from a plain program's by a relative error of at most 0.019.
Values may be sent and summed in bfloat16 or wider, within the bound.
A program may use at most 256 MiB of HBM per device.

v0:
```python
import math

import jax
import jax.numpy as jnp
from jax import lax
from jax.sharding import PartitionSpec as P

FRAMES = 16


EPSILON = 1e-06


def layer_norm(values, gain, shift):
    centred = values - jnp.mean(values, axis=-1, keepdims=True)
    scaled = centred * lax.rsqrt(jnp.mean(centred * centred, axis=-1, keepdims=True) + EPSILON)
    return scaled * gain + shift


def inner_left(left, right):
    return lax.dot_general(
        left, right, (((0,), (0,)), ((), ())), preferred_element_type=jnp.float32
    )


def inner_right(left, right):
    return lax.dot_general(
        left, right, (((1,), (1,)), ((), ())), preferred_element_type=jnp.float32
    )


def column_sum(values):
    return jnp.sum(values.astype(jnp.float32), axis=0)


def on_device(
    tokens,
    grad_out,
    first_gain,
    first_shift,
    query_proj,
    query_bias,
    key_proj,
    value_proj,
    value_bias,
    output_proj,
    output_bias,
    second_gain,
    second_shift,
    hidden_proj,
    hidden_bias,
    final_proj,
    final_bias,
    threshold,
):
    everything = (
        lax.all_gather(first_gain, "shard", axis=0, tiled=True),
        lax.all_gather(first_shift, "shard", axis=0, tiled=True),
        lax.all_gather(query_proj, "shard", axis=0, tiled=True),
        lax.all_gather(query_bias, "shard", axis=0, tiled=True),
        lax.all_gather(key_proj, "shard", axis=0, tiled=True),
        lax.all_gather(value_proj, "shard", axis=0, tiled=True),
        lax.all_gather(value_bias, "shard", axis=0, tiled=True),
        lax.all_gather(output_proj, "shard", axis=0, tiled=True),
        lax.all_gather(output_bias, "shard", axis=0, tiled=True),
        lax.all_gather(second_gain, "shard", axis=0, tiled=True),
        lax.all_gather(second_shift, "shard", axis=0, tiled=True),
        lax.all_gather(hidden_proj, "shard", axis=0, tiled=True),
        lax.all_gather(hidden_bias, "shard", axis=0, tiled=True),
        lax.all_gather(final_proj, "shard", axis=0, tiled=True),
        lax.all_gather(final_bias, "shard", axis=0, tiled=True),
    )
    attn_full = everything[:9]
    mlp_full = everything[9:]
    (
        gain_one,
        shift_one,
        query_full,
        qbias_full,
        key_full,
        value_full,
        vbias_full,
        output_full,
        obias_full,
    ) = attn_full
    gain_two, shift_two, hidden_full, hbias_full, final_full, fbias_full = mlp_full
    heads = threshold.shape[0]
    width = query_full.shape[1]
    head_dim = width // heads
    rows = tokens.shape[0]
    places = rows // FRAMES
    scale = 1.0 / math.sqrt(head_dim)
    shape_four = (places, FRAMES, heads, head_dim)
    tok_float = tokens.astype(jnp.float32)
    normed_one, norm_one_back = jax.vjp(
        layer_norm, tok_float, gain_one.astype(jnp.float32), shift_one.astype(jnp.float32)
    )
    inputs_one = normed_one.astype(jnp.bfloat16)
    queries = (
        (
            jnp.dot(inputs_one, query_full, preferred_element_type=jnp.float32)
            + qbias_full.astype(jnp.float32)
        )
        .astype(jnp.bfloat16)
        .reshape(shape_four)
    )
    keys_low = (
        jnp.dot(inputs_one, key_full, preferred_element_type=jnp.float32)
        .astype(jnp.bfloat16)
        .reshape(shape_four)
    )
    values_low = (
        (
            jnp.dot(inputs_one, value_full, preferred_element_type=jnp.float32)
            + vbias_full.astype(jnp.float32)
        )
        .astype(jnp.bfloat16)
        .reshape(shape_four)
    )
    scores = (
        jnp.einsum("pfhd,pghd->phfg", queries, keys_low, preferred_element_type=jnp.float32) * scale
    )
    local_max = jnp.max(scores, axis=(0, 2, 3))
    global_max = lax.pmax(local_max, ("shard", "rep"))
    row_top = jnp.max(scores, axis=-1, keepdims=True)
    expo = jnp.exp(scores - row_top)
    row_total = jnp.sum(expo, axis=-1, keepdims=True)
    probs = expo / row_total
    log_total = row_top + jnp.log(row_total)
    mixed = jnp.einsum(
        "phfg,pghd->pfhd",
        probs.astype(jnp.bfloat16),
        values_low,
        preferred_element_type=jnp.float32,
    )
    mixed_low = mixed.reshape(rows, width).astype(jnp.bfloat16)
    attended = jnp.dot(
        mixed_low, output_full, preferred_element_type=jnp.float32
    ) + obias_full.astype(jnp.float32)
    middle = tok_float + attended
    normed_two, norm_two_back = jax.vjp(
        layer_norm, middle, gain_two.astype(jnp.float32), shift_two.astype(jnp.float32)
    )
    inputs_two = normed_two.astype(jnp.bfloat16)
    hidden_pre = jnp.dot(
        inputs_two, hidden_full, preferred_element_type=jnp.float32
    ) + hbias_full.astype(jnp.float32)
    activated, gelu_back = jax.vjp(jax.nn.gelu, hidden_pre)
    act_low = activated.astype(jnp.bfloat16)
    result = middle + (
        jnp.dot(act_low, final_full, preferred_element_type=jnp.float32)
        + fbias_full.astype(jnp.float32)
    )
    layer_output = result.astype(jnp.bfloat16)
    upstream = grad_out.astype(jnp.float32)
    final_wgrad = inner_left(act_low, grad_out)
    fbias_grad = jnp.sum(upstream, axis=0)
    act_grad = inner_right(grad_out, final_full)
    hidden_grad = gelu_back(act_grad)[0].astype(jnp.bfloat16)
    hbias_grad = column_sum(hidden_grad)
    hidden_wgrad = inner_left(inputs_two, hidden_grad)
    two_grad = inner_right(hidden_grad, hidden_full)
    middle_back, gain_two_grad, shift_two_grad = norm_two_back(two_grad)
    middle_grad = upstream + middle_back
    branch_grad = middle_grad.astype(jnp.bfloat16)
    obias_grad = column_sum(branch_grad)
    output_wgrad = inner_left(mixed_low, branch_grad)
    mixed_grad = inner_right(branch_grad, output_full).astype(jnp.bfloat16).reshape(shape_four)
    scores_again = (
        jnp.einsum("pfhd,pghd->phfg", queries, keys_low, preferred_element_type=jnp.float32) * scale
    )
    probs_again = jnp.exp(scores_again - log_total)
    value_grad = (
        jnp.einsum(
            "phfg,pfhd->pghd",
            probs_again.astype(jnp.bfloat16),
            mixed_grad,
            preferred_element_type=jnp.float32,
        )
        .astype(jnp.bfloat16)
        .reshape(rows, width)
    )
    prob_grad = jnp.einsum(
        "pfhd,pghd->phfg", mixed_grad, values_low, preferred_element_type=jnp.float32
    )
    score_grad = (
        probs_again * (prob_grad - jnp.sum(prob_grad * probs_again, axis=-1, keepdims=True))
    ).astype(jnp.bfloat16)
    query_grad = (
        (
            jnp.einsum("phfg,pghd->pfhd", score_grad, keys_low, preferred_element_type=jnp.float32)
            * scale
        )
        .astype(jnp.bfloat16)
        .reshape(rows, width)
    )
    key_grad = (
        (
            jnp.einsum("phfg,pfhd->pghd", score_grad, queries, preferred_element_type=jnp.float32)
            * scale
        )
        .astype(jnp.bfloat16)
        .reshape(rows, width)
    )
    qbias_grad = column_sum(query_grad)
    vbias_grad = column_sum(value_grad)
    query_wgrad = inner_left(inputs_one, query_grad)
    key_wgrad = inner_left(inputs_one, key_grad)
    value_wgrad = inner_left(inputs_one, value_grad)
    one_grad = (
        inner_right(query_grad, query_full)
        + inner_right(key_grad, key_full)
        + inner_right(value_grad, value_full)
    )
    token_back, gain_one_grad, shift_one_grad = norm_one_back(one_grad)
    grad_tokens = (middle_grad + token_back).astype(jnp.bfloat16)
    owned = (
        lax.psum_scatter(
            gain_one_grad.astype(jnp.bfloat16), "shard", scatter_dimension=0, tiled=True
        ).astype(jnp.float32),
        lax.psum_scatter(
            shift_one_grad.astype(jnp.bfloat16), "shard", scatter_dimension=0, tiled=True
        ).astype(jnp.float32),
        lax.psum_scatter(
            query_wgrad.astype(jnp.bfloat16), "shard", scatter_dimension=0, tiled=True
        ).astype(jnp.float32),
        lax.psum_scatter(
            qbias_grad.astype(jnp.bfloat16), "shard", scatter_dimension=0, tiled=True
        ).astype(jnp.float32),
        lax.psum_scatter(
            key_wgrad.astype(jnp.bfloat16), "shard", scatter_dimension=0, tiled=True
        ).astype(jnp.float32),
        lax.psum_scatter(
            value_wgrad.astype(jnp.bfloat16), "shard", scatter_dimension=0, tiled=True
        ).astype(jnp.float32),
        lax.psum_scatter(
            vbias_grad.astype(jnp.bfloat16), "shard", scatter_dimension=0, tiled=True
        ).astype(jnp.float32),
        lax.psum_scatter(
            output_wgrad.astype(jnp.bfloat16), "shard", scatter_dimension=0, tiled=True
        ).astype(jnp.float32),
        lax.psum_scatter(
            obias_grad.astype(jnp.bfloat16), "shard", scatter_dimension=0, tiled=True
        ).astype(jnp.float32),
        lax.psum_scatter(
            gain_two_grad.astype(jnp.bfloat16), "shard", scatter_dimension=0, tiled=True
        ).astype(jnp.float32),
        lax.psum_scatter(
            shift_two_grad.astype(jnp.bfloat16), "shard", scatter_dimension=0, tiled=True
        ).astype(jnp.float32),
        lax.psum_scatter(
            hidden_wgrad.astype(jnp.bfloat16), "shard", scatter_dimension=0, tiled=True
        ).astype(jnp.float32),
        lax.psum_scatter(
            hbias_grad.astype(jnp.bfloat16), "shard", scatter_dimension=0, tiled=True
        ).astype(jnp.float32),
        lax.psum_scatter(
            final_wgrad.astype(jnp.bfloat16), "shard", scatter_dimension=0, tiled=True
        ).astype(jnp.float32),
        lax.psum_scatter(
            fbias_grad.astype(jnp.bfloat16), "shard", scatter_dimension=0, tiled=True
        ).astype(jnp.float32),
    )
    (
        own_gone,
        own_sone,
        own_query,
        own_qbias,
        own_key,
        own_value,
        own_vbias,
        own_output,
        own_obias,
        own_gtwo,
        own_stwo,
        own_hidden,
        own_hbias,
        own_final,
        own_fbias,
    ) = owned
    summed = (
        lax.psum(own_gone.astype(jnp.bfloat16), "rep").astype(jnp.float32),
        lax.psum(own_sone.astype(jnp.bfloat16), "rep").astype(jnp.float32),
        lax.psum(own_query.astype(jnp.bfloat16), "rep").astype(jnp.float32),
        lax.psum(own_qbias.astype(jnp.bfloat16), "rep").astype(jnp.float32),
        lax.psum(own_key.astype(jnp.bfloat16), "rep").astype(jnp.float32),
        lax.psum(own_value.astype(jnp.bfloat16), "rep").astype(jnp.float32),
        lax.psum(own_vbias.astype(jnp.bfloat16), "rep").astype(jnp.float32),
        lax.psum(own_output.astype(jnp.bfloat16), "rep").astype(jnp.float32),
        lax.psum(own_obias.astype(jnp.bfloat16), "rep").astype(jnp.float32),
        lax.psum(own_gtwo.astype(jnp.bfloat16), "rep").astype(jnp.float32),
        lax.psum(own_stwo.astype(jnp.bfloat16), "rep").astype(jnp.float32),
        lax.psum(own_hidden.astype(jnp.bfloat16), "rep").astype(jnp.float32),
        lax.psum(own_hbias.astype(jnp.bfloat16), "rep").astype(jnp.float32),
        lax.psum(own_final.astype(jnp.bfloat16), "rep").astype(jnp.float32),
        lax.psum(own_fbias.astype(jnp.bfloat16), "rep").astype(jnp.float32),
    )
    factor = jnp.minimum(1.0, threshold / global_max)
    column_scale = jnp.repeat(jnp.sqrt(factor), head_dim)
    clipped_query = query_proj.astype(jnp.float32) * column_scale[None, :]
    clipped_key = key_proj.astype(jnp.float32) * column_scale[None, :]
    shard_rows = query_bias.shape[0]
    bias_scale = lax.dynamic_slice_in_dim(
        column_scale, lax.axis_index("shard") * shard_rows, shard_rows
    )
    clipped_query_bias = query_bias.astype(jnp.float32) * bias_scale
    return (
        layer_output,
        grad_tokens,
        summed[0],
        summed[1],
        summed[2],
        summed[3],
        summed[4],
        summed[5],
        summed[6],
        summed[7],
        summed[8],
        summed[9],
        summed[10],
        summed[11],
        summed[12],
        summed[13],
        summed[14],
        global_max,
        factor,
        clipped_query,
        clipped_query_bias,
        clipped_key,
    )


def solution(mesh):
    in_specs = (
        P(("shard", "rep"), None),
        P(("shard", "rep"), None),
        P("shard"),
        P("shard"),
        P("shard", None),
        P("shard"),
        P("shard", None),
        P("shard", None),
        P("shard"),
        P("shard", None),
        P("shard"),
        P("shard"),
        P("shard"),
        P("shard", None),
        P("shard"),
        P("shard", None),
        P("shard"),
        P(),
    )
    out_specs = (
        P(("shard", "rep"), None),
        P(("shard", "rep"), None),
        P("shard"),
        P("shard"),
        P("shard", None),
        P("shard"),
        P("shard", None),
        P("shard", None),
        P("shard"),
        P("shard", None),
        P("shard"),
        P("shard"),
        P("shard"),
        P("shard", None),
        P("shard"),
        P("shard", None),
        P("shard"),
        P(),
        P(),
        P("shard", None),
        P("shard"),
        P("shard", None),
    )
    return jax.shard_map(
        on_device, mesh=mesh, in_specs=in_specs, out_specs=out_specs, check_vma=False
    )
```

profile of v0, /device:TPU:0, one launch (start us, length us, event | category | flops | bytes accessed | tf_op | source)
XLA Modules:
  0.0 1388.3 jit_solution(17855083184984079179)
XLA Ops:
  20.6 78.9 %all-reduce.19 = (bf16[768]{0:T(1024)(128)(2,1)S(1)}, bf16[768]{0:T(1024)(128)(2,1)S(1)}, bf16[768]{0:T(1024)(128)(2,1)S(1)}, bf16[768]{0:T(1024)(128)(2,1)S(1)}...) all-reduce(bf16[768]{0:T(1024)(128)(2,1)S(1)} %dynamic-update-slice, ...), channel_id=1, replica_groups=mesh['shard'=16,'rep'=2] {'shard'}, use_global_device_ids=true, to_apply=%add.1 | all-reduce | flops 8448 | bytes 33792
  146.8 12.6 multiply_reduce_fusion.2
  159.4 26.1 %all-gather.7.cloned.1.call-done = bf16[768,768]{1,0:T(8,128)(2,1)} async-done(((bf16[48,768]{1,0:T(8,128)(2,1)}), bf16[768,768]{1,0:T(8,128)(2,1)}) %all-gather.7.cloned.1.call-update) | async-done | bytes 1179664 | tf_op jit(solution)/shard_map/all_gather | solution.py:62
  202.7 14.2 %multiply_reduce_fusion.1 = (f32[12]{0:T(128)}, f32[128,12,16]{2,1,0:T(8,128)}) fusion(f32[128,12,16,16]{2,3,1,0:T(8,128)} %get-tuple-element.140, f32[128,12,16]{2,1,0:T(8,128)} %get-tuple-element.139), kind=kLoop, calls=%fused_computation.28 | loop fusion | flops 1548276 | bytes 1769520 | tf_op jit(solution)/shard_map/reduce_max | solution.py:123
  216.8 12.3 convert_bitcast_fusion.1
  238.6 11.1 convert_element_type.237
  258.9 66.3 %all-gather.15.cloned.1.call-done = bf16[768,3072]{1,0:T(8,128)(2,1)} async-done(((bf16[48,3072]{1,0:T(8,128)(2,1)}), bf16[768,3072]{1,0:T(8,128)(2,1)}) %all-gather.15.cloned.1.call-update) | async-done | bytes 4718608 | tf_op jit(solution)/shard_map/all_gather | solution.py:68
  325.2 26.9 %multiply_convert_fusion = (bf16[2048,3072]{1,0:T(8,128)(2,1)}, f32[2048,3072]{1,0:T(8,128)}) fusion(f32[3072]{0:T(1024)S(1)} %convert_element_type.242, bf16[768,3072]{1,0:T(8,128)(2,1)} %all-gather.15.cloned.1.call-done, f32[2048,768]{0,1:T(8,128)} %copy-done.4, f32[768]{0:T(1024)S(1)} %convert_element_type.240, f32[768]{0:T(1024)S(1)} %convert_element_type.239, ...), kind=kOutput, calls=%fused_computation.9 | convolution fusion | flops 9734455296 | bytes 48793600 | tf_op jit(solution)/shard_map/dot_general | solution.py:145
  352.2 54.8 %all-gather.17.cloned.1.call-done = bf16[3072,768]{1,0:T(8,128)(2,1)} async-done(((bf16[192,768]{1,0:T(8,128)(2,1)}), bf16[3072,768]{1,0:T(8,128)(2,1)}) %all-gather.17.cloned.1.call-update) | async-done | bytes 4718608 | tf_op jit(solution)/shard_map/all_gather | solution.py:70
  407.0 34.0 %fusion.66 = (bf16[3072]{0:T(1024)(128)(2,1)}, bf16[2048,3072]{1,0:T(8,128)(2,1)}) fusion(f32[2048,3072]{1,0:T(8,128)} %get-tuple-element.144, f32[3072]{0:T(1024)S(1)} %convert_element_type.242, bf16[2048,768]{1,0:T(8,128)(2,1)} %param.19, bf16[3072,768]{1,0:T(8,128)(2,1)} %all-gather.17.cloned.1.call-done), kind=kOutput, calls=%fused_computation.104 | convolution fusion | flops 9802085376 | bytes 45631488 | tf_op jit(solution)/shard_map/dot_general | solution.py:27
  441.1 15.1 %fusion.65 = (bf16[768]{0:T(1024)(128)(2,1)}, f32[2048,768]{1,0:T(8,128)}) fusion(bf16[2048,3072]{1,0:T(8,128)(2,1)} %get-tuple-element.155, bf16[768,3072]{1,0:T(8,128)(2,1)S(1)} %bitcast.50), kind=kOutput, calls=%fused_computation.103 | convolution fusion | flops 9665248256 | bytes 23594496 | tf_op jit(solution)/shard_map/dot_general | solution.py:27
  492.2 16.5 %multiply_reduce_fusion = (f32[128,12,16]{2,1,0:T(8,128)}, f32[128,12,16,16]{2,3,1,0:T(8,128)}) fusion(f32[128,12,16,16]{2,3,1,0:T(8,128)} %get-tuple-element.140, f32[128,12,16]{2,1,0:T(8,128)S(1)} %log_add_fusion, bf16[128,16,12,64]{3,2,1,0:T(8,128)(2,1)} %reshape.151, bf16[128,16,12,64]{3,2,1,0:T(8,128)(2,1)} %reshape.154), kind=kOutput, calls=%fused_computation.13 | convolution fusion | flops 51879936 | bytes 9633792 | tf_op jit(solution)/shard_map/pfhd,pghd->phfg/dot_general | solution.py:183
  519.2 11.7 fusion.23
  540.4 11.1 reshape.156
  572.3 11.2 reshape.155
  629.7 16.5 %convolution_convert_fusion.1 = bf16[768,3072]{1,0:T(8,128)(2,1)} fusion(bf16[2048,3072]{1,0:T(8,128)(2,1)} %get-tuple-element.155, f32[2048,768]{0,1:T(8,128)} %copy-done.4, f32[768]{0:T(1024)S(1)} %copy-done.33, f32[768]{0:T(1024)S(1)} %convert_element_type.239, f32[2048]{0:T(1024)S(1)} %fusion.52, f32[2048]{0:T(1024)S(1)} %broadcast_multiply_fusion), kind=kOutput, calls=%fused_computation.56 | convolution fusion | flops 9673900032 | bytes 23615488 | tf_op jit(solution)/shard_map/dot_general | solution.py:21
  646.3 14.6 %convolution_convert_fusion = bf16[3072,768]{1,0:T(8,128)(2,1)} fusion(bf16[2048,3072]{1,0:T(8,128)(2,1)} %get-tuple-element.143, bf16[2048,768]{1,0:T(8,128)(2,1)S(1)} %copy-done.10), kind=kOutput, calls=%fused_computation.55 | convolution fusion | flops 9666035712 | bytes 20447232 | tf_op jit(solution)/shard_map/dot_general | solution.py:21
  663.1 39.4 %pmax.7 = f32[12]{0:T(128)S(1)} all-reduce(f32[12]{0:T(128)S(1)} %copy-done.35), channel_id=1, replica_groups=mesh['shard'=16,'rep'=2] {'shard','rep'}, use_global_device_ids=true, to_apply=%region_51.0 | all-reduce | flops 12 | bytes 96 | tf_op jit(solution)/shard_map/pmax | solution.py:124
  721.9 76.4 %all-reduce.18 = (bf16[768]{0:T(1024)(128)(2,1)S(1)}, bf16[768]{0:T(1024)(128)(2,1)S(1)}, bf16[768]{0:T(1024)(128)(2,1)S(1)}, bf16[768]{0:T(1024)(128)(2,1)S(1)}...) all-reduce(bf16[768]{0:T(1024)(128)(2,1)S(1)} %dynamic-update-slice, ...), channel_id=1, replica_groups=mesh['shard'=16,'rep'=2] {'shard'}, use_global_device_ids=true, to_apply=%add.8 | all-reduce | flops 9984 | bytes 39936
  806.4 16.5 %add_convert_fusion.1 = bf16[2048,768]{0,1:T(8,128)(2,1)} fusion(f32[2048,768]{0,1:T(8,128)} %copy-done.4, bf16[2048,3072]{1,0:T(8,128)(2,1)} %get-tuple-element.143, bf16[3072,768]{1,0:T(8,128)(2,1)} %all-gather.17.cloned.1.call-done, f32[768]{0:T(1024)S(1)} %convert_element_type.244), kind=kOutput, calls=%fused_computation.47 | convolution fusion | flops 9668395008 | bytes 26741760 | tf_op jit(solution)/shard_map/dot_general | solution.py:151
  822.9 114.6 %reduce-scatter.13.cloned.1.call-done = bf16[48,768]{1,0:T(8,128)(2,1)} async-done(((bf16[768,768]{1,0:T(8,128)(2,1)}), bf16[48,768]{1,0:T(8,128)(2,1)}) %reduce-scatter.13.cloned.1.call-update) | async-done | bytes 73744 | tf_op jit(solution)/shard_map/reduce_scatter | solution.py:239
  937.5 127.9 %reduce-scatter.11.cloned.1.call-done = bf16[48,768]{1,0:T(8,128)(2,1)} async-done(((bf16[768,768]{1,0:T(8,128)(2,1)}), bf16[48,768]{1,0:T(8,128)(2,1)}) %reduce-scatter.11.cloned.1.call-update) | async-done | bytes 73744 | tf_op jit(solution)/shard_map/reduce_scatter | solution.py:233
  1065.4 142.1 %reduce-scatter.15.cloned.1.call-done = bf16[48,3072]{1,0:T(8,128)(2,1)} async-done(((bf16[768,3072]{1,0:T(8,128)(2,1)}), bf16[48,3072]{1,0:T(8,128)(2,1)}) %reduce-scatter.15.cloned.1.call-update) | async-done | bytes 294928 | tf_op jit(solution)/shard_map/reduce_scatter | solution.py:251
  1207.5 142.5 %reduce-scatter.17.cloned.1.call-done = bf16[192,768]{1,0:T(8,128)(2,1)} async-done(((bf16[3072,768]{1,0:T(8,128)(2,1)}), bf16[192,768]{1,0:T(8,128)(2,1)}) %reduce-scatter.17.cloned.1.call-update) | async-done | bytes 294928 | tf_op jit(solution)/shard_map/reduce_scatter | solution.py:257
  (234 shorter events, 277.3 us)
Async XLA Ops:
  7.2 105.2 %all-gather.9.cloned.1.call-start = ((), (), s32[]{:S(2)}) async-start(), calls=%async_computation.7 | async-start | bytes 1253376 | tf_op jit(solution)/shard_map/all_gather | solution.py:59
  7.9 121.8 %all-gather.11.cloned.1.call-start = ((), (), s32[]{:S(2)}) async-start(), calls=%async_computation.8 | async-start | bytes 1253376 | tf_op jit(solution)/shard_map/all_gather | solution.py:61
  8.7 176.8 %all-gather.7.cloned.1.call-start = ((), (), s32[]{:S(2)}) async-start(), calls=%async_computation.6 | async-start | bytes 1253376 | tf_op jit(solution)/shard_map/all_gather | solution.py:62
  9.4 240.4 %all-gather.13.cloned.1.call-start = ((), (), s32[]{:S(2)}) async-start(), calls=%async_computation.9 | async-start | bytes 1253376 | tf_op jit(solution)/shard_map/all_gather | solution.py:64
  10.0 315.3 %all-gather.15.cloned.1.call-start = ((), (), s32[]{:S(2)}) async-start(), calls=%async_computation.10 | async-start | bytes 5013504 | tf_op jit(solution)/shard_map/all_gather | solution.py:68
  10.6 396.4 %all-gather.17.cloned.1.call-start = ((), (), s32[]{:S(2)}) async-start(), calls=%async_computation.11 | async-start | bytes 5013504 | tf_op jit(solution)/shard_map/all_gather | solution.py:70
  11.1 811.7 %reduce-scatter.9.cloned.1.call-start = ((), (), s32[]{:S(2)}) async-start(), calls=%async_computation.13 | async-start | bytes 1253376 | tf_op jit(solution)/shard_map/reduce_scatter | solution.py:230
  102.7 147.1 %copy-start = (bf16[2048,768]{0,1:T(8,128)(2,1)}, bf16[2048,768]{0,1:T(8,128)(2,1)S(1)}, u32[]{:S(2)}) copy-start(bf16[2048,768]{0,1:T(8,128)(2,1)S(1)} %copy.84) | copy-start | bytes 9437188
  104.7 220.5 %copy-start.32 = (f32[768]{0:T(1024)}, f32[768]{0:T(1024)S(1)}, u32[]{:S(2)}) copy-start(f32[768]{0:T(1024)S(1)} %convert_element_type.240) | copy-start | bytes 9220
  325.2 115.8 %slice-start.2 = ((s8[4718592]{0:T(1024)(128)(4,1)}), s8[524288]{0:T(1024)(128)(4,1)S(1)}, s32[]{:S(2)}) async-start(s8[4718592]{0:T(1024)(128)(4,1)} %bitcast.49), calls=%async_computation.21 | async-start | bytes 1048576
  407.0 34.1 %slice-start.3 = ((s8[4718592]{0:T(1024)(128)(4,1)}), s8[4194304]{0:T(1024)(128)(4,1)S(1)}, s32[]{:S(2)}) async-start(s8[4718592]{0:T(1024)(128)(4,1)} %bitcast.49), calls=%async_computation.22 | async-start | bytes 8388608
  456.2 14.2 %slice-start = ((s8[6291456]{0:T(1024)(128)(4,1)}), s8[2097152]{0:T(1024)(128)(4,1)S(1)}, s32[]{:S(2)}) async-start(s8[6291456]{0:T(1024)(128)(4,1)} %bitcast.47), calls=%async_computation.19 | async-start | bytes 4194304
  558.0 264.8 %reduce-scatter.7.cloned.1.call-start = ((), (), s32[]{:S(2)}) async-start(), calls=%async_computation.12 | async-start | bytes 1253376 | tf_op jit(solution)/shard_map/reduce_scatter | solution.py:224
  590.0 347.5 %reduce-scatter.13.cloned.1.call-start = ((), (), s32[]{:S(2)}) async-start(), calls=%async_computation.15 | async-start | bytes 1253376 | tf_op jit(solution)/shard_map/reduce_scatter | solution.py:239
  596.6 468.8 %reduce-scatter.11.cloned.1.call-start = ((), (), s32[]{:S(2)}) async-start(), calls=%async_computation.14 | async-start | bytes 1253376 | tf_op jit(solution)/shard_map/reduce_scatter | solution.py:233
  629.7 16.6 %copy-start.10 = (bf16[2048,768]{1,0:T(8,128)(2,1)S(1)}, bf16[2048,768]{1,0:T(8,128)(2,1)}, u32[]{:S(2)}) copy-start(bf16[2048,768]{1,0:T(8,128)(2,1)} %param.19) | copy-start | bytes 9437188
  629.7 577.9 %reduce-scatter.15.cloned.1.call-start = ((), (), s32[]{:S(2)}) async-start(), calls=%async_computation.16 | async-start | bytes 5013504 | tf_op jit(solution)/shard_map/reduce_scatter | solution.py:251
  646.2 703.8 %reduce-scatter.17.cloned.1.call-start = ((), (), s32[]{:S(2)}) async-start(), calls=%async_computation.17 | async-start | bytes 5013504 | tf_op jit(solution)/shard_map/reduce_scatter | solution.py:257
  660.9 41.6 %copy-start.36 = (f32[12]{0:T(128)S(1)}, f32[12]{0:T(128)}, u32[]{:S(2)}) copy-start(f32[12]{0:T(128)} %param.35) | copy-start | bytes 148
  660.9 42.2 %copy-start.37 = (bf16[48]{0:T(256)(128)(2,1)S(1)}, bf16[48]{0:T(256)(128)(2,1)}, u32[]{:S(2)}) copy-start(bf16[48]{0:T(256)(128)(2,1)} %param.23) | copy-start | bytes 292
  660.9 42.8 %copy-start.19 = (bf16[48,768]{1,0:T(8,128)(2,1)S(1)}, bf16[48,768]{1,0:T(8,128)(2,1)}, u32[]{:S(2)}) copy-start(bf16[48,768]{1,0:T(8,128)(2,1)} %param.22) | copy-start | bytes 221188
  660.9 42.8 %copy-start.20 = (bf16[48,768]{1,0:T(8,128)(2,1)S(1)}, bf16[48,768]{1,0:T(8,128)(2,1)}, u32[]{:S(2)}) copy-start(bf16[48,768]{1,0:T(8,128)(2,1)} %param.24) | copy-start | bytes 221188
  661.0 710.5 %all-reduce.24.cloned.1.call-start = ((), (), s32[]{:S(2)}) async-start(), calls=%async_computation.18 | async-start | bytes 1769472 | tf_op jit(solution)/shard_map/psum | solution.py:284
  806.4 543.6 %copy-start.26 = (f32[2048]{0:T(1024)S(1)}, f32[2048]{0:T(1024)}, u32[]{:S(2)}) copy-start(f32[2048]{0:T(1024)} %copy-done.25) | copy-start | bytes 24580
  (35 other events, 166.7 us)
Sparse Core Ops, SparseCore 0:
  10.8 59.0 all-gather.8
  72.7 54.9 all-gather.10
  130.5 54.9 all-gather.6
  188.2 54.9 all-gather.12
  245.9 79.3 all-gather.14
  327.9 79.0 all-gather.16
  558.2 122.8 reduce-scatter.8
  685.8 123.3 reduce-scatter.6
  814.0 123.3 reduce-scatter.12
  942.1 123.2 reduce-scatter.10
  1070.6 136.8 reduce-scatter.14
  1213.4 136.5 reduce-scatter.16
  1352.8 18.6 all-reduce.23
where the time goes:
time: 1400 us; the launch traced here: 1390 us
  waiting for transfers between devices  684 us (49%)
  matrix products  260 us (19%)
  blocking collectives  197 us (14%)
  local copies, waits for them, and re-layouts  160 us (11%)
  other arithmetic  68.5 us (5%)
  between operations  17.6 us (1%)
    unnamed x2, blocking collectives  155 us
    reduce_scatter x1, waiting for transfers between devices, on_device(): lax.psum_scatter(final_wgrad.astype(jnp.bfloat16), 'shard', scatter_dimen...  142 us
    reduce_scatter x1, waiting for transfers between devices, on_device(): lax.psum_scatter(hidden_wgrad.astype(jnp.bfloat16), 'shard', scatter_dime...  142 us
    reduce_scatter x1, waiting for transfers between devices, on_device(): lax.psum_scatter(value_wgrad.astype(jnp.bfloat16), 'shard', scatter_dimen...  128 us
    reduce_scatter x1, waiting for transfers between devices, on_device(): lax.psum_scatter(output_wgrad.astype(jnp.bfloat16), 'shard', scatter_dime...  115 us
    all_gather x1, waiting for transfers between devices, on_device(): lax.all_gather(hidden_proj, 'shard', axis=0, tiled=True)  66.3 us
    dot_general x6, matrix products, inner_right(): lax.dot_general(left, right, (((1,), (1,)), ((), ())), preferred_element_...  64.1 us
    dot_general x6, matrix products, inner_left(): lax.dot_general(left, right, (((0,), (0,)), ((), ())), preferred_element_...  57.3 us
  transfers between devices with their start and end apart: 13, of which 8 were waited for; matrix products, arithmetic and copies ran while one was open for 23% of the time, Pallas kernels for 0%

commit v1 on v0

v1 whole, which is shorter than its diff:
```python
import math

import jax
import jax.numpy as jnp
from jax import lax
from jax.experimental import pallas as pl
from jax.experimental.pallas import tpu as pltpu
from jax.sharding import PartitionSpec as P

FRAMES = 16
EPSILON = 1e-06
BF = jnp.bfloat16
F32 = jnp.float32
ROWS = 512
BLOCK = 128
PAIR = 128


def nn(left, right):
    return lax.dot_general(left, right, (((1,), (0,)), ((), ())), preferred_element_type=F32)


def nt(left, right):
    return lax.dot_general(left, right, (((1,), (1,)), ((), ())), preferred_element_type=F32)


def tn(left, right):
    return lax.dot_general(left, right, (((0,), (0,)), ((), ())), preferred_element_type=F32)


def normalise(values):
    centred = values - jnp.mean(values, axis=-1, keepdims=True)
    inverse = lax.rsqrt(jnp.mean(centred * centred, axis=-1, keepdims=True) + EPSILON)
    return centred * inverse, inverse


def norm_back(grad, unit, inverse, gain):
    scaled = grad * gain
    return inverse * (
        scaled
        - jnp.mean(scaled, axis=-1, keepdims=True)
        - unit * jnp.mean(scaled * unit, axis=-1, keepdims=True)
    )


def column_sum(values):
    return jnp.sum(values, axis=0, keepdims=True)


def place_masks():
    lane = lax.broadcasted_iota(jnp.int32, (FRAMES, 2 * BLOCK), 1)
    return [(lane % BLOCK) // FRAMES == p for p in range(BLOCK // FRAMES)]


def halves(width):
    lane = lax.broadcasted_iota(jnp.int32, (1, PAIR), 1)
    first = (lane < width).astype(F32)
    return first.astype(BF), (1.0 - first).astype(BF)


def compress(wide, masks):
    total = wide[:FRAMES]
    for p in range(1, len(masks)):
        total = jnp.where(masks[p], wide[p * FRAMES : (p + 1) * FRAMES], total)
    return total


def expand(packed, masks):
    zero = jnp.zeros_like(packed)
    return jnp.concatenate([jnp.where(m, packed, zero).astype(BF) for m in masks], axis=0)


def split(two, first, second):
    return jnp.concatenate([two * first, two * second], axis=0)


def stack(wide):
    return jnp.concatenate([wide[:, :BLOCK], wide[:, BLOCK:]], axis=0)


def attend_kernel(
    width, tok_ref, wq_ref, wk_ref, wv_ref, wo_ref, vec_ref,
    q_ref, k_ref, v_ref, p_ref, mix_ref, mid_ref, top_ref,
):
    scale = 1.0 / math.sqrt(width)
    gain, shift = vec_ref[0:1], vec_ref[1:2]
    tok = tok_ref[...].astype(F32)
    unit, _ = normalise(tok)
    one = (unit * gain + shift).astype(BF)
    q_ref[...] = (nn(one, wq_ref[...]) + vec_ref[2:3]).astype(BF)
    k_ref[...] = nn(one, wk_ref[...]).astype(BF)
    v_ref[...] = (nn(one, wv_ref[...]) + vec_ref[3:4]).astype(BF)
    masks = place_masks()
    first, second = halves(width)
    pairs = tok_ref.shape[1] // PAIR

    @pl.when(pl.program_id(0) == 0)
    def _():
        top_ref[...] = jnp.full(top_ref.shape, -3e38, F32)

    def body(i, carry):
        rows = pl.ds(pl.multiple_of(i * BLOCK, BLOCK), BLOCK)
        for h in range(pairs):
            cols = slice(h * PAIR, (h + 1) * PAIR)
            two_q, two_k, two_v = q_ref[rows, cols], k_ref[rows, cols], v_ref[rows, cols]
            scores = compress(nt(two_k, split(two_q, first, second)), masks) * scale
            top_ref[h] = jnp.maximum(top_ref[h], scores)
            expo = jnp.exp(scores - jnp.max(scores, axis=0, keepdims=True))
            probs = expo / jnp.sum(expo, axis=0, keepdims=True)
            p_ref[i, h] = probs
            mixed = tn(stack(expand(probs, masks)), split(two_v, first, second))
            mix_ref[rows, cols] = mixed.astype(BF)
        return carry

    lax.fori_loop(0, tok_ref.shape[0] // BLOCK, body, 0)
    mid_ref[...] = tok + (nn(mix_ref[...], wo_ref[...]) + vec_ref[4:5])


def mlp_kernel(
    chunk, mid_ref, dy_ref, w1_ref, w2_ref, vec_ref, hb_ref,
    out_ref, mg_ref, w1g_ref, w2g_ref, vg_ref, hbg_ref,
    acc1, acc2, res_ref, two_ref,
):
    step, last = pl.program_id(0), pl.num_programs(0) - 1
    gain, shift = vec_ref[5:6], vec_ref[6:7]
    mid = mid_ref[...]
    unit, inverse = normalise(mid)
    inp = (unit * gain + shift).astype(BF)
    dy = dy_ref[...]
    hidden = w1_ref.shape[1]

    @pl.when(step == 0)
    def _():
        acc1[...] = jnp.zeros_like(acc1)
        acc2[...] = jnp.zeros_like(acc2)
        vg_ref[...] = jnp.zeros_like(vg_ref)
        hbg_ref[...] = jnp.zeros_like(hbg_ref)

    res_ref[...] = mid + vec_ref[7:8]
    two_ref[...] = jnp.zeros_like(two_ref)
    root = math.sqrt(2.0 / math.pi)

    def body(j, carry):
        cols = pl.ds(pl.multiple_of(j * chunk, chunk), chunk)
        z = nn(inp, w1_ref[:, cols]) + hb_ref[:, cols]
        act_grad = nt(dy, w2_ref[cols, :])
        square = z * z
        bend = jnp.tanh(root * z * (1.0 + 0.044715 * square))
        half = 0.5 * (1.0 + bend)
        act = (z * half).astype(BF)
        slope = half + 0.5 * z * (1.0 - bend * bend) * (root * (1.0 + 0.134145 * square))
        grad = (act_grad * slope).astype(BF)
        res_ref[...] += nn(act, w2_ref[cols, :])
        two_ref[...] += nt(grad, w1_ref[:, cols])
        acc2[cols, :] += tn(act, dy)
        acc1[:, cols] += tn(inp, grad)
        hbg_ref[:, cols] += column_sum(grad.astype(F32))
        return carry

    lax.fori_loop(0, hidden // chunk, body, 0)
    out_ref[...] = res_ref[...].astype(BF)
    two = two_ref[...]
    up = dy.astype(F32)
    mg_ref[...] = up + norm_back(two, unit, inverse, gain)
    vg_ref[0:1] += column_sum(two * unit)
    vg_ref[1:2] += column_sum(two)
    vg_ref[2:3] += column_sum(up)

    @pl.when(step == last)
    def _():
        w1g_ref[...] = acc1[...].astype(BF)
        w2g_ref[...] = acc2[...].astype(BF)


def back_kernel(
    width, tok_ref, mg_ref, q_ref, k_ref, v_ref, p_ref, mix_ref,
    wq_ref, wk_ref, wv_ref, wo_ref, vec_ref,
    gt_ref, wqg_ref, wkg_ref, wvg_ref, wog_ref, vg_ref,
    accq, acck, accv, acco, mgl_ref, dq_ref, dk_ref, dv_ref,
):
    step, last = pl.program_id(0), pl.num_programs(0) - 1
    scale = 1.0 / math.sqrt(width)
    gain, shift = vec_ref[0:1], vec_ref[1:2]
    accs = (accq, acck, accv, acco)

    @pl.when(step == 0)
    def _():
        for acc in accs:
            acc[...] = jnp.zeros_like(acc)
        vg_ref[...] = jnp.zeros_like(vg_ref)

    branch = mg_ref[...].astype(BF)
    mgl_ref[...] = nt(branch, wo_ref[...]).astype(BF)
    acco[...] += tn(mix_ref[...], branch)
    vg_ref[4:5] += column_sum(branch.astype(F32))
    masks = place_masks()
    first, second = halves(width)
    pairs = tok_ref.shape[1] // PAIR

    def body(i, carry):
        rows = pl.ds(pl.multiple_of(i * BLOCK, BLOCK), BLOCK)
        for h in range(pairs):
            cols = slice(h * PAIR, (h + 1) * PAIR)
            two_q, two_k, two_v = q_ref[rows, cols], k_ref[rows, cols], v_ref[rows, cols]
            mixed = split(mgl_ref[rows, cols], first, second)
            probs = p_ref[i, h]
            slope = compress(nt(two_v, mixed), masks)
            score = probs * (slope - jnp.sum(slope * probs, axis=0, keepdims=True))
            wide = expand(score, masks)
            dv_ref[rows, cols] = nn(expand(probs, masks), mixed).astype(BF)
            dk_ref[rows, cols] = (nn(wide, split(two_q, first, second)) * scale).astype(BF)
            dq_ref[rows, cols] = (tn(stack(wide), split(two_k, first, second)) * scale).astype(BF)
        return carry

    lax.fori_loop(0, tok_ref.shape[0] // BLOCK, body, 0)
    unit, inverse = normalise(tok_ref[...].astype(F32))
    one = (unit * gain + shift).astype(BF)
    dq, dk, dv = dq_ref[...], dk_ref[...], dv_ref[...]
    vg_ref[2:3] += column_sum(dq.astype(F32))
    vg_ref[3:4] += column_sum(dv.astype(F32))
    accq[...] += tn(one, dq)
    acck[...] += tn(one, dk)
    accv[...] += tn(one, dv)
    grad = nt(dq, wq_ref[...]) + nt(dk, wk_ref[...]) + nt(dv, wv_ref[...])
    vg_ref[0:1] += column_sum(grad * unit)
    vg_ref[1:2] += column_sum(grad)
    gt_ref[...] = (mg_ref[...] + norm_back(grad, unit, inverse, gain)).astype(BF)

    @pl.when(step == last)
    def _():
        for out, acc in zip((wqg_ref, wkg_ref, wvg_ref, wog_ref), accs):
            out[...] = acc[...].astype(BF)


def whole(shape):
    return pl.BlockSpec(shape, lambda i: (0,) * len(shape), pipeline_mode=pl.Buffered(1))


def tiles(height, width):
    return pl.BlockSpec((height, width), lambda i: (i, 0))


def shaped(shape, dtype):
    return jax.ShapeDtypeStruct(shape, dtype)


VMEM_LIMIT = 60 * 1024 * 1024


def params():
    return pltpu.CompilerParams(
        dimension_semantics=("arbitrary",), vmem_limit_bytes=VMEM_LIMIT
    )


def attend(tokens, wq, wk, wv, wo, vec, heads):
    rows, d = tokens.shape
    t = min(ROWS, rows)
    pairs = d // PAIR
    blocks = rows // BLOCK
    big = tiles(t, d)
    w = whole((d, d))
    return pl.pallas_call(
        lambda *refs: attend_kernel(d // heads, *refs),
        grid=(rows // t,),
        in_specs=[big, w, w, w, w, whole(vec.shape)],
        out_specs=[
            big, big, big,
            pl.BlockSpec((t // BLOCK, pairs, FRAMES, 2 * BLOCK), lambda i: (i, 0, 0, 0)),
            big, big,
            whole((pairs, FRAMES, 2 * BLOCK)),
        ],
        out_shape=[shaped((rows, d), BF)] * 3
        + [shaped((blocks, pairs, FRAMES, 2 * BLOCK), F32), shaped((rows, d), BF), shaped((rows, d), F32)]
        + [shaped((pairs, FRAMES, 2 * BLOCK), F32)],
        compiler_params=params(),
        cost_estimate=pl.CostEstimate(flops=10 * rows * d * d, bytes_accessed=24 * rows * d, transcendentals=0),
        name="attend",
    )(tokens, wq, wk, wv, wo, vec)


def mlp(middle, dy, w1, w2, vec, hb):
    rows, d = middle.shape
    hidden = w1.shape[1]
    t = min(ROWS, rows)
    big = tiles(t, d)
    return pl.pallas_call(
        lambda *refs: mlp_kernel(768, *refs),
        grid=(rows // t,),
        in_specs=[big, big, whole(w1.shape), whole(w2.shape), whole(vec.shape), whole(hb.shape)],
        out_specs=[big, big, whole(w1.shape), whole(w2.shape), whole((8, d)), whole((1, hidden))],
        out_shape=[
            shaped((rows, d), BF), shaped((rows, d), F32), shaped(w1.shape, BF), shaped(w2.shape, BF),
            shaped((8, d), F32), shaped((1, hidden), F32),
        ],
        scratch_shapes=[
            pltpu.VMEM(w1.shape, F32), pltpu.VMEM(w2.shape, F32), pltpu.VMEM((t, d), F32), pltpu.VMEM((t, d), F32),
        ],
        compiler_params=params(),
        cost_estimate=pl.CostEstimate(flops=12 * rows * d * hidden, bytes_accessed=14 * rows * d, transcendentals=0),
        name="mlp",
    )(middle, dy, w1, w2, vec, hb)


def back(tokens, mg, q, k, v, p, mixed, wq, wk, wv, wo, vec, heads):
    rows, d = tokens.shape
    t = min(ROWS, rows)
    pairs = d // PAIR
    big = tiles(t, d)
    w = whole((d, d))
    return pl.pallas_call(
        lambda *refs: back_kernel(d // heads, *refs),
        grid=(rows // t,),
        in_specs=[
            big, big, big, big, big,
            pl.BlockSpec((t // BLOCK, pairs, FRAMES, 2 * BLOCK), lambda i: (i, 0, 0, 0)),
            big, w, w, w, w, whole(vec.shape),
        ],
        out_specs=[big, w, w, w, w, whole((8, d))],
        out_shape=[shaped((rows, d), BF)] + [shaped((d, d), BF)] * 4 + [shaped((8, d), F32)],
        scratch_shapes=[pltpu.VMEM((d, d), F32)] * 4 + [pltpu.VMEM((t, d), BF)] * 4,
        compiler_params=params(),
        cost_estimate=pl.CostEstimate(flops=20 * rows * d * d, bytes_accessed=24 * rows * d, transcendentals=0),
        name="back",
    )(tokens, mg, q, k, v, p, mixed, wq, wk, wv, wo, vec)


def on_device(
    tokens, grad_out, first_gain, first_shift, query_proj, query_bias, key_proj, value_proj, value_bias,
    output_proj, output_bias, second_gain, second_shift, hidden_proj, hidden_bias, final_proj, final_bias, threshold,
):
    def gather(x):
        return lax.all_gather(x, "shard", axis=0, tiled=True)

    heads = threshold.shape[0]
    wq, wk, wv, wo = (gather(x) for x in (query_proj, key_proj, value_proj, output_proj))
    small = (first_gain, first_shift, query_bias, value_bias, output_bias, second_gain, second_shift, final_bias)
    vec = jnp.stack([gather(x) for x in small]).astype(F32)
    hb = gather(hidden_bias).astype(F32)[None]
    w1, w2 = gather(hidden_proj), gather(final_proj)
    q, k, v, p, mixed, middle, top = attend(tokens, wq, wk, wv, wo, vec, heads)
    head_dim = tokens.shape[1] // heads
    local = jnp.max(top.reshape(top.shape[0], FRAMES, 2, BLOCK), axis=(1, 3)).reshape(heads)
    global_max = lax.pmax(local, ("shard", "rep"))
    layer_output, mg, w1g, w2g, vg2, hbg = mlp(middle, grad_out, w1, w2, vec, hb)
    grad_tokens, wqg, wkg, wvg, wog, vg1 = back(tokens, mg, q, k, v, p, mixed, wq, wk, wv, wo, vec, heads)

    def scatter(x):
        y = lax.psum_scatter(x.astype(BF), "shard", scatter_dimension=0, tiled=True)
        return lax.psum(y, "rep").astype(F32)

    factor = jnp.minimum(1.0, threshold / global_max)
    column_scale = jnp.repeat(jnp.sqrt(factor), head_dim)
    shard_rows = query_bias.shape[0]
    bias_scale = lax.dynamic_slice_in_dim(column_scale, lax.axis_index("shard") * shard_rows, shard_rows)
    return (
        layer_output, grad_tokens, scatter(vg1[0]), scatter(vg1[1]), scatter(wqg), scatter(vg1[2]), scatter(wkg),
        scatter(wvg), scatter(vg1[3]), scatter(wog), scatter(vg1[4]), scatter(vg2[0]), scatter(vg2[1]), scatter(w1g),
        scatter(hbg[0]), scatter(w2g), scatter(vg2[2]), global_max, factor,
        query_proj.astype(F32) * column_scale[None, :], query_bias.astype(F32) * bias_scale,
        key_proj.astype(F32) * column_scale[None, :],
    )


def solution(mesh):
    in_specs = (
        P(("shard", "rep"), None),
        P(("shard", "rep"), None),
        P("shard"),
        P("shard"),
        P("shard", None),
        P("shard"),
        P("shard", None),
        P("shard", None),
        P("shard"),
        P("shard", None),
        P("shard"),
        P("shard"),
        P("shard"),
        P("shard", None),
        P("shard"),
        P("shard", None),
        P("shard"),
        P(),
    )
    out_specs = (
        P(("shard", "rep"), None),
        P(("shard", "rep"), None),
        P("shard"),
        P("shard"),
        P("shard", None),
        P("shard"),
        P("shard", None),
        P("shard", None),
        P("shard"),
        P("shard", None),
        P("shard"),
        P("shard"),
        P("shard"),
        P("shard", None),
        P("shard"),
        P("shard", None),
        P("shard"),
        P(),
        P(),
        P("shard", None),
        P("shard"),
        P("shard", None),
    )
    return jax.shard_map(
        on_device, mesh=mesh, in_specs=in_specs, out_specs=out_specs, check_vma=False
    )
```

time: 1400 us -> 1440 us (1.029)
  waiting for transfers between devices: 684 us -> 1030 us
  matrix products: 260 us -> 0 us
  Pallas kernels: 0 us -> 170 us
  local copies, waits for them, and re-layouts: 160 us -> 10 us
  other arithmetic: 68.5 us -> 17.7 us
    dot_general x24 -> x0, matrix products: 260 us -> none  [the longest x6 64.1 us: inner_right(): lax.dot_general(left, right, (((1,), (1,)), ((), ())), preferred_element_...]
    reduce_scatter x6, waiting for transfers between devices: 527 us -> 747 us  [scatter(): y = lax.psum_scatter(x.astype(BF), 'shard', scatter_dimension=0, tiled=True)]
    pallas_call x0 -> x3, Pallas kernels: none -> 170 us  [the longest x1 84.2 us: mlp(): pl.pallas_call(lambda *refs: mlp_kernel(768, *refs), grid=(rows // t,), i...]
    all_gather x6, waiting for transfers between devices: 147 us -> 275 us  [gather(): return lax.all_gather(x, 'shard', axis=0, tiled=True)]
    reshape x7 -> x1, local copies, waits for them, and re-layouts: 74.5 us -> 0.08 us  [on_device(): jnp.max(top.reshape(top.shape[0], FRAMES, 2, BLOCK), axis=(1, 3))]
    convert_element_type x5 -> x0, local copies, waits for them, and re-layouts: 43.7 us -> none  [the longest x2 20.6 us: on_device(): mixed_low = mixed.reshape(rows, width).astype(jnp.bfloat16)]
    unnamed x124 -> x46, local copies, waits for them, and re-layouts: 34.6 us -> 9.59 us
    convert_element_type x27 -> x17, other arithmetic: 36.1 us -> 15.2 us  [the longest x15 14.5 us: scatter(): return lax.psum(y, 'rep').astype(F32)]
  transfers between devices with their start and end apart: 13 -> 13, of which waited for: 8 -> 11; matrix products, arithmetic and copies ran while one was open for 23% -> 1% of each run, Pallas kernels for 0% -> 2%
where the time goes in v1:
time: 1440 us
  waiting for transfers between devices  1030 us (72%)
  blocking collectives  196 us (14%)
  Pallas kernels  170 us (12%)
  other arithmetic  17.7 us (1%)
  between operations  16.8 us (1%)
    reduce_scatter x6, waiting for transfers between devices, scatter(): y = lax.psum_scatter(x.astype(BF), 'shard', scatter_dimension=0, tiled=True)  747 us
    all_gather x6, waiting for transfers between devices, gather(): return lax.all_gather(x, 'shard', axis=0, tiled=True)  275 us
    unnamed x2, blocking collectives  154 us
    pallas_call x1, Pallas kernels, mlp(): pl.pallas_call(lambda *refs: mlp_kernel(768, *refs), grid=(rows // t,), i...  84.2 us
    pallas_call x1, Pallas kernels, back(): pl.pallas_call(lambda *refs: back_kernel(d // heads, *refs), grid=(rows /...  55.8 us
    pmax x1, blocking collectives, on_device(): global_max = lax.pmax(local, ('shard', 'rep'))  39.4 us
    pallas_call x1, Pallas kernels, attend(): pl.pallas_call(lambda *refs: attend_kernel(d // heads, *refs), grid=(rows...  29.7 us
  transfers between devices with their start and end apart: 13, of which 11 were waited for; matrix products, arithmetic and copies ran while one was open for 1% of the time, Pallas kernels for 2%

profile of v1, /device:TPU:0, one launch (start us, length us, event | category | flops | bytes accessed | tf_op | source)
XLA Modules:
  0.0 1440.1 jit_solution(504136063349449209)
XLA Ops:
  21.4 79.0 %all-reduce.19 = (bf16[768]{0:T(1024)(128)(2,1)S(1)}, bf16[768]{0:T(1024)(128)(2,1)S(1)}, bf16[768]{0:T(1024)(128)(2,1)S(1)}, bf16[768]{0:T(1024)(128)(2,1)S(1)}...) all-reduce(bf16[768]{0:T(1024)(128)(2,1)S(1)} %dynamic-update-slice, ...), channel_id=1, replica_groups=mesh['shard'=16,'rep'=2] {'shard'}, use_global_device_ids=true, to_apply=%add | all-reduce | flops 9216 | bytes 36864
  101.8 25.9 %all-gather.13.cloned.1.call-done.refs_4_.refs_10_ = bf16[768,768]{1,0:T(8,128)(2,1)} async-done(((bf16[48,768]{1,0:T(8,128)(2,1)}), bf16[768,768]{1,0:T(8,128)(2,1)}) %all-gather.13.cloned.1.call-update) | async-done | bytes 1179664 | tf_op jit(solution)/shard_map/all_gather | solution.py:333
  127.7 57.8 %all-gather.7.cloned.1.call-done.refs_1_.refs_7_ = bf16[768,768]{1,0:T(8,128)(2,1)} async-done(((bf16[48,768]{1,0:T(8,128)(2,1)}), bf16[768,768]{1,0:T(8,128)(2,1)}) %all-gather.7.cloned.1.call-update) | async-done | bytes 1179664 | tf_op jit(solution)/shard_map/all_gather | solution.py:333
  185.5 57.7 %all-gather.9.cloned.1.call-done.refs_2_.refs_8_ = bf16[768,768]{1,0:T(8,128)(2,1)} async-done(((bf16[48,768]{1,0:T(8,128)(2,1)}), bf16[768,768]{1,0:T(8,128)(2,1)}) %all-gather.9.cloned.1.call-update) | async-done | bytes 1179664 | tf_op jit(solution)/shard_map/all_gather | solution.py:333
  243.2 29.7 %attend.1 = (bf16[2048,768]{1,0:T(8,128)(2,1)}, bf16[2048,768]{1,0:T(8,128)(2,1)}, bf16[2048,768]{1,0:T(8,128)(2,1)}, f32[16,6,16,256]{3,2,1,0:T(8,128)}, bf16[2...) custom-call(bf16[2048,768]{1,0:T(8,128)(2,1)} %refs_0_.3, ...), custom_call_target="tpu_custom_call" | custom-call | flops 12079595520 | bytes 37748736 | tf_op jit(solution)/shard_map/attend/pallas_call | solution.py:263
  272.9 52.2 %all-gather.15.cloned.1.call-done.refs_2_ = bf16[768,3072]{1,0:T(8,128)(2,1)} async-done(((bf16[48,3072]{1,0:T(8,128)(2,1)}), bf16[768,3072]{1,0:T(8,128)(2,1)}) %all-gather.15.cloned.1.call-update) | async-done | bytes 4718608 | tf_op jit(solution)/shard_map/all_gather | solution.py:333
  325.1 81.8 %all-gather.17.cloned.1.call-done.refs_3_ = bf16[3072,768]{1,0:T(8,128)(2,1)} async-done(((bf16[192,768]{1,0:T(8,128)(2,1)}), bf16[3072,768]{1,0:T(8,128)(2,1)}) %all-gather.17.cloned.1.call-update) | async-done | bytes 4718608 | tf_op jit(solution)/shard_map/all_gather | solution.py:333
  406.9 84.2 %mlp.1 = (bf16[2048,768]{1,0:T(8,128)(2,1)}, f32[2048,768]{1,0:T(8,128)}, bf16[768,3072]{1,0:T(8,128)(2,1)}, bf16[3072,768]{1,0:T(8,128)(2,1)}, f32[8,768]{1,0:T(8,128)}, /*index=5*/f32[1,3072]{1,0:T(1,128)}) custom-call(f32[2048,768]{1,0:T(8,128)} %get-tuple-element.41.refs_0_, bf16[2048,768]{1,0:T(8,128)(2,1)} %refs_1_.1, ...), custom_call_target="tpu_custom_call" | custom-call | flops 57982058496 | bytes 22020096 | tf_op jit(solution)/shard_map/mlp/pallas_call | solution.py:287
  491.0 55.8 %back.1 = (bf16[2048,768]{1,0:T(8,128)(2,1)}, bf16[768,768]{1,0:T(8,128)(2,1)}, bf16[768,768]{1,0:T(8,128)(2,1)}, bf16[768,768]{1,0:T(8,128)(2,1)}, bf16[768,768]{1,0:T(8,128)(2,1)}, /*index=5*/f32[8,768]{1,0:T(8,128)}) custom-call(bf16[2048,768]{1,0:T(8,128)(2,1)} %refs_0_.3, f32[2048,768]{1,0:T(8,128)} %get-tuple-element.43.refs_1_, ...), custom_call_target="tpu_custom_call" | custom-call | flops 24159191040 | bytes 37748736 | tf_op jit(solution)/shard_map/back/pallas_call | solution.py:311
  551.9 39.4 %pmax.7 = f32[12]{0:T(128)S(1)} all-reduce(f32[12]{0:T(128)S(1)} %reshape.60), channel_id=1, replica_groups=mesh['shard'=16,'rep'=2] {'shard','rep'}, use_global_device_ids=true, to_apply=%region_32.33 | all-reduce | flops 12 | bytes 96 | tf_op jit(solution)/shard_map/pmax | solution.py:344
  591.4 78.7 %reduce-scatter.11.cloned.1.call-done = bf16[48,768]{1,0:T(8,128)(2,1)} async-done(((bf16[768,768]{1,0:T(8,128)(2,1)}), bf16[48,768]{1,0:T(8,128)(2,1)}) %reduce-scatter.11.cloned.1.call-update) | async-done | bytes 73744 | tf_op jit(solution)/shard_map/reduce_scatter | solution.py:349
  670.1 128.2 %reduce-scatter.13.cloned.1.call-done = bf16[48,768]{1,0:T(8,128)(2,1)} async-done(((bf16[768,768]{1,0:T(8,128)(2,1)}), bf16[48,768]{1,0:T(8,128)(2,1)}) %reduce-scatter.13.cloned.1.call-update) | async-done | bytes 73744 | tf_op jit(solution)/shard_map/reduce_scatter | solution.py:349
  798.2 128.2 %reduce-scatter.7.cloned.1.call-done = bf16[48,768]{1,0:T(8,128)(2,1)} async-done(((bf16[768,768]{1,0:T(8,128)(2,1)}), bf16[48,768]{1,0:T(8,128)(2,1)}) %reduce-scatter.7.cloned.1.call-update) | async-done | bytes 73744 | tf_op jit(solution)/shard_map/reduce_scatter | solution.py:349
  926.4 128.0 %reduce-scatter.9.cloned.1.call-done = bf16[48,768]{1,0:T(8,128)(2,1)} async-done(((bf16[768,768]{1,0:T(8,128)(2,1)}), bf16[48,768]{1,0:T(8,128)(2,1)}) %reduce-scatter.9.cloned.1.call-update) | async-done | bytes 73744 | tf_op jit(solution)/shard_map/reduce_scatter | solution.py:349
  1054.5 141.9 %reduce-scatter.15.cloned.1.call-done = bf16[48,3072]{1,0:T(8,128)(2,1)} async-done(((bf16[768,3072]{1,0:T(8,128)(2,1)}), bf16[48,3072]{1,0:T(8,128)(2,1)}) %reduce-scatter.15.cloned.1.call-update) | async-done | bytes 294928 | tf_op jit(solution)/shard_map/reduce_scatter | solution.py:349
  1196.4 142.3 %reduce-scatter.17.cloned.1.call-done = bf16[192,768]{1,0:T(8,128)(2,1)} async-done(((bf16[3072,768]{1,0:T(8,128)(2,1)}), bf16[192,768]{1,0:T(8,128)(2,1)}) %reduce-scatter.17.cloned.1.call-update) | async-done | bytes 294928 | tf_op jit(solution)/shard_map/reduce_scatter | solution.py:349
  1340.8 75.1 %all-reduce.18 = (bf16[768]{0:T(1024)(128)(2,1)S(1)}, bf16[768]{0:T(1024)(128)(2,1)S(1)}, bf16[768]{0:T(1024)(128)(2,1)S(1)}, bf16[768]{0:T(1024)(128)(2,1)S(1)}...) all-reduce(bf16[768]{0:T(1024)(128)(2,1)S(1)} %get-tuple-element.10, ...), channel_id=2, replica_groups=mesh['shard'=16,'rep'=2] {'shard'}, use_global_device_ids=true, to_apply=%region_0.0.clone | all-reduce | flops 9216 | bytes 36864
  1416.6 2.5 all-reduce.20
  1423.7 1.8 convert_element_type.115
  1425.5 1.8 convert_element_type.119
  1427.3 1.6 convert_element_type.101
  1428.9 1.6 convert_element_type.104
  1430.4 1.6 convert_element_type.105
  1432.0 1.6 convert_element_type.108
  (107 shorter events, 25.1 us)
Async XLA Ops:
  7.2 94.6 %all-gather.11.cloned.1.call-start = ((), (), s32[]{:S(2)}) async-start(), calls=%async_computation.8 | async-start | bytes 1253376 | tf_op jit(solution)/shard_map/all_gather | solution.py:333
  7.9 119.8 %all-gather.13.cloned.1.call-start = ((), (), s32[]{:S(2)}) async-start(), calls=%async_computation.9 | async-start | bytes 1253376 | tf_op jit(solution)/shard_map/all_gather | solution.py:333
  8.7 176.9 %all-gather.7.cloned.1.call-start = ((), (), s32[]{:S(2)}) async-start(), calls=%async_computation.6 | async-start | bytes 1253376 | tf_op jit(solution)/shard_map/all_gather | solution.py:333
  9.4 233.8 %all-gather.9.cloned.1.call-start = ((), (), s32[]{:S(2)}) async-start(), calls=%async_computation.7 | async-start | bytes 1253376 | tf_op jit(solution)/shard_map/all_gather | solution.py:333
  10.0 315.1 %all-gather.15.cloned.1.call-start = ((), (), s32[]{:S(2)}) async-start(), calls=%async_computation.10 | async-start | bytes 5013504 | tf_op jit(solution)/shard_map/all_gather | solution.py:333
  10.6 396.3 %all-gather.17.cloned.1.call-start = ((), (), s32[]{:S(2)}) async-start(), calls=%async_computation.11 | async-start | bytes 5013504 | tf_op jit(solution)/shard_map/all_gather | solution.py:333
  11.1 658.9 %reduce-scatter.11.cloned.1.call-start = ((), (), s32[]{:S(2)}) async-start(), calls=%async_computation.14 | async-start | bytes 1253376 | tf_op jit(solution)/shard_map/reduce_scatter | solution.py:349
  546.9 251.3 %reduce-scatter.13.cloned.1.call-start = ((), (), s32[]{:S(2)}) async-start(), calls=%async_computation.15 | async-start | bytes 1253376 | tf_op jit(solution)/shard_map/reduce_scatter | solution.py:349
  547.7 378.7 %reduce-scatter.7.cloned.1.call-start = ((), (), s32[]{:S(2)}) async-start(), calls=%async_computation.12 | async-start | bytes 1253376 | tf_op jit(solution)/shard_map/reduce_scatter | solution.py:349
  548.4 506.0 %reduce-scatter.9.cloned.1.call-start = ((), (), s32[]{:S(2)}) async-start(), calls=%async_computation.13 | async-start | bytes 1253376 | tf_op jit(solution)/shard_map/reduce_scatter | solution.py:349
  549.0 647.4 %reduce-scatter.15.cloned.1.call-start = ((), (), s32[]{:S(2)}) async-start(), calls=%async_computation.16 | async-start | bytes 5013504 | tf_op jit(solution)/shard_map/reduce_scatter | solution.py:349
  549.7 2.0 copy-start.2
  549.7 788.9 %copy-start.6 = (f32[12]{0:T(128)S(1)}, f32[12]{0:T(128)}, u32[]{:S(2)}) copy-start(f32[12]{0:T(128)} %param.35) | copy-start | bytes 148
  549.8 789.6 %copy-start.7 = (bf16[48]{0:T(256)(128)(2,1)S(1)}, bf16[48]{0:T(256)(128)(2,1)}, u32[]{:S(2)}) copy-start(bf16[48]{0:T(256)(128)(2,1)} %param.23) | copy-start | bytes 292
  549.8 790.2 %copy-start = (bf16[48,768]{1,0:T(8,128)(2,1)S(1)}, bf16[48,768]{1,0:T(8,128)(2,1)}, u32[]{:S(2)}) copy-start(bf16[48,768]{1,0:T(8,128)(2,1)} %param.22) | copy-start | bytes 221188
  549.8 790.1 %copy-start.1 = (bf16[48,768]{1,0:T(8,128)(2,1)S(1)}, bf16[48,768]{1,0:T(8,128)(2,1)}, u32[]{:S(2)}) copy-start(bf16[48,768]{1,0:T(8,128)(2,1)} %param.24) | copy-start | bytes 221188
  549.8 790.9 %copy-start.4 = (f32[8,768]{1,0:T(8,128)S(1)}, f32[8,768]{1,0:T(8,128)}, u32[]{:S(2)}) copy-start(f32[8,768]{1,0:T(8,128)} %get-tuple-element.50) | copy-start | bytes 73732
  549.8 788.8 %reduce-scatter.17.cloned.1.call-start = ((), (), s32[]{:S(2)}) async-start(), calls=%async_computation.17 | async-start | bytes 5013504 | tf_op jit(solution)/shard_map/reduce_scatter | solution.py:349
  549.8 790.8 %copy-start.3 = (f32[8,768]{1,0:T(8,128)S(1)}, f32[8,768]{1,0:T(8,128)}, u32[]{:S(2)}) copy-start(f32[8,768]{1,0:T(8,128)} %get-tuple-element.55) | copy-start | bytes 73732
  549.9 790.8 %copy-start.5 = (f32[1,3072]{1,0:T(1,128)S(1)}, f32[1,3072]{1,0:T(1,128)}, u32[]{:S(2)}) copy-start(f32[1,3072]{1,0:T(1,128)} %get-tuple-element.57) | copy-start | bytes 36868
  550.4 873.3 %all-reduce.24.cloned.1.call-start = ((), (), s32[]{:S(2)}) async-start(), calls=%async_computation.18 | async-start | bytes 1769472 | tf_op jit(solution)/shard_map/psum | solution.py:350
  591.4 842.2 %copy-start.8 = (f32[12]{0:T(128)}, f32[12]{0:T(128)S(1)}, u32[]{:S(2)}) copy-start(f32[12]{0:T(128)S(1)} %pmax.7) | copy-start | bytes 148
Sparse Core Ops, SparseCore 0:
  10.8 59.1 all-gather.10
  72.9 54.7 all-gather.12
  130.5 54.9 all-gather.6
  188.2 54.9 all-gather.8
  245.9 79.1 all-gather.14
  327.8 79.0 all-gather.16
  547.0 122.9 reduce-scatter.10
  674.8 123.3 reduce-scatter.12
  803.0 123.3 reduce-scatter.6
  931.0 123.3 reduce-scatter.8
  1059.6 136.6 reduce-scatter.14
  1202.2 136.3 reduce-scatter.16
  1341.4 18.8 all-reduce.23

commit v2 on v1

--- a/solution.py
+++ b/solution.py
@@ -1,3 +1,4 @@
+import functools
 import math
 
 import jax
@@ -78,18 +79,24 @@
     return jnp.concatenate([wide[:, :BLOCK], wide[:, BLOCK:]], axis=0)
 
 
+def square(ref):
+    value = ref[...]
+    return value.reshape(-1, value.shape[-1])
+
+
 def attend_kernel(
-    width, tok_ref, wq_ref, wk_ref, wv_ref, wo_ref, vec_ref,
+    width, tok_ref, w_refs, vec_ref,
     q_ref, k_ref, v_ref, p_ref, mix_ref, mid_ref, top_ref,
 ):
     scale = 1.0 / math.sqrt(width)
+    wq, wk, wv, wo = (square(w) for w in w_refs)
     gain, shift = vec_ref[0:1], vec_ref[1:2]
     tok = tok_ref[...].astype(F32)
     unit, _ = normalise(tok)
     one = (unit * gain + shift).astype(BF)
-    q_ref[...] = (nn(one, wq_ref[...]) + vec_ref[2:3]).astype(BF)
-    k_ref[...] = nn(one, wk_ref[...]).astype(BF)
-    v_ref[...] = (nn(one, wv_ref[...]) + vec_ref[3:4]).astype(BF)
+    q_ref[...] = (nn(one, wq) + vec_ref[2:3]).astype(BF)
+    k_ref[...] = nn(one, wk).astype(BF)
+    v_ref[...] = (nn(one, wv) + vec_ref[3:4]).astype(BF)
     masks = place_masks()
     first, second = halves(width)
     pairs = tok_ref.shape[1] // PAIR
@@ -113,7 +120,7 @@
         return carry
 
     lax.fori_loop(0, tok_ref.shape[0] // BLOCK, body, 0)
-    mid_ref[...] = tok + (nn(mix_ref[...], wo_ref[...]) + vec_ref[4:5])
+    mid_ref[...] = tok + (nn(mix_ref[...], wo) + vec_ref[4:5])
 
 
 def mlp_kernel(
@@ -174,14 +181,15 @@
 
 def back_kernel(
     width, tok_ref, mg_ref, q_ref, k_ref, v_ref, p_ref, mix_ref,
-    wq_ref, wk_ref, wv_ref, wo_ref, vec_ref,
-    gt_ref, wqg_ref, wkg_ref, wvg_ref, wog_ref, vg_ref,
+    w_refs, vec_ref,
+    gt_ref, wg_refs, vg_ref,
     accq, acck, accv, acco, mgl_ref, dq_ref, dk_ref, dv_ref,
 ):
     step, last = pl.program_id(0), pl.num_programs(0) - 1
     scale = 1.0 / math.sqrt(width)
     gain, shift = vec_ref[0:1], vec_ref[1:2]
     accs = (accq, acck, accv, acco)
+    wq, wk, wv, wo = (square(w) for w in w_refs)
 
     @pl.when(step == 0)
     def _():
@@ -190,7 +198,7 @@
         vg_ref[...] = jnp.zeros_like(vg_ref)
 
     branch = mg_ref[...].astype(BF)
-    mgl_ref[...] = nt(branch, wo_ref[...]).astype(BF)
+    mgl_ref[...] = nt(branch, wo).astype(BF)
     acco[...] += tn(mix_ref[...], branch)
     vg_ref[4:5] += column_sum(branch.astype(F32))
     masks = place_masks()
@@ -221,15 +229,20 @@
     accq[...] += tn(one, dq)
     acck[...] += tn(one, dk)
     accv[...] += tn(one, dv)
-    grad = nt(dq, wq_ref[...]) + nt(dk, wk_ref[...]) + nt(dv, wv_ref[...])
+    grad = nt(dq, wq) + nt(dk, wk) + nt(dv, wv)
     vg_ref[0:1] += column_sum(grad * unit)
     vg_ref[1:2] += column_sum(grad)
     gt_ref[...] = (mg_ref[...] + norm_back(grad, unit, inverse, gain)).astype(BF)
 
     @pl.when(step == last)
     def _():
-        for out, acc in zip((wqg_ref, wkg_ref, wvg_ref, wog_ref), accs):
-            out[...] = acc[...].astype(BF)
+        for i, acc in enumerate(accs):
+            value = acc[...].astype(BF)
+            if len(wg_refs) == 1:
+                rows = wg_refs[0].shape[1] // 4
+                wg_refs[0][:, i * rows : (i + 1) * rows, :] = value.reshape(-1, rows, value.shape[1])
+            else:
+                wg_refs[i][...] = value
 
 
 def whole(shape):
@@ -253,17 +266,30 @@
     )
 
 
-def attend(tokens, wq, wk, wv, wo, vec, heads):
+def weight_specs(weights):
+    if len(weights) == 1:
+        shards, rows, d = weights[0].shape
+        return [
+            pl.BlockSpec((shards, rows // 4, d), lambda i, j=j: (0, j, 0), pipeline_mode=pl.Buffered(1))
+            for j in range(4)
+        ]
+    return [whole(w.shape) for w in weights]
+
+
+def four(weights):
+    return tuple(weights) * (4 // len(weights))
+
+
+def attend(tokens, weights, vec, heads):
     rows, d = tokens.shape
     t = min(ROWS, rows)
     pairs = d // PAIR
     blocks = rows // BLOCK
     big = tiles(t, d)
-    w = whole((d, d))
     return pl.pallas_call(
-        lambda *refs: attend_kernel(d // heads, *refs),
+        lambda tok, wq, wk, wv, wo, *refs: attend_kernel(d // heads, tok, (wq, wk, wv, wo), *refs),
         grid=(rows // t,),
-        in_specs=[big, w, w, w, w, whole(vec.shape)],
+        in_specs=[big] + weight_specs(weights) + [whole(vec.shape)],
         out_specs=[
             big, big, big,
             pl.BlockSpec((t // BLOCK, pairs, FRAMES, 2 * BLOCK), lambda i: (i, 0, 0, 0)),
@@ -276,7 +302,7 @@
         compiler_params=params(),
         cost_estimate=pl.CostEstimate(flops=10 * rows * d * d, bytes_accessed=24 * rows * d, transcendentals=0),
         name="attend",
-    )(tokens, wq, wk, wv, wo, vec)
+    )(tokens, *four(weights), vec)
 
 
 def mlp(middle, dy, w1, w2, vec, hb):
@@ -302,61 +328,431 @@
     )(middle, dy, w1, w2, vec, hb)
 
 
-def back(tokens, mg, q, k, v, p, mixed, wq, wk, wv, wo, vec, heads):
+def back(tokens, mg, q, k, v, p, mixed, weights, vec, heads):
     rows, d = tokens.shape
     t = min(ROWS, rows)
     pairs = d // PAIR
     big = tiles(t, d)
-    w = whole((d, d))
-    return pl.pallas_call(
-        lambda *refs: back_kernel(d // heads, *refs),
+    count = len(weights)
+
+    def kernel(*refs):
+        ins, w_refs, vec_ref, gt_ref = refs[:7], refs[7:11], refs[11], refs[12]
+        wg_refs, rest = refs[13 : 13 + count], refs[13 + count :]
+        back_kernel(d // heads, *ins, w_refs, vec_ref, gt_ref, wg_refs, *rest)
+
+    out = pl.pallas_call(
+        kernel,
         grid=(rows // t,),
         in_specs=[
             big, big, big, big, big,
             pl.BlockSpec((t // BLOCK, pairs, FRAMES, 2 * BLOCK), lambda i: (i, 0, 0, 0)),
-            big, w, w, w, w, whole(vec.shape),
-        ],
-        out_specs=[big, w, w, w, w, whole((8, d))],
-        out_shape=[shaped((rows, d), BF)] + [shaped((d, d), BF)] * 4 + [shaped((8, d), F32)],
+            big,
+        ] + weight_specs(weights) + [whole(vec.shape)],
+        out_specs=[big] + [whole(w.shape) for w in weights] + [whole((8, d))],
+        out_shape=[shaped((rows, d), BF)] + [shaped(w.shape, BF) for w in weights] + [shaped((8, d), F32)],
         scratch_shapes=[pltpu.VMEM((d, d), F32)] * 4 + [pltpu.VMEM((t, d), BF)] * 4,
         compiler_params=params(),
         cost_estimate=pl.CostEstimate(flops=20 * rows * d * d, bytes_accessed=24 * rows * d, transcendentals=0),
         name="back",
-    )(tokens, mg, q, k, v, p, mixed, wq, wk, wv, wo, vec)
-
-
-def on_device(
-    tokens, grad_out, first_gain, first_shift, query_proj, query_bias, key_proj, value_proj, value_bias,
-    output_proj, output_bias, second_gain, second_shift, hidden_proj, hidden_bias, final_proj, final_bias, threshold,
-):
+    )(tokens, mg, q, k, v, p, mixed, *four(weights), vec)
+    return out[0], out[1 : 1 + count], out[1 + count]
+
+
+MESH = pl.DeviceIdType.MESH
+
+
+class Place:
+    def __init__(self, shards):
+        self.shards = shards
+        self.depth = shards // 4
+        self.me = lax.axis_index("shard")
+        self.core = lax.axis_index("rep")
+        self.zed = self.me // 4
+        x, y = self.me % 2, (self.me // 2) % 2
+        self.near_step, self.far_step = 1 + self.core, 2 - self.core
+        self.near = x + self.core * (y - x)
+        self.far = y + self.core * (x - y)
+        self.sibling = (self.me, 1 - self.core)
+        self.near_peer = (self.block(self.zed, 1 - self.near, self.far), self.core)
+        self.far_peer = (self.block(self.zed, self.near, 1 - self.far), self.core)
+        self.columns = [lax.rem(self.zed + k, self.depth) for k in range(self.depth)]
+        self.column_peers = [(self.block(z, self.near, self.far), self.core) for z in self.columns]
+
+    def block(self, zed, near, far):
+        return zed * 4 + near * self.near_step + far * self.far_step
+
+    def greet(self):
+        barrier = pltpu.get_barrier_semaphore()
+        peers = [self.sibling, self.near_peer, self.far_peer] + self.column_peers[1:]
+        for peer in peers:
+            pl.semaphore_signal(barrier, inc=1, device_id=peer, device_id_type=MESH)
+        pl.semaphore_wait(barrier, len(peers))
+
+
+def half_of(ref, core):
+    width = ref.shape[-1] // 2
+    return pl.ds(pl.multiple_of(core * width, width), width)
+
+
+class Gather:
+    def __init__(self, place, full, send, recv, other):
+        self.place, self.full, self.send, self.recv, self.other = place, full, send, recv, other
+        self.cols = half_of(full, place.core)
+        self.count = 0
+        self.sent = []
+
+    def push(self, block, peer, recv):
+        view = self.full.at[block, :, self.cols]
+        copy = pltpu.make_async_remote_copy(
+            src_ref=view, dst_ref=view, send_sem=self.send.at[self.count], recv_sem=recv.at[block],
+            device_id=peer, device_id_type=MESH,
+        )
+        copy.start()
+        self.count += 1
+        self.sent.append(copy)
+
+    def arrived(self, block, recv, cols):
+        view = self.full.at[block, :, cols]
+        pltpu.make_async_remote_copy(
+            src_ref=view, dst_ref=view, send_sem=self.send.at[0], recv_sem=recv.at[block],
+            device_id=self.place.sibling, device_id_type=MESH,
+        ).wait_recv()
+
+    def own(self):
+        p = self.place
+        for peer in p.column_peers[1:]:
+            self.push(p.me, peer, self.recv)
+        self.push(p.me, p.near_peer, self.recv)
+        self.push(p.me, p.far_peer, self.recv)
+
+    def column(self):
+        p = self.place
+        for z in p.columns[1:]:
+            block = p.block(z, p.near, p.far)
+            self.arrived(block, self.recv, self.cols)
+            self.push(block, p.near_peer, self.recv)
+            self.push(block, p.far_peer, self.recv)
+            self.push(block, p.sibling, self.other)
+
+    def plane(self):
+        p = self.place
+        for z in p.columns:
+            block = p.block(z, 1 - p.near, p.far)
+            self.arrived(block, self.recv, self.cols)
+            self.push(block, p.far_peer, self.recv)
+            self.push(block, p.sibling, self.other)
+
+    def rest(self):
+        p = self.place
+        for z in p.columns:
+            for near in (p.near, 1 - p.near):
+                block = p.block(z, near, 1 - p.far)
+                self.arrived(block, self.recv, self.cols)
+                self.push(block, p.sibling, self.other)
+
+    def finish(self):
+        p = self.place
+        cols = half_of(self.full, 1 - p.core)
+        for k in range(1, p.shards):
+            self.arrived(lax.rem(p.me + k, p.shards), self.other, cols)
+        for copy in self.sent:
+            copy.wait_send()
+
+    def sends(shards):
+        return 3 * (shards // 4) + (shards // 4 - 1) + shards // 4 + shards - 1
+
+
+def gather_kernel(shards, wq, wk, wv, wo, w1, w2, small, attn_out, w1_out, w2_out, small_out, local, send, recv, other):
+    p = Place(shards)
+    rows = wq.shape[0]
+    copies = [
+        pltpu.make_async_copy(w, attn_out.at[p.me, pl.ds(i * rows, rows), :], local.at[i])
+        for i, w in enumerate((wq, wk, wv, wo))
+    ] + [
+        pltpu.make_async_copy(w, out.at[p.me], local.at[4 + i])
+        for i, (w, out) in enumerate(((w1, w1_out), (w2, w2_out), (small, small_out)))
+    ]
+    for copy in copies:
+        copy.start()
+    p.greet()
+    for copy in copies:
+        copy.wait()
+    s, a, b, c = (
+        Gather(p, full, send.at[i], recv.at[i], other.at[i])
+        for i, full in enumerate((small_out, attn_out, w1_out, w2_out))
+    )
+    s.own(), a.own(), b.own(), s.column(), a.column(), c.own()
+    s.plane(), a.plane(), b.column(), s.rest(), b.plane(), c.column(), c.plane()
+    a.rest(), b.rest(), c.rest()
+    for g in (s, a, b, c):
+        g.finish()
+
+
+def gather_all(shards, wq, wk, wv, wo, w1, w2, small):
+    rows, d = wq.shape
+    sends = Gather.sends(shards)
+    anywhere = pl.BlockSpec(memory_space=pl.ANY)
+    return pl.pallas_call(
+        lambda *refs: gather_kernel(shards, *refs),
+        in_specs=[pl.BlockSpec(memory_space=pltpu.VMEM)] * 7,
+        out_specs=[anywhere] * 4,
+        out_shape=[
+            shaped((shards, 4 * rows, d), BF), shaped((shards,) + w1.shape, BF), shaped((shards,) + w2.shape, BF),
+            shaped((shards,) + small.shape, F32),
+        ],
+        scratch_shapes=[
+            pltpu.SemaphoreType.DMA((7,)), pltpu.SemaphoreType.DMA((4, sends)),
+            pltpu.SemaphoreType.DMA((4, shards)), pltpu.SemaphoreType.DMA((4, shards)),
+        ],
+        compiler_params=pltpu.CompilerParams(collective_id=0, has_side_effects=True),
+        name="gather",
+    )(wq, wk, wv, wo, w1, w2, small)
+
+
+class Scatter:
+    def kinds(shards, rows, cols, dtype):
+        depth, half = shards // 4, cols // 2
+        many = lambda *lead: pltpu.VMEM(lead + (rows, half), dtype)
+        return [
+            many(shards), many(shards), many(depth, 2), many(depth, 2), many(depth), many(depth),
+            many(depth - 1), many(depth - 1), pltpu.VMEM((rows, half), F32), pltpu.VMEM((rows, half), F32),
+            pltpu.SemaphoreType.DMA((depth,)), pltpu.SemaphoreType.DMA((4 * depth,)), pltpu.SemaphoreType.DMA((4 * depth,)),
+        ]
+
+    def __init__(self, place, full, out, scratch):
+        self.p, self.full, self.out = place, full, out
+        (self.mine, self.got_one, self.send_two, self.got_two, self.send_three, self.got_three,
+         self.send_four, self.got_four, self.total, self.joined, self.local, self.send, self.recv) = scratch
+        self.sent = []
+
+    def copy(self, src, dst, slot, peer):
+        return pltpu.make_async_remote_copy(
+            src_ref=src, dst_ref=dst, send_sem=self.send.at[slot], recv_sem=self.recv.at[slot],
+            device_id=peer, device_id_type=MESH,
+        )
+
+    def push(self, src, dst, slot, peer):
+        copy = self.copy(src, dst, slot, peer)
+        copy.start()
+        self.sent.append(copy)
+
+    def order(self):
+        return self.p.columns[1:] + self.p.columns[:1]
+
+    def first(self):
+        p = self.p
+        for z in self.order():
+            rows = pl.ds(4 * z, 4)
+            self.push(self.full.at[rows, :, half_of(self.full, 1 - p.core)], self.got_one.at[rows], z, p.sibling)
+        for z in self.order():
+            self.load(z).start()
+
+    def load(self, z):
+        rows = pl.ds(4 * z, 4)
+        return pltpu.make_async_copy(
+            self.full.at[rows, :, half_of(self.full, self.p.core)], self.mine.at[rows], self.local.at[z]
+        )
+
+    def pair(self, block):
+        return self.mine[block].astype(F32) + self.got_one[block].astype(F32)
+
+    def second(self):
+        p, d = self.p, self.p.depth
+        for z in self.order():
+            rows = pl.ds(4 * z, 4)
+            self.load(z).wait()
+            self.copy(self.got_one.at[rows], self.got_one.at[rows], z, p.sibling).wait_recv()
+            for near in range(2):
+                block = p.block(z, near, 1 - p.far)
+                self.send_two[z, near] = self.pair(block).astype(self.mine.dtype)
+            self.push(self.send_two.at[z], self.got_two.at[z], d + z, p.far_peer)
+
+    def third(self):
+        p, d = self.p, self.p.depth
+        for z in self.order():
+            self.copy(self.send_two.at[z], self.got_two.at[z], d + z, p.far_peer).wait_recv()
+            block = p.block(z, 1 - p.near, p.far)
+            value = self.pair(block) + self.got_two[z, 1 - p.near].astype(F32)
+            self.send_three[z] = value.astype(self.mine.dtype)
+            self.push(self.send_three.at[z], self.got_three.at[z], 2 * d + z, p.near_peer)
+
+    def triple(self, z):
+        p, d = self.p, self.p.depth
+        self.copy(self.send_three.at[z], self.got_three.at[z], 2 * d + z, p.near_peer).wait_recv()
+        block = p.block(z, p.near, p.far)
+        return self.pair(block) + self.got_two[z, p.near].astype(F32) + self.got_three[z].astype(F32)
+
+    def fourth(self):
+        p, d = self.p, self.p.depth
+        for k in range(1, d):
+            self.send_four[k - 1] = self.triple(p.columns[k]).astype(self.mine.dtype)
+            self.push(self.send_four.at[k - 1], self.got_four.at[k - 1], 3 * d + k - 1, p.column_peers[k])
+
+    def fifth(self):
+        p, d = self.p, self.p.depth
+        value = self.triple(p.zed)
+        for k in range(1, d):
+            self.copy(self.send_four.at[k - 1], self.got_four.at[k - 1], 3 * d + k - 1, p.column_peers[k]).wait_recv()
+            value = value + self.got_four[k - 1].astype(F32)
+        self.total[...] = value
+        self.push(self.total, self.joined, 4 * d - 1, p.sibling)
+        self.out[:, half_of(self.out, p.core)] = value
+
+    def finish(self):
+        p, d = self.p, self.p.depth
+        self.copy(self.total, self.joined, 4 * d - 1, p.sibling).wait_recv()
+        self.out[:, half_of(self.out, 1 - p.core)] = self.joined[...]
+        for copy in self.sent:
+            copy.wait_send()
+
+
+class Largest:
+    def __init__(self, place, own, out, got, kept, send, recv):
+        self.p, self.own, self.out, self.got, self.kept, self.send, self.recv = place, own, out, got, kept, send, recv
+        self.sent = []
+        d = place.depth
+        self.stages = [
+            [(place.sibling, 0)], [(place.far_peer, 1)], [(place.near_peer, 2)],
+            [(place.column_peers[k], 2 + k) for k in range(1, d)],
+        ]
+
+    def push(self, stage):
+        if stage == 0:
+            self.kept[0] = self.own[...]
+        for peer, slot in self.stages[stage]:
+            copy = pltpu.make_async_remote_copy(
+                src_ref=self.kept.at[stage], dst_ref=self.got.at[slot], send_sem=self.send.at[slot],
+                recv_sem=self.recv.at[slot], device_id=peer, device_id_type=MESH,
+            )
+            copy.start()
+            self.sent.append((copy, stage))
+
+    def take(self, stage):
+        value = self.kept[stage]
+        for (copy, s), (_, slot) in zip([c for c in self.sent if c[1] == stage], self.stages[stage]):
+            copy.wait_recv()
+            value = jnp.maximum(value, self.got[slot])
+        if stage == 3:
+            self.out[...] = value
+            for copy, _ in self.sent:
+                copy.wait_send()
+        else:
+            self.kept[stage + 1] = value
+
+
+def scatter_kernel(shards, *refs):
+    (attn, w1, w2, small, top, attn_out, w1_out, w2_out, small_out, top_out), scratch = refs[:10], refs[10:]
+    p = Place(shards)
+    count = len(scratch) // 4
+    s, a, b, c = (
+        Scatter(p, full, out, scratch[13 * i : 13 * i + 13])
+        for i, (full, out) in enumerate(((small, small_out), (attn, attn_out), (w1, w1_out), (w2, w2_out)))
+    )
+    t = Largest(p, top, top_out, *scratch[52:])
+    p.greet()
+    t.push(0)
+    for g in (s, c, b, a):
+        g.first()
+    s.second(), t.take(0), t.push(1), c.second(), s.third(), b.second(), c.third(), a.second(), b.third()
+    t.take(1), t.push(2), s.fourth(), c.fourth(), a.third(), b.fourth(), a.fourth()
+    t.take(2), t.push(3), s.fifth(), c.fifth(), b.fifth(), a.fifth(), t.take(3)
+    for g in (s, c, b, a):
+        g.finish()
+
+
+def scatter_all(shards, attn, w1, w2, small, top):
+    depth = shards // 4
+    arrays = ((small, F32), (attn, BF), (w1, BF), (w2, BF))
+    scratch = sum((Scatter.kinds(shards, x.shape[1], x.shape[2], dtype) for x, dtype in arrays), [])
+    scratch += [
+        pltpu.VMEM((depth + 2, 8, 128), F32), pltpu.VMEM((4, 8, 128), F32),
+        pltpu.SemaphoreType.DMA((depth + 2,)), pltpu.SemaphoreType.DMA((depth + 2,)),
+    ]
+    anywhere, inside = pl.BlockSpec(memory_space=pl.ANY), pl.BlockSpec(memory_space=pltpu.VMEM)
+    return pl.pallas_call(
+        lambda *refs: scatter_kernel(shards, *refs),
+        in_specs=[anywhere] * 4 + [inside],
+        out_specs=[inside] * 5,
+        out_shape=[shaped(x.shape[1:], F32) for x in (attn, w1, w2, small)] + [shaped((8, 128), F32)],
+        scratch_shapes=scratch,
+        compiler_params=pltpu.CompilerParams(collective_id=1, has_side_effects=True, vmem_limit_bytes=VMEM_LIMIT),
+        name="scatter",
+    )(attn, w1, w2, small, top)
+
+
+def on_device(shards, reps, *args):
+    (
+        tokens, grad_out, first_gain, first_shift, query_proj, query_bias, key_proj, value_proj, value_bias,
+        output_proj, output_bias, second_gain, second_shift, hidden_proj, hidden_bias, final_proj, final_bias, threshold,
+    ) = args
+    heads = threshold.shape[0]
+    d = tokens.shape[1]
+    hidden = hidden_proj.shape[1]
+    head_dim = d // heads
+    small = (first_gain, first_shift, query_bias, value_bias, output_bias, second_gain, second_shift, final_bias)
+    rows, more = small[0].shape[0], hidden_bias.shape[0] // 8
+    own = reps == 2 and shards % 4 == 0 and shards > 4 and rows % 16 == 0 and rows <= 128 and more <= 128
+
     def gather(x):
         return lax.all_gather(x, "shard", axis=0, tiled=True)
-
-    heads = threshold.shape[0]
-    wq, wk, wv, wo = (gather(x) for x in (query_proj, key_proj, value_proj, output_proj))
-    small = (first_gain, first_shift, query_bias, value_bias, output_bias, second_gain, second_shift, final_bias)
-    vec = jnp.stack([gather(x) for x in small]).astype(F32)
-    hb = gather(hidden_bias).astype(F32)[None]
-    w1, w2 = gather(hidden_proj), gather(final_proj)
-    q, k, v, p, mixed, middle, top = attend(tokens, wq, wk, wv, wo, vec, heads)
-    head_dim = tokens.shape[1] // heads
-    local = jnp.max(top.reshape(top.shape[0], FRAMES, 2, BLOCK), axis=(1, 3)).reshape(heads)
-    global_max = lax.pmax(local, ("shard", "rep"))
-    layer_output, mg, w1g, w2g, vg2, hbg = mlp(middle, grad_out, w1, w2, vec, hb)
-    grad_tokens, wqg, wkg, wvg, wog, vg1 = back(tokens, mg, q, k, v, p, mixed, wq, wk, wv, wo, vec, heads)
 
     def scatter(x):
         y = lax.psum_scatter(x.astype(BF), "shard", scatter_dimension=0, tiled=True)
         return lax.psum(y, "rep").astype(F32)
 
+    if own:
+        tile = jnp.concatenate(
+            [
+                jnp.pad(jnp.stack(small).astype(F32), ((0, 0), (0, 128 - rows))),
+                jnp.pad(hidden_bias.astype(F32).reshape(8, more), ((0, 0), (0, 128 - more))),
+            ],
+            axis=1,
+        )
+        attn, w1, w2, tile = gather_all(
+            shards, query_proj, key_proj, value_proj, output_proj, hidden_proj, final_proj, tile
+        )
+        weights = (attn,)
+        w1, w2 = w1.reshape(d, hidden), w2.reshape(hidden, d)
+        vec = jnp.moveaxis(tile[:, :, :rows], 0, 1).reshape(8, d)
+        hb = tile[:, :, 128 : 128 + more].reshape(1, hidden)
+    else:
+        weights = tuple(gather(x) for x in (query_proj, key_proj, value_proj, output_proj))
+        w1, w2 = gather(hidden_proj), gather(final_proj)
+        vec = jnp.stack([gather(x) for x in small]).astype(F32)
+        hb = gather(hidden_bias).astype(F32)[None]
+    q, k, v, p, mixed, middle, top = attend(tokens, weights, vec, heads)
+    local = jnp.max(top.reshape(top.shape[0], FRAMES, 2, BLOCK), axis=(1, 3)).reshape(heads)
+    layer_output, mg, w1g, w2g, vg2, hbg = mlp(middle, grad_out, w1, w2, vec, hb)
+    grad_tokens, wg, vg1 = back(tokens, mg, q, k, v, p, mixed, weights, vec, heads)
+    vg = jnp.concatenate([vg1[:5], vg2[:3]])
+    if own:
+        tile = jnp.concatenate(
+            [
+                jnp.pad(jnp.moveaxis(vg.reshape(8, shards, rows), 1, 0), ((0, 0), (0, 0), (0, 128 - rows))),
+                jnp.pad(hbg.reshape(shards, 8, more), ((0, 0), (0, 0), (0, 128 - more))),
+            ],
+            axis=2,
+        )
+        attn, w1g, w2g, tile, top = scatter_all(
+            shards, wg[0], w1g.reshape(shards, -1, hidden), w2g.reshape(shards, -1, d), tile,
+            jnp.broadcast_to(jnp.pad(local, (0, 128 - heads))[None], (8, 128)),
+        )
+        wg = tuple(attn[i * rows : (i + 1) * rows] for i in range(4))
+        vg = tuple(tile[i, :rows] for i in range(8))
+        hbg = tile[:, 128 : 128 + more].reshape(-1)
+        global_max = top[0, :heads]
+    else:
+        global_max = lax.pmax(local, ("shard", "rep"))
+        wg = tuple(scatter(x) for x in wg)
+        w1g, w2g = scatter(w1g), scatter(w2g)
+        vg = tuple(scatter(vg[i]) for i in range(8))
+        hbg = scatter(hbg[0])
     factor = jnp.minimum(1.0, threshold / global_max)
     column_scale = jnp.repeat(jnp.sqrt(factor), head_dim)
-    shard_rows = query_bias.shape[0]
-    bias_scale = lax.dynamic_slice_in_dim(column_scale, lax.axis_index("shard") * shard_rows, shard_rows)
+    bias_scale = lax.dynamic_slice_in_dim(column_scale, lax.axis_index("shard") * rows, rows)
     return (
-        layer_output, grad_tokens, scatter(vg1[0]), scatter(vg1[1]), scatter(wqg), scatter(vg1[2]), scatter(wkg),
-        scatter(wvg), scatter(vg1[3]), scatter(wog), scatter(vg1[4]), scatter(vg2[0]), scatter(vg2[1]), scatter(w1g),
-        scatter(hbg[0]), scatter(w2g), scatter(vg2[2]), global_max, factor,
+        layer_output, grad_tokens, vg[0], vg[1], wg[0], vg[2], wg[1], wg[2], vg[3], wg[3], vg[4], vg[5], vg[6],
+        w1g, hbg, w2g, vg[7], global_max, factor,
         query_proj.astype(F32) * column_scale[None, :], query_bias.astype(F32) * bias_scale,
         key_proj.astype(F32) * column_scale[None, :],
     )
@@ -407,6 +803,7 @@
         P("shard"),
         P("shard", None),
     )
+    shards, reps = mesh.shape["shard"], mesh.shape["rep"]
     return jax.shard_map(
-        on_device, mesh=mesh, in_specs=in_specs, out_specs=out_specs, check_vma=False
+        functools.partial(on_device, shards, reps), mesh=mesh, in_specs=in_specs, out_specs=out_specs, check_vma=False
     )

time: 1440 us -> 368 us (0.26)
  waiting for transfers between devices: 1030 us -> 0 us
  blocking collectives: 196 us -> 0 us
  Pallas kernels: 170 us -> 347 us
  between operations: 16.8 us -> 0.8 us
    reduce_scatter x6 -> x0, waiting for transfers between devices: 747 us -> none  [scatter(): y = lax.psum_scatter(x.astype(BF), 'shard', scatter_dimension=0, tiled=True)]
    all_gather x6 -> x0, waiting for transfers between devices: 275 us -> none  [gather(): return lax.all_gather(x, 'shard', axis=0, tiled=True)]
    pallas_call x2 -> x4, Pallas kernels: 85.5 us -> 263 us  [the longest x1 103 us: scatter_all(): pl.pallas_call(lambda *refs: scatter_kernel(shards, *refs), in_specs=[any...]
    unnamed x2 -> x0, blocking collectives: 154 us -> none
    pmax x1 -> x0, blocking collectives: 39.4 us -> none  [on_device(): global_max = lax.pmax(local, ('shard', 'rep'))]
    convert_element_type x17 -> x0, other arithmetic: 15.2 us -> none  [the longest x15 14.5 us: scatter(): return lax.psum(y, 'rep').astype(F32)]
  transfers between devices with their start and end apart: 13 -> 0, of which waited for: 11 -> 0; matrix products, arithmetic and copies ran while one was open for 1% -> 0% of each run, Pallas kernels for 2% -> 0%
where the time goes in v2:
time: 368 us; the launch traced here: 367 us
  Pallas kernels  347 us (94%)
  local copies, waits for them, and re-layouts  11.8 us (3%)
  other arithmetic  7.6 us (2%)
    pallas_call x1, Pallas kernels, scatter_all(): pl.pallas_call(lambda *refs: scatter_kernel(shards, *refs), in_specs=[any...  103 us
    pallas_call x1, Pallas kernels, mlp(): pl.pallas_call(lambda *refs: mlp_kernel(768, *refs), grid=(rows // t,), i...  84.1 us
    pallas_call x1, Pallas kernels, gather_all(): pl.pallas_call(lambda *refs: gather_kernel(shards, *refs), in_specs=[pl.B...  73.1 us
    pallas_call x1, Pallas kernels, back(): pl.pallas_call(kernel, grid=(rows // t,), in_specs=[big, big, big, big, b...  56.3 us
    pallas_call x1, Pallas kernels, attend(): pl.pallas_call(lambda tok, wq, wk, wv, wo, *refs: attend_kernel(d // head...  30.2 us

profile of v2, /device:TPU:0, one launch (start us, length us, event | category | flops | bytes accessed | tf_op | source)
XLA Modules:
  0.0 367.0 jit_solution(9835856174531187145)
XLA Ops:
  0.7 0.8 stack.35
  1.5 0.7 reshape.83
  2.2 0.6 fusion.3.refs_6_
  2.8 73.1 %gather.1 = (bf16[16,192,768]{2,1,0:T(8,128)(2,1)}, bf16[16,48,3072]{2,1,0:T(8,128)(2,1)}, bf16[16,192,768]{2,1,0:T(8,128)(2,1)}, f32[16,8,256]{2,1,0:T(8,128)}) custom-call(bf16[48,768]{1,0:T(8,128)(2,1)} %refs_0_.2, bf16[48,768]{1,0:T(8,128)(2,1)} %refs_1_.2, bf16[48,768]{1,0:T(8,128)(2,1)} %refs_2_.1, bf16[48,768]{1,0:T(8,128)(2,1)} %refs_3_.1, ...), custom_call_target="tpu_custom_call" | custom-call | tf_op jit(solution)/shard_map/gather/pallas_call | solution.py:495
  76.0 0.8 slice.55
  76.8 0.8 slice_bitcast_fusion
  77.7 0.7 reshape.87.refs_5_
  78.4 0.7 reshape.84.refs_0_.refs_4_.refs_11_
  79.1 30.2 %attend.1 = (bf16[2048,768]{1,0:T(8,128)(2,1)}, bf16[2048,768]{1,0:T(8,128)(2,1)}, bf16[2048,768]{1,0:T(8,128)(2,1)}, f32[16,6,16,256]{3,2,1,0:T(8,128)}, bf16[2...) custom-call(bf16[2048,768]{1,0:T(8,128)(2,1)} %refs_0_.3, ...), custom_call_target="tpu_custom_call" | custom-call | flops 12079595520 | bytes 37748736 | tf_op jit(solution)/shard_map/attend/pallas_call | solution.py:289
  109.2 0.9 reduce_max.10
  110.3 0.6 broadcast_in_dim.4.refs_4_
  110.9 84.1 %mlp.1 = (bf16[2048,768]{1,0:T(8,128)(2,1)}, f32[2048,768]{1,0:T(8,128)}, bf16[768,3072]{1,0:T(8,128)(2,1)}, bf16[3072,768]{1,0:T(8,128)(2,1)}, f32[8,768]{1,0:T(8,128)}, /*index=5*/f32[1,3072]{1,0:T(1,128)}) custom-call(f32[2048,768]{1,0:T(8,128)} %get-tuple-element.49.refs_0_, bf16[2048,768]{1,0:T(8,128)(2,1)} %refs_1_.3, bf16[768,3072]{1,0:T(8,128)(2,1)} %bitcast.49, ...), custom_call_target="tpu_custom_call" | custom-call | flops 57982058496 | bytes 22020096 | tf_op jit(solution)/shard_map/mlp/pallas_call | solution.py:313
  195.1 56.3 %back.1 = (bf16[2048,768]{1,0:T(8,128)(2,1)}, bf16[16,192,768]{2,1,0:T(8,128)(2,1)}, f32[8,768]{1,0:T(8,128)}) custom-call(bf16[2048,768]{1,0:T(8,128)(2,1)} %refs_0_.3, f32[2048,768]{1,0:T(8,128)} %get-tuple-element.53.refs_1_, bf16[2048,768]{1,0:T(8,128)(2,1)} %get-tuple-element.54.refs_2_, bf16[2048,768]{1,0:T(8,128)(2,1)} %get-tuple-element.55.refs_3_, ...), custom_call_target="tpu_custom_call" | custom-call | flops 24159191040 | bytes 37748736 | tf_op jit(solution)/shard_map/back/pallas_call | solution.py:343
  251.9 0.7 reduce.5
  252.6 0.8 pad_maximum_fusion
  253.6 0.7 select_maximum_fusion.refs_3_
  254.2 103.1 %scatter.1 = (f32[192,768]{1,0:T(8,128)}, f32[48,3072]{1,0:T(8,128)}, f32[192,768]{1,0:T(8,128)}, f32[8,256]{1,0:T(8,128)}, f32[8,128]{1,0:T(8,128)}) custom-call(bf16[16,192,768]{2,1,0:T(8,128)(2,1)} %get-tuple-element.60.refs_0_, bf16[16,48,3072]{2,1,0:T(8,128)(2,1)} %bitcast.37, bf16[16,192,768]{2,1,0:T(8,128)(2,1)} %bitcast.38, ...), custom_call_target="tpu_custom_call" | custom-call | tf_op jit(solution)/shard_map/scatter/pallas_call | solution.py:672
  357.3 1.3 fusion.4
  358.6 0.7 slice.69
  359.3 1.5 slice_bitcast_fusion.2
  360.8 0.6 reshape.93
  362.2 2.1 convert_multiply_fusion
  364.2 1.9 copy.49
  366.2 0.8 copy.50
  (27 shorter events, 1.7 us)
Async XLA Ops:
  195.1 56.8 %copy-start.3 = (f32[1,3072]{1,0:T(1,128)S(1)}, f32[1,3072]{1,0:T(1,128)}, u32[]{:S(2)}) copy-start(f32[1,3072]{1,0:T(1,128)} %get-tuple-element.65) | copy-start | bytes 36868
  195.1 57.5 %copy-start.4 = (f32[8,768]{1,0:T(8,128)S(1)}, f32[8,768]{1,0:T(8,128)}, u32[]{:S(2)}) copy-start(f32[8,768]{1,0:T(8,128)} %get-tuple-element.64) | copy-start | bytes 73732
  254.2 103.1 %copy-start.6 = (f32[12]{0:T(128)S(1)}, f32[12]{0:T(128)}, u32[]{:S(2)}) copy-start(f32[12]{0:T(128)} %param.35) | copy-start | bytes 148
  254.2 107.4 %copy-start.5 = (bf16[48]{0:T(256)(128)(2,1)S(1)}, bf16[48]{0:T(256)(128)(2,1)}, u32[]{:S(2)}) copy-start(bf16[48]{0:T(256)(128)(2,1)} %param.23) | copy-start | bytes 292
  254.2 108.0 %copy-start.1 = (bf16[48,768]{1,0:T(8,128)(2,1)S(1)}, bf16[48,768]{1,0:T(8,128)(2,1)}, u32[]{:S(2)}) copy-start(bf16[48,768]{1,0:T(8,128)(2,1)} %refs_0_.2) | copy-start | bytes 221188
  254.2 108.0 %copy-start.2 = (bf16[48,768]{1,0:T(8,128)(2,1)S(1)}, bf16[48,768]{1,0:T(8,128)(2,1)}, u32[]{:S(2)}) copy-start(bf16[48,768]{1,0:T(8,128)(2,1)} %refs_1_.2) | copy-start | bytes 221188
  357.3 8.8 %copy-start = (f32[192,768]{1,0:T(8,128)S(1)}, f32[192,768]{1,0:T(8,128)}, u32[]{:S(2)}) copy-start(f32[192,768]{1,0:T(8,128)} %get-tuple-element.130) | copy-start | bytes 1769476

commit v3 on v2

--- a/solution.py
+++ b/solution.py
@@ -86,7 +86,7 @@
 
 def attend_kernel(
     width, tok_ref, w_refs, vec_ref,
-    q_ref, k_ref, v_ref, p_ref, mix_ref, mid_ref, top_ref,
+    q_ref, k_ref, v_ref, p_ref, mix_ref, mid_ref, top_ref, tick=lambda point: None,
 ):
     scale = 1.0 / math.sqrt(width)
     wq, wk, wv, wo = (square(w) for w in w_refs)
@@ -97,6 +97,7 @@
     q_ref[...] = (nn(one, wq) + vec_ref[2:3]).astype(BF)
     k_ref[...] = nn(one, wk).astype(BF)
     v_ref[...] = (nn(one, wv) + vec_ref[3:4]).astype(BF)
+    tick(1)
     masks = place_masks()
     first, second = halves(width)
     pairs = tok_ref.shape[1] // PAIR
@@ -120,7 +121,9 @@
         return carry
 
     lax.fori_loop(0, tok_ref.shape[0] // BLOCK, body, 0)
-    mid_ref[...] = tok + (nn(mix_ref[...], wo) + vec_ref[4:5])
+    tick(2)
+    mid_ref[...] = tok_ref[...].astype(F32) + (nn(mix_ref[...], wo) + vec_ref[4:5])
+    tick(3)
 
 
 def mlp_kernel(
@@ -183,7 +186,7 @@
     width, tok_ref, mg_ref, q_ref, k_ref, v_ref, p_ref, mix_ref,
     w_refs, vec_ref,
     gt_ref, wg_refs, vg_ref,
-    accq, acck, accv, acco, mgl_ref, dq_ref, dk_ref, dv_ref,
+    accq, acck, accv, acco, mgl_ref, dq_ref, dk_ref, dv_ref, tick=lambda point: None,
 ):
     step, last = pl.program_id(0), pl.num_programs(0) - 1
     scale = 1.0 / math.sqrt(width)
@@ -197,10 +200,12 @@
             acc[...] = jnp.zeros_like(acc)
         vg_ref[...] = jnp.zeros_like(vg_ref)
 
+    tick(0)
     branch = mg_ref[...].astype(BF)
     mgl_ref[...] = nt(branch, wo).astype(BF)
     acco[...] += tn(mix_ref[...], branch)
     vg_ref[4:5] += column_sum(branch.astype(F32))
+    tick(1)
     masks = place_masks()
     first, second = halves(width)
     pairs = tok_ref.shape[1] // PAIR
@@ -221,6 +226,7 @@
         return carry
 
     lax.fori_loop(0, tok_ref.shape[0] // BLOCK, body, 0)
+    tick(2)
     unit, inverse = normalise(tok_ref[...].astype(F32))
     one = (unit * gain + shift).astype(BF)
     dq, dk, dv = dq_ref[...], dk_ref[...], dv_ref[...]
@@ -229,10 +235,12 @@
     accq[...] += tn(one, dq)
     acck[...] += tn(one, dk)
     accv[...] += tn(one, dv)
+    tick(3)
     grad = nt(dq, wq) + nt(dk, wk) + nt(dv, wv)
     vg_ref[0:1] += column_sum(grad * unit)
     vg_ref[1:2] += column_sum(grad)
     gt_ref[...] = (mg_ref[...] + norm_back(grad, unit, inverse, gain)).astype(BF)
+    tick(4)
 
     @pl.when(step == last)
     def _():
@@ -396,117 +404,74 @@
 
 class Gather:
     def __init__(self, place, full, send, recv, other):
-        self.place, self.full, self.send, self.recv, self.other = place, full, send, recv, other
+        self.p, self.full, self.send, self.recv, self.other = place, full, send, recv, other
         self.cols = half_of(full, place.core)
         self.count = 0
-        self.sent = []
-
-    def push(self, block, peer, recv):
-        view = self.full.at[block, :, self.cols]
-        copy = pltpu.make_async_remote_copy(
-            src_ref=view, dst_ref=view, send_sem=self.send.at[self.count], recv_sem=recv.at[block],
+
+    def copy(self, block, slot, peer, recv, cols):
+        view = self.full.at[block, :, cols]
+        return pltpu.make_async_remote_copy(
+            src_ref=view, dst_ref=view, send_sem=self.send.at[slot], recv_sem=recv.at[block],
             device_id=peer, device_id_type=MESH,
         )
-        copy.start()
-        self.count += 1
-        self.sent.append(copy)
+
+    def push(self, block, *peers):
+        for peer in peers:
+            recv = self.other if peer is self.p.sibling else self.recv
+            self.copy(block, self.count, peer, recv, self.cols).start()
+            self.count += 1
 
     def arrived(self, block, recv, cols):
-        view = self.full.at[block, :, cols]
-        pltpu.make_async_remote_copy(
-            src_ref=view, dst_ref=view, send_sem=self.send.at[0], recv_sem=recv.at[block],
-            device_id=self.place.sibling, device_id_type=MESH,
-        ).wait_recv()
+        self.copy(block, 0, self.p.sibling, recv, cols).wait_recv()
 
     def own(self):
-        p = self.place
-        for peer in p.column_peers[1:]:
-            self.push(p.me, peer, self.recv)
-        self.push(p.me, p.near_peer, self.recv)
-        self.push(p.me, p.far_peer, self.recv)
-
-    def column(self):
-        p = self.place
-        for z in p.columns[1:]:
-            block = p.block(z, p.near, p.far)
+        p = self.p
+        self.push(p.me, *p.column_peers[1:], p.near_peer, p.far_peer)
+
+    def column(self, k):
+        p = self.p
+        block = p.block(p.columns[k + 1], p.near, p.far)
+        self.arrived(block, self.recv, self.cols)
+        self.push(block, p.near_peer, p.far_peer, p.sibling)
+
+    def plane(self, k):
+        p = self.p
+        block = p.block(p.columns[k], 1 - p.near, p.far)
+        self.arrived(block, self.recv, self.cols)
+        self.push(block, p.far_peer, p.sibling)
+
+    def rest(self, k):
+        p = self.p
+        for near in (p.near, 1 - p.near):
+            block = p.block(p.columns[k], near, 1 - p.far)
             self.arrived(block, self.recv, self.cols)
-            self.push(block, p.near_peer, self.recv)
-            self.push(block, p.far_peer, self.recv)
-            self.push(block, p.sibling, self.other)
-
-    def plane(self):
-        p = self.place
-        for z in p.columns:
-            block = p.block(z, 1 - p.near, p.far)
-            self.arrived(block, self.recv, self.cols)
-            self.push(block, p.far_peer, self.recv)
-            self.push(block, p.sibling, self.other)
-
-    def rest(self):
-        p = self.place
-        for z in p.columns:
-            for near in (p.near, 1 - p.near):
-                block = p.block(z, near, 1 - p.far)
-                self.arrived(block, self.recv, self.cols)
-                self.push(block, p.sibling, self.other)
-
-    def finish(self):
-        p = self.place
+            self.push(block, p.sibling)
+
+    def joined(self):
+        p = self.p
         cols = half_of(self.full, 1 - p.core)
         for k in range(1, p.shards):
             self.arrived(lax.rem(p.me + k, p.shards), self.other, cols)
-        for copy in self.sent:
-            copy.wait_send()
+
+    def drained(self):
+        p = self.p
+        for slot in range(self.count):
+            self.copy(p.me, slot, p.sibling, self.other, self.cols).wait_send()
 
     def sends(shards):
         return 3 * (shards // 4) + (shards // 4 - 1) + shards // 4 + shards - 1
 
 
-def gather_kernel(shards, wq, wk, wv, wo, w1, w2, small, attn_out, w1_out, w2_out, small_out, local, send, recv, other):
-    p = Place(shards)
-    rows = wq.shape[0]
-    copies = [
-        pltpu.make_async_copy(w, attn_out.at[p.me, pl.ds(i * rows, rows), :], local.at[i])
-        for i, w in enumerate((wq, wk, wv, wo))
-    ] + [
-        pltpu.make_async_copy(w, out.at[p.me], local.at[4 + i])
-        for i, (w, out) in enumerate(((w1, w1_out), (w2, w2_out), (small, small_out)))
-    ]
-    for copy in copies:
-        copy.start()
-    p.greet()
-    for copy in copies:
-        copy.wait()
-    s, a, b, c = (
-        Gather(p, full, send.at[i], recv.at[i], other.at[i])
-        for i, full in enumerate((small_out, attn_out, w1_out, w2_out))
-    )
-    s.own(), a.own(), b.own(), s.column(), a.column(), c.own()
-    s.plane(), a.plane(), b.column(), s.rest(), b.plane(), c.column(), c.plane()
-    a.rest(), b.rest(), c.rest()
-    for g in (s, a, b, c):
-        g.finish()
-
-
-def gather_all(shards, wq, wk, wv, wo, w1, w2, small):
-    rows, d = wq.shape
-    sends = Gather.sends(shards)
-    anywhere = pl.BlockSpec(memory_space=pl.ANY)
-    return pl.pallas_call(
-        lambda *refs: gather_kernel(shards, *refs),
-        in_specs=[pl.BlockSpec(memory_space=pltpu.VMEM)] * 7,
-        out_specs=[anywhere] * 4,
-        out_shape=[
-            shaped((shards, 4 * rows, d), BF), shaped((shards,) + w1.shape, BF), shaped((shards,) + w2.shape, BF),
-            shaped((shards,) + small.shape, F32),
-        ],
-        scratch_shapes=[
-            pltpu.SemaphoreType.DMA((7,)), pltpu.SemaphoreType.DMA((4, sends)),
-            pltpu.SemaphoreType.DMA((4, shards)), pltpu.SemaphoreType.DMA((4, shards)),
-        ],
-        compiler_params=pltpu.CompilerParams(collective_id=0, has_side_effects=True),
-        name="gather",
-    )(wq, wk, wv, wo, w1, w2, small)
+def ticker(plan, step):
+    def tick(point):
+        for (when, where), events in plan.items():
+            if where == point:
+                @pl.when(step == when)
+                def _():
+                    for event in events:
+                        event()
+
+    return tick
 
 
 class Scatter:
@@ -523,7 +488,6 @@
         self.p, self.full, self.out = place, full, out
         (self.mine, self.got_one, self.send_two, self.got_two, self.send_three, self.got_three,
          self.send_four, self.got_four, self.total, self.joined, self.local, self.send, self.recv) = scratch
-        self.sent = []
 
     def copy(self, src, dst, slot, peer):
         return pltpu.make_async_remote_copy(
@@ -532,9 +496,7 @@
         )
 
     def push(self, src, dst, slot, peer):
-        copy = self.copy(src, dst, slot, peer)
-        copy.start()
-        self.sent.append(copy)
+        self.copy(src, dst, slot, peer).start()
 
     def order(self):
         return self.p.columns[1:] + self.p.columns[:1]
@@ -556,9 +518,10 @@
     def pair(self, block):
         return self.mine[block].astype(F32) + self.got_one[block].astype(F32)
 
-    def second(self):
+    def second(self, *turns):
         p, d = self.p, self.p.depth
-        for z in self.order():
+        for i in turns or range(d):
+            z = self.order()[i]
             rows = pl.ds(4 * z, 4)
             self.load(z).wait()
             self.copy(self.got_one.at[rows], self.got_one.at[rows], z, p.sibling).wait_recv()
@@ -567,9 +530,10 @@
                 self.send_two[z, near] = self.pair(block).astype(self.mine.dtype)
             self.push(self.send_two.at[z], self.got_two.at[z], d + z, p.far_peer)
 
-    def third(self):
+    def third(self, *turns):
         p, d = self.p, self.p.depth
-        for z in self.order():
+        for i in turns or range(d):
+            z = self.order()[i]
             self.copy(self.send_two.at[z], self.got_two.at[z], d + z, p.far_peer).wait_recv()
             block = p.block(z, 1 - p.near, p.far)
             value = self.pair(block) + self.got_two[z, 1 - p.near].astype(F32)
@@ -582,18 +546,18 @@
         block = p.block(z, p.near, p.far)
         return self.pair(block) + self.got_two[z, p.near].astype(F32) + self.got_three[z].astype(F32)
 
-    def fourth(self):
+    def fourth(self, *turns):
         p, d = self.p, self.p.depth
-        for k in range(1, d):
-            self.send_four[k - 1] = self.triple(p.columns[k]).astype(self.mine.dtype)
-            self.push(self.send_four.at[k - 1], self.got_four.at[k - 1], 3 * d + k - 1, p.column_peers[k])
+        for i in turns or range(d - 1):
+            self.send_four[i] = self.triple(p.columns[i + 1]).astype(self.mine.dtype)
+            self.push(self.send_four.at[i], self.got_four.at[i], 3 * d + i, p.column_peers[i + 1])
 
     def fifth(self):
         p, d = self.p, self.p.depth
         value = self.triple(p.zed)
-        for k in range(1, d):
-            self.copy(self.send_four.at[k - 1], self.got_four.at[k - 1], 3 * d + k - 1, p.column_peers[k]).wait_recv()
-            value = value + self.got_four[k - 1].astype(F32)
+        for i in range(d - 1):
+            self.copy(self.send_four.at[i], self.got_four.at[i], 3 * d + i, p.column_peers[i + 1]).wait_recv()
+            value = value + self.got_four[i].astype(F32)
         self.total[...] = value
         self.push(self.total, self.joined, 4 * d - 1, p.sibling)
         self.out[:, half_of(self.out, p.core)] = value
@@ -602,8 +566,14 @@
         p, d = self.p, self.p.depth
         self.copy(self.total, self.joined, 4 * d - 1, p.sibling).wait_recv()
         self.out[:, half_of(self.out, 1 - p.core)] = self.joined[...]
-        for copy in self.sent:
-            copy.wait_send()
+        for z in range(d):
+            rows = self.got_one.at[pl.ds(4 * z, 4)]
+            self.copy(rows, rows, z, p.sibling).wait_send()
+            self.copy(self.send_two.at[z], self.got_two.at[z], d + z, p.far_peer).wait_send()
+            self.copy(self.send_three.at[z], self.got_three.at[z], 2 * d + z, p.near_peer).wait_send()
+            if z < d - 1:
+                self.copy(self.send_four.at[z], self.got_four.at[z], 3 * d + z, p.sibling).wait_send()
+        self.copy(self.total, self.joined, 4 * d - 1, p.sibling).wait_send()
 
 
 class Largest:
@@ -641,29 +611,22 @@
 
 
 def scatter_kernel(shards, *refs):
-    (attn, w1, w2, small, top, attn_out, w1_out, w2_out, small_out, top_out), scratch = refs[:10], refs[10:]
+    (attn, small, top, attn_out, small_out, top_out), scratch = refs[:6], refs[6:]
     p = Place(shards)
-    count = len(scratch) // 4
-    s, a, b, c = (
-        Scatter(p, full, out, scratch[13 * i : 13 * i + 13])
-        for i, (full, out) in enumerate(((small, small_out), (attn, attn_out), (w1, w1_out), (w2, w2_out)))
-    )
-    t = Largest(p, top, top_out, *scratch[52:])
+    s = Scatter(p, small, small_out, scratch[:13])
+    a = Scatter(p, attn, attn_out, scratch[13:26])
+    t = Largest(p, top, top_out, *scratch[26:])
     p.greet()
-    t.push(0)
-    for g in (s, c, b, a):
-        g.first()
-    s.second(), t.take(0), t.push(1), c.second(), s.third(), b.second(), c.third(), a.second(), b.third()
-    t.take(1), t.push(2), s.fourth(), c.fourth(), a.third(), b.fourth(), a.fourth()
-    t.take(2), t.push(3), s.fifth(), c.fifth(), b.fifth(), a.fifth(), t.take(3)
-    for g in (s, c, b, a):
-        g.finish()
-
-
-def scatter_all(shards, attn, w1, w2, small, top):
+    t.push(0), s.first(), a.first()
+    s.second(), t.take(0), t.push(1), a.second(), s.third(), t.take(1), t.push(2), a.third()
+    s.fourth(), t.take(2), t.push(3), a.fourth(), s.fifth(), t.take(3), a.fifth()
+    s.finish(), a.finish()
+
+
+def scatter_last(shards, attn, small, top):
     depth = shards // 4
-    arrays = ((small, F32), (attn, BF), (w1, BF), (w2, BF))
-    scratch = sum((Scatter.kinds(shards, x.shape[1], x.shape[2], dtype) for x, dtype in arrays), [])
+    scratch = Scatter.kinds(shards, small.shape[1], small.shape[2], F32)
+    scratch += Scatter.kinds(shards, attn.shape[1], attn.shape[2], BF)
     scratch += [
         pltpu.VMEM((depth + 2, 8, 128), F32), pltpu.VMEM((4, 8, 128), F32),
         pltpu.SemaphoreType.DMA((depth + 2,)), pltpu.SemaphoreType.DMA((depth + 2,)),
@@ -671,13 +634,178 @@
     anywhere, inside = pl.BlockSpec(memory_space=pl.ANY), pl.BlockSpec(memory_space=pltpu.VMEM)
     return pl.pallas_call(
         lambda *refs: scatter_kernel(shards, *refs),
-        in_specs=[anywhere] * 4 + [inside],
-        out_specs=[inside] * 5,
-        out_shape=[shaped(x.shape[1:], F32) for x in (attn, w1, w2, small)] + [shaped((8, 128), F32)],
+        in_specs=[anywhere] * 2 + [inside],
+        out_specs=[inside] * 3,
+        out_shape=[shaped(x.shape[1:], F32) for x in (attn, small)] + [shaped((8, 128), F32)],
         scratch_shapes=scratch,
-        compiler_params=pltpu.CompilerParams(collective_id=1, has_side_effects=True, vmem_limit_bytes=VMEM_LIMIT),
+        compiler_params=pltpu.CompilerParams(collective_id=2, has_side_effects=True, vmem_limit_bytes=VMEM_LIMIT),
         name="scatter",
-    )(attn, w1, w2, small, top)
+    )(attn, small, top)
+
+
+def enter_kernel(shards, width, steps, *refs):
+    tok_ref, wq, wk, wv, wo, w1, w2, small = refs[:8]
+    attn_out, w1_out, w2_out, small_out, vec_out = refs[8:13]
+    results = refs[13:20]
+    attn, tiles_in, local, send, recv, other = refs[20:]
+    step = pl.program_id(0)
+    p = Place(shards)
+    rows = wq.shape[0]
+    s, a, b, c = (
+        Gather(p, full, send.at[i], recv.at[i], other.at[i])
+        for i, full in enumerate((tiles_in, attn, w1_out, w2_out))
+    )
+    depth = p.depth
+
+    def start():
+        attn[p.me] = jnp.concatenate([w[...] for w in (wq, wk, wv, wo)], axis=0)
+        tiles_in[p.me] = small[...]
+        copies = [pltpu.make_async_copy(w, out.at[p.me], local.at[i]) for i, (w, out) in enumerate(((w1, w1_out), (w2, w2_out)))]
+        for copy in copies:
+            copy.start()
+        p.greet()
+        s.own(), a.own()
+        for copy in copies:
+            copy.wait()
+        b.own()
+        for g in (s, a):
+            for k in range(depth - 1):
+                g.column(k)
+        c.own()
+        for g in (s, a):
+            for k in range(depth):
+                g.plane(k)
+        for k in range(depth):
+            s.rest(k)
+        for k in range(depth):
+            a.rest(k)
+            if k < depth - 1:
+                b.column(k)
+        s.joined(), a.joined()
+        keep().start()
+        vec = jnp.zeros(vec_out.shape, F32)
+        blank = jnp.zeros((8, vec.shape[1] - 128), F32)
+        for i in range(shards):
+            piece = jnp.concatenate([tiles_in[i, :, :128], blank], axis=1)
+            vec = vec + (pltpu.roll(piece, i * rows, 1) if i else piece)
+        vec_out[...] = vec
+        small_out[...] = tiles_in[...]
+
+    def keep():
+        return pltpu.make_async_copy(attn, attn_out, local.at[2])
+
+    def end():
+        b.joined(), c.joined()
+        for g in (s, a, b, c):
+            g.drained()
+        keep().wait()
+
+    pl.when(step == 0)(start)
+    queue = (
+        [[(c.column, k), (b.plane, k)] for k in range(depth - 1)] + [[(b.plane, depth - 1)]]
+        + [[(b.rest, k), (c.plane, k)] for k in range(depth)] + [[(c.rest, k)] for k in range(depth)]
+    )
+    points = [(when, where) for when in range(steps) for where in (1, 2, 3)]
+    plan = {}
+    for i, events in enumerate(queue):
+        point = points[min(i, len(points) - 1)]
+        plan.setdefault(point, []).extend(functools.partial(event, k) for event, k in events)
+    plan.setdefault(points[-1], []).append(end)
+    view = [attn.at[:, i * rows : (i + 1) * rows, :] for i in range(4)]
+    attend_kernel(width, tok_ref, view, vec_out, *results, tick=ticker(plan, step))
+
+
+def enter(shards, tokens, wq, wk, wv, wo, w1, w2, small, heads):
+    rows, d = tokens.shape
+    t = min(ROWS, rows)
+    pairs = d // PAIR
+    blocks = rows // BLOCK
+    big = tiles(t, d)
+    sends = Gather.sends(shards)
+    anywhere = pl.BlockSpec(memory_space=pl.ANY)
+    packed = (shards, 4 * wq.shape[0], d)
+    full_small = (shards,) + small.shape
+    return pl.pallas_call(
+        lambda *refs: enter_kernel(shards, d // heads, rows // t, *refs),
+        grid=(rows // t,),
+        in_specs=[big] + [whole(w.shape) for w in (wq, wk, wv, wo, w1, w2, small)],
+        out_specs=[
+            anywhere, anywhere, anywhere, whole(full_small), whole((8, d)), big, big, big,
+            pl.BlockSpec((t // BLOCK, pairs, FRAMES, 2 * BLOCK), lambda i: (i, 0, 0, 0)),
+            big, big,
+            whole((pairs, FRAMES, 2 * BLOCK)),
+        ],
+        out_shape=[
+            shaped(packed, BF), shaped((shards,) + w1.shape, BF), shaped((shards,) + w2.shape, BF),
+            shaped(full_small, F32), shaped((8, d), F32),
+        ]
+        + [shaped((rows, d), BF)] * 3
+        + [shaped((blocks, pairs, FRAMES, 2 * BLOCK), F32), shaped((rows, d), BF), shaped((rows, d), F32)]
+        + [shaped((pairs, FRAMES, 2 * BLOCK), F32)],
+        scratch_shapes=[
+            pltpu.VMEM(packed, BF), pltpu.VMEM(full_small, F32), pltpu.SemaphoreType.DMA((3,)), pltpu.SemaphoreType.DMA((4, sends)),
+            pltpu.SemaphoreType.DMA((4, shards)), pltpu.SemaphoreType.DMA((4, shards)),
+        ],
+        compiler_params=pltpu.CompilerParams(
+            dimension_semantics=("arbitrary",), collective_id=0, has_side_effects=True, vmem_limit_bytes=VMEM_LIMIT
+        ),
+        name="enter",
+    )(tokens, wq, wk, wv, wo, w1, w2, small)
+
+
+BACK_ROWS = 256
+
+
+def leave_kernel(shards, width, steps, *refs):
+    ins, w_refs, vec_ref, w1g, w2g = refs[:7], refs[7:11], refs[11], refs[12], refs[13]
+    gt_ref, wg_ref, vg_ref, w1_out, w2_out = refs[14:19]
+    scratch, own = refs[19:27], refs[27:]
+    step = pl.program_id(0)
+    p = Place(shards)
+    b = Scatter(p, w1g, w1_out, own[:13])
+    c = Scatter(p, w2g, w2_out, own[13:26])
+    depth = p.depth
+    many = lambda event, *turns: functools.partial(event, *turns)
+    events = [(0, p.greet), (0, c.first), (0, b.first)]
+    for i in range(depth):
+        events += [(1 + i, many(c.second, i)), (5 + i, many(b.second, i)), (9 + i, many(c.third, i)), (16 + i, many(b.third, i))]
+    for i in range(depth - 1):
+        events += [(17 + i, many(c.fourth, i)), (24 + i, many(b.fourth, i))]
+    events += [(23, c.fifth)]
+    points = [(when, where) for when in range(steps) for where in range(4)]
+    plan = {}
+    for at, event in events:
+        plan.setdefault(points[at * len(points) // 32], []).append(event)
+    plan[(steps - 1, 4)] = [c.finish, b.fifth, b.finish]
+    back_kernel(width, *ins, w_refs, vec_ref, gt_ref, (wg_ref,), vg_ref, *scratch, tick=ticker(plan, step))
+
+
+def leave(shards, tokens, mg, q, k, v, p, mixed, attn, vec, w1g, w2g, heads):
+    rows, d = tokens.shape
+    t = min(BACK_ROWS, rows)
+    pairs = d // PAIR
+    big = tiles(t, d)
+    anywhere = pl.BlockSpec(memory_space=pl.ANY)
+    return pl.pallas_call(
+        lambda *refs: leave_kernel(shards, d // heads, rows // t, *refs),
+        grid=(rows // t,),
+        in_specs=[
+            big, big, big, big, big,
+            pl.BlockSpec((t // BLOCK, pairs, FRAMES, 2 * BLOCK), lambda i: (i, 0, 0, 0)),
+            big,
+        ] + weight_specs((attn,)) + [whole(vec.shape), anywhere, anywhere],
+        out_specs=[big, whole(attn.shape), whole((8, d)), whole(w1g.shape[1:]), whole(w2g.shape[1:])],
+        out_shape=[
+            shaped((rows, d), BF), shaped(attn.shape, BF), shaped((8, d), F32),
+            shaped(w1g.shape[1:], F32), shaped(w2g.shape[1:], F32),
+        ],
+        scratch_shapes=[pltpu.VMEM((d, d), F32)] * 4 + [pltpu.VMEM((t, d), BF)] * 4
+        + Scatter.kinds(shards, w1g.shape[1], w1g.shape[2], BF) + Scatter.kinds(shards, w2g.shape[1], w2g.shape[2], BF),
+        compiler_params=pltpu.CompilerParams(
+            dimension_semantics=("arbitrary",), collective_id=1, has_side_effects=True, vmem_limit_bytes=VMEM_LIMIT
+        ),
+        name="leave",
+    )(tokens, mg, q, k, v, p, mixed, *four((attn,)), vec, w1g, w2g)
 
 
 def on_device(shards, reps, *args):
@@ -708,22 +836,26 @@
             ],
             axis=1,
         )
-        attn, w1, w2, tile = gather_all(
-            shards, query_proj, key_proj, value_proj, output_proj, hidden_proj, final_proj, tile
+        attn, w1, w2, tile, vec, q, k, v, p, mixed, middle, top = enter(
+            shards, tokens, query_proj, key_proj, value_proj, output_proj, hidden_proj, final_proj, tile, heads
         )
-        weights = (attn,)
         w1, w2 = w1.reshape(d, hidden), w2.reshape(hidden, d)
-        vec = jnp.moveaxis(tile[:, :, :rows], 0, 1).reshape(8, d)
         hb = tile[:, :, 128 : 128 + more].reshape(1, hidden)
     else:
         weights = tuple(gather(x) for x in (query_proj, key_proj, value_proj, output_proj))
         w1, w2 = gather(hidden_proj), gather(final_proj)
         vec = jnp.stack([gather(x) for x in small]).astype(F32)
         hb = gather(hidden_bias).astype(F32)[None]
-    q, k, v, p, mixed, middle, top = attend(tokens, weights, vec, heads)
+        q, k, v, p, mixed, middle, top = attend(tokens, weights, vec, heads)
     local = jnp.max(top.reshape(top.shape[0], FRAMES, 2, BLOCK), axis=(1, 3)).reshape(heads)
     layer_output, mg, w1g, w2g, vg2, hbg = mlp(middle, grad_out, w1, w2, vec, hb)
-    grad_tokens, wg, vg1 = back(tokens, mg, q, k, v, p, mixed, weights, vec, heads)
+    if own:
+        grad_tokens, wg, vg1, w1g, w2g = leave(
+            shards, tokens, mg, q, k, v, p, mixed, attn, vec,
+            w1g.reshape(shards, -1, hidden), w2g.reshape(shards, -1, d), heads,
+        )
+    else:
+        grad_tokens, wg, vg1 = back(tokens, mg, q, k, v, p, mixed, weights, vec, heads)
     vg = jnp.concatenate([vg1[:5], vg2[:3]])
     if own:
         tile = jnp.concatenate(
@@ -733,9 +865,8 @@
             ],
             axis=2,
         )
-        attn, w1g, w2g, tile, top = scatter_all(
-            shards, wg[0], w1g.reshape(shards, -1, hidden), w2g.reshape(shards, -1, d), tile,
-            jnp.broadcast_to(jnp.pad(local, (0, 128 - heads))[None], (8, 128)),
+        attn, tile, top = scatter_last(
+            shards, wg, tile, jnp.broadcast_to(jnp.pad(local, (0, 128 - heads))[None], (8, 128))
         )
         wg = tuple(attn[i * rows : (i + 1) * rows] for i in range(4))
         vg = tuple(tile[i, :rows] for i in range(8))

time: 368 us -> 309 us (0.84)
  Pallas kernels: 347 us -> 288 us
    pallas_call x4 -> x3, Pallas kernels: 263 us -> 204 us  [the longest x1 83.7 us: leave(): pl.pallas_call(lambda *refs: leave_kernel(shards, d // heads, rows // t,...]
where the time goes in v3:
time: 309 us; the launch traced here: 307 us
  Pallas kernels  288 us (93%)
  local copies, waits for them, and re-layouts  10.8 us (3%)
  other arithmetic  7.54 us (2%)
    pallas_call x1, Pallas kernels, mlp(): pl.pallas_call(lambda *refs: mlp_kernel(768, *refs), grid=(rows // t,), i...  84.2 us
    pallas_call x1, Pallas kernels, leave(): pl.pallas_call(lambda *refs: leave_kernel(shards, d // heads, rows // t,...  83.7 us
    pallas_call x1, Pallas kernels, enter(): pl.pallas_call(lambda *refs: enter_kernel(shards, d // heads, rows // t,...  79.2 us
    pallas_call x1, Pallas kernels, scatter_last(): pl.pallas_call(lambda *refs: scatter_kernel(shards, *refs), in_specs=[any...  40.9 us

profile of v3, /device:TPU:0, one launch (start us, length us, event | category | flops | bytes accessed | tf_op | source)
XLA Modules:
  0.0 307.3 jit_solution(12046204709502799009)
XLA Ops:
  0.7 0.8 stack.35
  1.5 0.7 reshape.80
  2.2 0.6 fusion.3.refs_7_
  2.8 79.2 %enter.1 = (bf16[16,192,768]{2,1,0:T(8,128)(2,1)}, bf16[16,48,3072]{2,1,0:T(8,128)(2,1)}, bf16[16,192,768]{2,1,0:T(8,128)(2,1)}, f32[16,8,256]{2,1,0:T(8,128)}, ...) custom-call(bf16[2048,768]{1,0:T(8,128)(2,1)} %refs_0_.3, ...), custom_call_target="tpu_custom_call" | custom-call | tf_op jit(solution)/shard_map/enter/pallas_call | solution.py:728
  82.0 0.9 reduce_max.10
  83.1 0.6 broadcast_in_dim.4.refs_2_
  83.7 0.8 slice.51
  84.6 0.7 reshape.83.refs_5_
  85.3 84.2 %mlp.1 = (bf16[2048,768]{1,0:T(8,128)(2,1)}, f32[2048,768]{1,0:T(8,128)}, bf16[768,3072]{1,0:T(8,128)(2,1)}, bf16[3072,768]{1,0:T(8,128)(2,1)}, f32[8,768]{1,0:T(8,128)}, /*index=5*/f32[1,3072]{1,0:T(1,128)}) custom-call(f32[2048,768]{1,0:T(8,128)} %get-tuple-element.48.refs_0_, bf16[2048,768]{1,0:T(8,128)(2,1)} %refs_1_.3, bf16[768,3072]{1,0:T(8,128)(2,1)} %bitcast.47, ...), custom_call_target="tpu_custom_call" | custom-call | flops 57982058496 | bytes 22020096 | tf_op jit(solution)/shard_map/mlp/pallas_call | solution.py:321
  169.6 83.7 %leave.1 = (bf16[2048,768]{1,0:T(8,128)(2,1)}, bf16[16,192,768]{2,1,0:T(8,128)(2,1)}, f32[8,768]{1,0:T(8,128)}, f32[48,3072]{1,0:T(8,128)}, f32[192,768]{1,0:T(8,128)}) custom-call(bf16[2048,768]{1,0:T(8,128)(2,1)} %refs_0_.3, f32[2048,768]{1,0:T(8,128)} %get-tuple-element.54.refs_1_, bf16[2048,768]{1,0:T(8,128)(2,1)} %get-tuple-element.55.refs_2_, ...), custom_call_target="tpu_custom_call" | custom-call | tf_op jit(solution)/shard_map/leave/pallas_call | solution.py:789
  253.3 0.5 broadcast.31
  253.9 0.7 reduce.5
  254.6 0.7 pad_maximum_fusion
  255.5 0.7 select_maximum_fusion.refs_1_
  256.2 40.9 %scatter.1 = (f32[192,768]{1,0:T(8,128)}, f32[8,256]{1,0:T(8,128)}, f32[8,128]{1,0:T(8,128)}) custom-call(bf16[16,192,768]{2,1,0:T(8,128)(2,1)} %get-tuple-element.64.refs_0_, f32[16,8,256]{2,1,0:T(8,128)} %select_maximum_fusion.refs_1_, f32[8,128]{1,0:T(8,128)} %broadcast_in_dim.4.refs_2_), custom_call_target="tpu_custom_call" | custom-call | tf_op jit(solution)/shard_map/scatter/pallas_call | solution.py:635
  297.1 1.2 fusion.4
  298.3 0.7 slice.65
  299.0 1.5 slice_bitcast_fusion.1
  300.5 0.6 reshape.89
  301.3 0.6 dynamic-slice_multiply_fusion
  301.9 2.1 convert_multiply_fusion
  304.0 1.7 copy.47
  305.6 0.8 copy.48
  306.4 0.8 copy.49
  (28 shorter events, 0.6 us)
Async XLA Ops:
  169.5 84.3 %copy-start.5 = (f32[1,3072]{1,0:T(1,128)S(1)}, f32[1,3072]{1,0:T(1,128)}, u32[]{:S(2)}) copy-start(f32[1,3072]{1,0:T(1,128)} %get-tuple-element.67) | copy-start | bytes 36868
  169.5 85.0 %copy-start.6 = (f32[8,768]{1,0:T(8,128)S(1)}, f32[8,768]{1,0:T(8,128)}, u32[]{:S(2)}) copy-start(f32[8,768]{1,0:T(8,128)} %get-tuple-element.66) | copy-start | bytes 73732
  253.3 43.8 %copy-start.8 = (f32[12]{0:T(128)S(1)}, f32[12]{0:T(128)}, u32[]{:S(2)}) copy-start(f32[12]{0:T(128)} %param.35) | copy-start | bytes 148
  253.3 48.0 %copy-start.7 = (bf16[48]{0:T(256)(128)(2,1)S(1)}, bf16[48]{0:T(256)(128)(2,1)}, u32[]{:S(2)}) copy-start(bf16[48]{0:T(256)(128)(2,1)} %param.23) | copy-start | bytes 292
  253.3 48.6 %copy-start.3 = (bf16[48,768]{1,0:T(8,128)(2,1)S(1)}, bf16[48,768]{1,0:T(8,128)(2,1)}, u32[]{:S(2)}) copy-start(bf16[48,768]{1,0:T(8,128)(2,1)} %refs_1_.2) | copy-start | bytes 221188
  253.3 48.6 %copy-start.4 = (bf16[48,768]{1,0:T(8,128)(2,1)S(1)}, bf16[48,768]{1,0:T(8,128)(2,1)}, u32[]{:S(2)}) copy-start(bf16[48,768]{1,0:T(8,128)(2,1)} %refs_2_.1) | copy-start | bytes 221188
  256.2 47.8 %copy-start = (bf16[2048,768]{1,0:T(8,128)(2,1)S(1)}, bf16[2048,768]{1,0:T(8,128)(2,1)}, u32[]{:S(2)}) copy-start(bf16[2048,768]{1,0:T(8,128)(2,1)} %get-tuple-element.118) | copy-start | bytes 9437188
  303.9 1.7 copy-start.2
  304.0 2.5 copy-start.1

commit v4 on v1

--- a/solution.py
+++ b/solution.py
@@ -1,3 +1,4 @@
+import functools
 import math
 
 import jax
@@ -78,18 +79,27 @@
     return jnp.concatenate([wide[:, :BLOCK], wide[:, BLOCK:]], axis=0)
 
 
+def square(ref):
+    value = ref[...]
+    return value.reshape(-1, value.shape[-1])
+
+
 def attend_kernel(
-    width, tok_ref, wq_ref, wk_ref, wv_ref, wo_ref, vec_ref,
-    q_ref, k_ref, v_ref, p_ref, mix_ref, mid_ref, top_ref,
+    width, tok_ref, w_refs, vec_ref,
+    q_ref, k_ref, v_ref, p_ref, mix_ref, mid_ref, top_ref, one_ref=None, tick=lambda point: None,
 ):
     scale = 1.0 / math.sqrt(width)
+    wq, wk, wv = (square(w) for w in w_refs[:3])
     gain, shift = vec_ref[0:1], vec_ref[1:2]
     tok = tok_ref[...].astype(F32)
     unit, _ = normalise(tok)
     one = (unit * gain + shift).astype(BF)
-    q_ref[...] = (nn(one, wq_ref[...]) + vec_ref[2:3]).astype(BF)
-    k_ref[...] = nn(one, wk_ref[...]).astype(BF)
-    v_ref[...] = (nn(one, wv_ref[...]) + vec_ref[3:4]).astype(BF)
+    if one_ref is not None:
+        one_ref[...] = one
+    q_ref[...] = (nn(one, wq) + vec_ref[2:3]).astype(BF)
+    k_ref[...] = nn(one, wk).astype(BF)
+    v_ref[...] = (nn(one, wv) + vec_ref[3:4]).astype(BF)
+    tick(1)
     masks = place_masks()
     first, second = halves(width)
     pairs = tok_ref.shape[1] // PAIR
@@ -113,7 +123,9 @@
         return carry
 
     lax.fori_loop(0, tok_ref.shape[0] // BLOCK, body, 0)
-    mid_ref[...] = tok + (nn(mix_ref[...], wo_ref[...]) + vec_ref[4:5])
+    tick(2)
+    mid_ref[...] = tok_ref[...].astype(F32) + (nn(mix_ref[...], square(w_refs[3])) + vec_ref[4:5])
+    tick(3)
 
 
 def mlp_kernel(
@@ -172,30 +184,11 @@
         w2g_ref[...] = acc2[...].astype(BF)
 
 
-def back_kernel(
-    width, tok_ref, mg_ref, q_ref, k_ref, v_ref, p_ref, mix_ref,
-    wq_ref, wk_ref, wv_ref, wo_ref, vec_ref,
-    gt_ref, wqg_ref, wkg_ref, wvg_ref, wog_ref, vg_ref,
-    accq, acck, accv, acco, mgl_ref, dq_ref, dk_ref, dv_ref,
-):
-    step, last = pl.program_id(0), pl.num_programs(0) - 1
+def attention_back(width, mgl_ref, q_ref, k_ref, v_ref, p_ref, dq_ref, dk_ref, dv_ref):
     scale = 1.0 / math.sqrt(width)
-    gain, shift = vec_ref[0:1], vec_ref[1:2]
-    accs = (accq, acck, accv, acco)
-
-    @pl.when(step == 0)
-    def _():
-        for acc in accs:
-            acc[...] = jnp.zeros_like(acc)
-        vg_ref[...] = jnp.zeros_like(vg_ref)
-
-    branch = mg_ref[...].astype(BF)
-    mgl_ref[...] = nt(branch, wo_ref[...]).astype(BF)
-    acco[...] += tn(mix_ref[...], branch)
-    vg_ref[4:5] += column_sum(branch.astype(F32))
     masks = place_masks()
     first, second = halves(width)
-    pairs = tok_ref.shape[1] // PAIR
+    pairs = q_ref.shape[1] // PAIR
 
     def body(i, carry):
         rows = pl.ds(pl.multiple_of(i * BLOCK, BLOCK), BLOCK)
@@ -212,7 +205,31 @@
             dq_ref[rows, cols] = (tn(stack(wide), split(two_k, first, second)) * scale).astype(BF)
         return carry
 
-    lax.fori_loop(0, tok_ref.shape[0] // BLOCK, body, 0)
+    lax.fori_loop(0, q_ref.shape[0] // BLOCK, body, 0)
+
+
+def back_kernel(
+    width, tok_ref, mg_ref, q_ref, k_ref, v_ref, p_ref, mix_ref,
+    w_refs, vec_ref,
+    gt_ref, wg_refs, vg_ref,
+    accq, acck, accv, acco, mgl_ref, dq_ref, dk_ref, dv_ref,
+):
+    step, last = pl.program_id(0), pl.num_programs(0) - 1
+    gain, shift = vec_ref[0:1], vec_ref[1:2]
+    accs = (accq, acck, accv, acco)
+    wq, wk, wv, wo = (square(w) for w in w_refs)
+
+    @pl.when(step == 0)
+    def _():
+        for acc in accs:
+            acc[...] = jnp.zeros_like(acc)
+        vg_ref[...] = jnp.zeros_like(vg_ref)
+
+    branch = mg_ref[...].astype(BF)
+    mgl_ref[...] = nt(branch, wo).astype(BF)
+    acco[...] += tn(mix_ref[...], branch)
+    vg_ref[4:5] += column_sum(branch.astype(F32))
+    attention_back(width, mgl_ref, q_ref, k_ref, v_ref, p_ref, dq_ref, dk_ref, dv_ref)
     unit, inverse = normalise(tok_ref[...].astype(F32))
     one = (unit * gain + shift).astype(BF)
     dq, dk, dv = dq_ref[...], dk_ref[...], dv_ref[...]
@@ -221,15 +238,20 @@
     accq[...] += tn(one, dq)
     acck[...] += tn(one, dk)
     accv[...] += tn(one, dv)
-    grad = nt(dq, wq_ref[...]) + nt(dk, wk_ref[...]) + nt(dv, wv_ref[...])
+    grad = nt(dq, wq) + nt(dk, wk) + nt(dv, wv)
     vg_ref[0:1] += column_sum(grad * unit)
     vg_ref[1:2] += column_sum(grad)
     gt_ref[...] = (mg_ref[...] + norm_back(grad, unit, inverse, gain)).astype(BF)
 
     @pl.when(step == last)
     def _():
-        for out, acc in zip((wqg_ref, wkg_ref, wvg_ref, wog_ref), accs):
-            out[...] = acc[...].astype(BF)
+        for i, acc in enumerate(accs):
+            value = acc[...].astype(BF)
+            if len(wg_refs) == 1:
+                rows = wg_refs[0].shape[1] // 4
+                wg_refs[0][:, i * rows : (i + 1) * rows, :] = value.reshape(-1, rows, value.shape[1])
+            else:
+                wg_refs[i][...] = value
 
 
 def whole(shape):
@@ -253,17 +275,30 @@
     )
 
 
-def attend(tokens, wq, wk, wv, wo, vec, heads):
+def weight_specs(weights):
+    if len(weights) == 1:
+        shards, rows, d = weights[0].shape
+        return [
+            pl.BlockSpec((shards, rows // 4, d), lambda i, j=j: (0, j, 0), pipeline_mode=pl.Buffered(1))
+            for j in range(4)
+        ]
+    return [whole(w.shape) for w in weights]
+
+
+def four(weights):
+    return tuple(weights) * (4 // len(weights))
+
+
+def attend(tokens, weights, vec, heads):
     rows, d = tokens.shape
     t = min(ROWS, rows)
     pairs = d // PAIR
     blocks = rows // BLOCK
     big = tiles(t, d)
-    w = whole((d, d))
     return pl.pallas_call(
-        lambda *refs: attend_kernel(d // heads, *refs),
+        lambda tok, wq, wk, wv, wo, *refs: attend_kernel(d // heads, tok, (wq, wk, wv, wo), *refs),
         grid=(rows // t,),
-        in_specs=[big, w, w, w, w, whole(vec.shape)],
+        in_specs=[big] + weight_specs(weights) + [whole(vec.shape)],
         out_specs=[
             big, big, big,
             pl.BlockSpec((t // BLOCK, pairs, FRAMES, 2 * BLOCK), lambda i: (i, 0, 0, 0)),
@@ -276,7 +311,7 @@
         compiler_params=params(),
         cost_estimate=pl.CostEstimate(flops=10 * rows * d * d, bytes_accessed=24 * rows * d, transcendentals=0),
         name="attend",
-    )(tokens, wq, wk, wv, wo, vec)
+    )(tokens, *four(weights), vec)
 
 
 def mlp(middle, dy, w1, w2, vec, hb):
@@ -302,61 +337,854 @@
     )(middle, dy, w1, w2, vec, hb)
 
 
-def back(tokens, mg, q, k, v, p, mixed, wq, wk, wv, wo, vec, heads):
+def back(tokens, mg, q, k, v, p, mixed, weights, vec, heads):
     rows, d = tokens.shape
     t = min(ROWS, rows)
     pairs = d // PAIR
     big = tiles(t, d)
-    w = whole((d, d))
-    return pl.pallas_call(
-        lambda *refs: back_kernel(d // heads, *refs),
+    count = len(weights)
+
+    def kernel(*refs):
+        ins, w_refs, vec_ref, gt_ref = refs[:7], refs[7:11], refs[11], refs[12]
+        wg_refs, rest = refs[13 : 13 + count], refs[13 + count :]
+        back_kernel(d // heads, *ins, w_refs, vec_ref, gt_ref, wg_refs, *rest)
+
+    out = pl.pallas_call(
+        kernel,
         grid=(rows // t,),
         in_specs=[
             big, big, big, big, big,
             pl.BlockSpec((t // BLOCK, pairs, FRAMES, 2 * BLOCK), lambda i: (i, 0, 0, 0)),
-            big, w, w, w, w, whole(vec.shape),
-        ],
-        out_specs=[big, w, w, w, w, whole((8, d))],
-        out_shape=[shaped((rows, d), BF)] + [shaped((d, d), BF)] * 4 + [shaped((8, d), F32)],
+            big,
+        ] + weight_specs(weights) + [whole(vec.shape)],
+        out_specs=[big] + [whole(w.shape) for w in weights] + [whole((8, d))],
+        out_shape=[shaped((rows, d), BF)] + [shaped(w.shape, BF) for w in weights] + [shaped((8, d), F32)],
         scratch_shapes=[pltpu.VMEM((d, d), F32)] * 4 + [pltpu.VMEM((t, d), BF)] * 4,
         compiler_params=params(),
         cost_estimate=pl.CostEstimate(flops=20 * rows * d * d, bytes_accessed=24 * rows * d, transcendentals=0),
         name="back",
-    )(tokens, mg, q, k, v, p, mixed, wq, wk, wv, wo, vec)
-
-
-def on_device(
-    tokens, grad_out, first_gain, first_shift, query_proj, query_bias, key_proj, value_proj, value_bias,
-    output_proj, output_bias, second_gain, second_shift, hidden_proj, hidden_bias, final_proj, final_bias, threshold,
-):
+    )(tokens, mg, q, k, v, p, mixed, *four(weights), vec)
+    return out[0], out[1 : 1 + count], out[1 + count]
+
+
+MESH = pl.DeviceIdType.MESH
+
+
+class Place:
+    def __init__(self, shards):
+        self.shards = shards
+        self.depth = shards // 4
+        self.me = lax.axis_index("shard")
+        self.core = lax.axis_index("rep")
+        self.zed = self.me // 4
+        x, y = self.me % 2, (self.me // 2) % 2
+        self.near_step, self.far_step = 1 + self.core, 2 - self.core
+        self.near = x + self.core * (y - x)
+        self.far = y + self.core * (x - y)
+        self.sibling = (self.me, 1 - self.core)
+        self.near_peer = (self.block(self.zed, 1 - self.near, self.far), self.core)
+        self.far_peer = (self.block(self.zed, self.near, 1 - self.far), self.core)
+        self.columns = [lax.rem(self.zed + k, self.depth) for k in range(self.depth)]
+        self.column_peers = [(self.block(z, self.near, self.far), self.core) for z in self.columns]
+
+    def block(self, zed, near, far):
+        return zed * 4 + near * self.near_step + far * self.far_step
+
+    def greet(self):
+        barrier = pltpu.get_barrier_semaphore()
+        peers = [self.sibling, self.near_peer, self.far_peer] + self.column_peers[1:]
+        for peer in peers:
+            pl.semaphore_signal(barrier, inc=1, device_id=peer, device_id_type=MESH)
+        pl.semaphore_wait(barrier, len(peers))
+
+
+def half_of(ref, core):
+    width = ref.shape[-1] // 2
+    return pl.ds(pl.multiple_of(core * width, width), width)
+
+
+class Gather:
+    def kinds(depth, count):
+        return [pltpu.SemaphoreType.DMA((count, depth + 6)), pltpu.SemaphoreType.DMA((count, depth + 6))]
+
+    def __init__(self, place, full, sems, at, first=0, width=None):
+        self.p, self.full = place, full
+        self.send, self.recv = (sem.at[at] for sem in sems)
+        half = (width or full.shape[-1]) // 2
+        self.cols = pl.ds(pl.multiple_of(first + place.core * half, half), half)
+        self.here = place.near * place.near_step + place.far * place.far_step
+        self.there = (1 - place.near) * place.near_step + place.far * place.far_step
+        self.beyond = [near * place.near_step + (1 - place.far) * place.far_step for near in (place.near, 1 - place.near)]
+
+    def copy(self, slot):
+        p, d = self.p, self.p.depth
+        if slot < d - 1:
+            view, peer = self.full.at[p.zed, self.here, :, self.cols], p.column_peers[slot + 1]
+        elif slot < d + 1:
+            view, peer = self.full.at[:, self.here, :, self.cols], (p.near_peer, p.far_peer)[slot - d + 1]
+        elif slot == d + 1:
+            view, peer = self.full.at[:, self.there, :, self.cols], p.far_peer
+        else:
+            at = (self.here, self.there, *self.beyond)[slot - d - 2]
+            view, peer = self.full.at[:, at, :, self.cols], p.sibling
+        return pltpu.make_async_remote_copy(
+            src_ref=view, dst_ref=view, send_sem=self.send.at[slot], recv_sem=self.recv.at[slot],
+            device_id=peer, device_id_type=MESH,
+        )
+
+    def own(self):
+        for slot in range(self.p.depth - 1):
+            self.copy(slot).start()
+
+    def column(self):
+        d = self.p.depth
+        for slot in range(d - 1):
+            self.copy(slot).wait_recv()
+        for slot in (d - 1, d, d + 2):
+            self.copy(slot).start()
+
+    def plane(self):
+        d = self.p.depth
+        self.copy(d - 1).wait_recv()
+        self.copy(d + 1).start()
+        self.copy(d + 3).start()
+
+    def rest(self):
+        d = self.p.depth
+        for slot in (d, d + 1):
+            self.copy(slot).wait_recv()
+            self.copy(slot + 4).start()
+
+    def joined(self):
+        for slot in range(self.p.depth + 2, self.p.depth + 6):
+            self.copy(slot).wait_recv()
+
+    def drained(self):
+        for slot in range(self.p.depth + 6):
+            self.copy(slot).wait_send()
+
+
+def ticker(plan, step):
+    def tick(point):
+        for (when, where), events in plan.items():
+            if where == point:
+                @pl.when(step == when)
+                def _():
+                    for event in events:
+                        event()
+
+    return tick
+
+
+class Largest:
+    def __init__(self, place, own, out, got, kept, send, recv):
+        self.p, self.own, self.out, self.got, self.kept, self.send, self.recv = place, own, out, got, kept, send, recv
+        d = place.depth
+        self.stages = [
+            [(place.sibling, 0)], [(place.far_peer, 1)], [(place.near_peer, 2)],
+            [(place.column_peers[k], 2 + k) for k in range(1, d)],
+        ]
+
+    def copies(self, stage):
+        return [
+            pltpu.make_async_remote_copy(
+                src_ref=self.kept.at[stage], dst_ref=self.got.at[slot], send_sem=self.send.at[slot],
+                recv_sem=self.recv.at[slot], device_id=peer, device_id_type=MESH,
+            )
+            for peer, slot in self.stages[stage]
+        ]
+
+    def push(self, stage):
+        if stage == 0:
+            self.kept[0] = self.own[...]
+        for copy in self.copies(stage):
+            copy.start()
+
+    def take(self, stage):
+        value = self.kept[stage]
+        for copy, (_, slot) in zip(self.copies(stage), self.stages[stage]):
+            copy.wait_recv()
+            value = jnp.maximum(value, self.got[slot])
+        if stage == 3:
+            self.out[...] = value
+            for done in range(4):
+                for copy in self.copies(done):
+                    copy.wait_send()
+        else:
+            self.kept[stage + 1] = value
+
+
+class BlockSum:
+    def kinds(full, dtype, sets=1):
+        depth, _, rows, cols = full
+        one = (rows, cols // 2)
+        many = lambda *lead: pltpu.VMEM((sets,) + lead + one, dtype)
+        return [
+            many(depth, 4), many(2, depth), many(2, depth), many(depth), many(depth), many(depth - 1), many(depth - 1),
+            pltpu.VMEM((sets,) + one, F32), pltpu.VMEM((sets,) + one, F32),
+            pltpu.SemaphoreType.DMA((sets, 4 + depth)), pltpu.SemaphoreType.DMA((sets, 4 + depth)),
+        ]
+
+    def __init__(self, place, full, scratch, at=0):
+        self.p, self.full = place, full
+        (self.got_one, self.send_two, self.got_two, self.send_three, self.got_three, self.send_four, self.got_four,
+         self.total, self.joined, self.send, self.recv) = (ref.at[at] for ref in scratch)
+        self.dtype = scratch[0].dtype
+        self.cols, self.others = half_of(full, place.core), half_of(full, 1 - place.core)
+
+    def copy(self, slot):
+        p = self.p
+        if slot < 4:
+            src, dst, peer = (
+                (self.full.at[:, :, :, self.others], self.got_one, p.sibling),
+                (self.send_two.at[0], self.got_two.at[0], p.far_peer),
+                (self.send_two.at[1], self.got_two.at[1], p.far_peer),
+                (self.send_three, self.got_three, p.near_peer),
+            )[slot]
+        elif slot < 3 + p.depth:
+            src, dst, peer = self.send_four.at[slot - 4], self.got_four.at[slot - 4], p.column_peers[slot - 3]
+        else:
+            src, dst, peer = self.total, self.joined, p.sibling
+        return pltpu.make_async_remote_copy(
+            src_ref=src, dst_ref=dst, send_sem=self.send.at[slot], recv_sem=self.recv.at[slot],
+            device_id=peer, device_id_type=MESH,
+        )
+
+    def pair(self, near, far):
+        at = near * self.p.near_step + far * self.p.far_step
+        return self.full[:, at, :, self.cols].astype(F32) + self.got_one[:, at].astype(F32)
+
+    def first(self):
+        self.copy(0).start()
+
+    def second(self):
+        p = self.p
+        self.copy(0).wait_recv()
+        for slot, near in ((1, 1 - p.near), (0, p.near)):
+            at = near * p.near_step + (1 - p.far) * p.far_step
+            self.send_two[slot] = self.full[:, at, :, self.cols] + self.got_one[:, at]
+            self.copy(1 + slot).start()
+
+    def third(self):
+        p = self.p
+        self.copy(2).wait_recv()
+        self.send_three[...] = (self.pair(1 - p.near, p.far) + self.got_two[1].astype(F32)).astype(self.dtype)
+        self.copy(3).start()
+
+    def fourth(self):
+        p = self.p
+        self.copy(1).wait_recv()
+        self.copy(3).wait_recv()
+        self.copy(0).wait_send()
+        at = p.near * p.near_step + p.far * p.far_step
+
+        def value(z):
+            return (
+                self.full[z, at, :, self.cols].astype(F32) + self.got_one[z, at].astype(F32)
+                + self.got_two[0, z].astype(F32) + self.got_three[z].astype(F32)
+            )
+
+        for i in range(p.depth - 1):
+            self.send_four[i] = value(p.columns[i + 1]).astype(self.dtype)
+            self.copy(4 + i).start()
+        self.total[...] = value(p.zed)
+
+    def fifth(self):
+        p = self.p
+        value = self.total[...]
+        for i in range(p.depth - 1):
+            self.copy(4 + i).wait_recv()
+            value = value + self.got_four[i].astype(F32)
+        self.total[...] = value
+        self.copy(3 + p.depth).start()
+
+    def finish(self, write):
+        self.copy(3 + self.p.depth).wait_recv()
+        write(self.p.core, self.total[...])
+        write(1 - self.p.core, self.joined[...])
+        for slot in range(1, 4 + self.p.depth):
+            self.copy(slot).wait_send()
+
+
+def writer(ref, rows, first, width):
+    def write(core, value):
+        ref[rows, pl.ds(pl.multiple_of(first + core * width, width), width)] = value
+
+    return write
+
+
+def middle_kernel(shards, tall, *refs):
+    mid_hbm, dy_ref, own_ref, b0_hbm, w2_ref, vec_ref, hb_ref = refs[:7]
+    out_hbm, mg_hbm, bl_hbm, w2g_ref, w1g_ref, vg_ref, hbg_ref = refs[7:14]
+    inp_ref, act_ref, grad_ref, res_ref, two_ref, stage, w1_ref, fullb, local = refs[14:23]
+    sems, sums = refs[23:25], refs[25:]
+    j, p = pl.program_id(0), Place(shards)
+    depth = p.depth
+    chunk = w2_ref.shape[1] * 4
+    rows_all = dy_ref.shape[0]
+    turns = rows_all // tall
+    gain, shift = vec_ref[5:6], vec_ref[6:7]
+    root = math.sqrt(2.0 / math.pi)
+    weights = [
+        Gather(p, w1_ref, sems, k - 1, k * chunk, chunk) for k in range(1, depth)
+    ]
+    def blocks(k):
+        return BlockSum(p, fullb.at[lax.rem(k, 2)], sums, k)
+
+    def rows_of(t):
+        return pl.ds(pl.multiple_of(t * tall, tall), tall)
+
+    def fetch(t):
+        return pltpu.make_async_copy(mid_hbm.at[rows_of(t)], res_ref.at[rows_of(t)], local.at[t])
+
+    def again(t):
+        return pltpu.make_async_copy(mid_hbm.at[rows_of(t)], stage.at[t % 2], local.at[t])
+
+    def results(t):
+        return (
+            pltpu.make_async_copy(act_ref.at[rows_of(t)], out_hbm.at[rows_of(t)], local.at[turns + t]),
+            pltpu.make_async_copy(two_ref.at[rows_of(t)], mg_hbm.at[rows_of(t)], local.at[2 * turns + t]),
+        )
+
+    def first_chunk():
+        return pltpu.make_async_copy(b0_hbm, w1_ref.at[:, :, :, pl.ds(0, chunk)], local.at[3 * turns])
+
+    @pl.when(j == 0)
+    def _():
+        first_chunk().start()
+        for t in range(turns):
+            fetch(t).start()
+        w1_ref[p.zed, lax.rem(p.me, 4), :, pl.ds(chunk, (depth - 1) * chunk)] = own_ref[:, pl.ds(chunk, (depth - 1) * chunk)]
+        p.greet()
+        for w in weights:
+            w.own()
+        for t in range(turns):
+            fetch(t).wait()
+        first_chunk().wait()
+
+        def body(t, carry):
+            rows = rows_of(t)
+            unit, _ = normalise(res_ref[rows, :])
+            inp_ref[rows, :] = (unit * gain + shift).astype(BF)
+            two_ref[rows, :] = jnp.zeros((tall, two_ref.shape[1]), F32)
+            return carry
+
+        lax.fori_loop(0, turns, body, 0)
+
+    cols = pl.ds(pl.multiple_of(j * chunk, chunk), chunk)
+
+    def chunk_rows(t, carry):
+        rows = rows_of(t)
+        w1 = w1_ref[:, :, :, cols].reshape(-1, chunk)
+        w2 = w2_ref[...].reshape(chunk, -1)
+        z = nn(inp_ref[rows, :], w1) + hb_ref[...]
+        act_grad = nt(dy_ref[rows, :], w2)
+        square = z * z
+        bend = jnp.tanh(root * z * (1.0 + 0.044715 * square))
+        half = 0.5 * (1.0 + bend)
+        act = (z * half).astype(BF)
+        slope = half + 0.5 * z * (1.0 - bend * bend) * (root * (1.0 + 0.134145 * square))
+        grad = (act_grad * slope).astype(BF)
+        act_ref[rows, :] = act
+        grad_ref[rows, :] = grad
+        res_ref[rows, :] += nn(act, w2)
+        two_ref[rows, :] += nt(grad, w1)
+        hbg_ref[...] += column_sum(grad.astype(F32))
+
+        first, later = weights[0], weights[1:]
+
+        @pl.when(j == 0)
+        def _():
+            @pl.when(t == 0)
+            def _():
+                first.column()
+
+            @pl.when(t == 1)
+            def _():
+                first.plane()
+                for w in later:
+                    w.column()
+
+            pl.when(t == 2)(first.rest)
+
+            @pl.when(t == 3)
+            def _():
+                for w in later:
+                    w.plane()
+
+        @pl.when((j == 1) & (t == 0))
+        def _():
+            for w in later:
+                w.rest()
+
+        @pl.when(j > 0)
+        def _():
+            pl.when(t == 0)(blocks(j - 1).second)
+            pl.when(t == 2)(blocks(j - 1).third)
+
+            @pl.when(j > 1)
+            def _():
+                pl.when(t == 1)(blocks(j - 2).fifth)
+
+        return carry
+
+    hbg_ref[...] = jnp.zeros_like(hbg_ref)
+    lax.fori_loop(0, turns, chunk_rows, 0)
+    for k, w in enumerate(weights):
+        pl.when(j == k)(w.joined)
+
+    w2g_ref[...] = tn(act_ref[...], dy_ref[...]).astype(BF).reshape(w2g_ref.shape)
+    fullb[lax.rem(j, 2)] = tn(inp_ref[...], grad_ref[...]).astype(BF).reshape(fullb.shape[1:])
+
+    @pl.when(j < depth - 1)
+    def _():
+        blocks(j).first()
+
+    @pl.when(j > 0)
+    def _():
+        blocks(j - 1).fourth()
+
+    @pl.when(j == depth - 1)
+    def _():
+        last = pltpu.make_async_copy(fullb.at[(depth - 1) % 2], bl_hbm, local.at[3 * turns])
+        last.start()
+        again(0).start()
+        vg_ref[...] = jnp.zeros_like(vg_ref)
+        for t in range(turns):
+            rows = rows_of(t)
+            if t + 1 < turns:
+                again(t + 1).start()
+            again(t).wait()
+            unit, inverse = normalise(stage[t % 2])
+            two, up = two_ref[rows, :], dy_ref[rows, :].astype(F32)
+            vg_ref[0:1] += column_sum(two * unit)
+            vg_ref[1:2] += column_sum(two)
+            vg_ref[2:3] += column_sum(up)
+            act_ref[rows, :] = (res_ref[rows, :] + vec_ref[7:8]).astype(BF)
+            two_ref[rows, :] = up + norm_back(two, unit, inverse, gain)
+            for copy in results(t):
+                copy.start()
+        blocks(depth - 2).fifth()
+        for t in range(turns):
+            for copy in results(t):
+                copy.wait()
+        last.wait()
+        for w in weights:
+            w.drained()
+        for k in range(depth - 1):
+            blocks(k).finish(writer(w1g_ref, slice(None), k * chunk, chunk // 2))
+
+
+def middle(shards, mid, dy, w1_own, b0, w2, vec, hb):
+    rows, d = mid.shape
+    depth = shards // 4
+    hidden = w1_own.shape[1]
+    chunk = hidden // depth
+    tall = min(ROWS, rows)
+    turns = rows // tall
+    less = depth - 1
+    anywhere = pl.BlockSpec(memory_space=pl.ANY)
+    fullb = (depth, 4, w1_own.shape[0], chunk)
+    w1g = (w1_own.shape[0], less * chunk)
+    return pl.pallas_call(
+        lambda *refs: middle_kernel(shards, tall, *refs),
+        grid=(depth,),
+        in_specs=[
+            anywhere, whole(dy.shape), whole(w1_own.shape), anywhere,
+            pl.BlockSpec((4,) + w2.shape[1:], lambda j: (j, 0, 0)), whole(vec.shape), pl.BlockSpec((1, chunk), lambda j: (0, j)),
+        ],
+        out_specs=[
+            anywhere, anywhere, anywhere, pl.BlockSpec((4,) + w2.shape[1:], lambda j: (j, 0, 0)), whole(w1g), whole((8, d)),
+            pl.BlockSpec((1, chunk), lambda j: (0, j)),
+        ],
+        out_shape=[
+            shaped((rows, d), BF), shaped((rows, d), F32), shaped(fullb, BF), shaped(w2.shape, BF), shaped(w1g, F32),
+            shaped((8, d), F32), shaped((1, hidden), F32),
+        ],
+        scratch_shapes=[
+            pltpu.VMEM((rows, d), BF), pltpu.VMEM((rows, chunk), BF), pltpu.VMEM((rows, chunk), BF),
+            pltpu.VMEM((rows, d), F32), pltpu.VMEM((rows, d), F32), pltpu.VMEM((2, tall, d), F32),
+            pltpu.VMEM((depth, 4) + w1_own.shape, BF), pltpu.VMEM((2,) + fullb, BF),
+            pltpu.SemaphoreType.DMA((3 * turns + 1,)),
+        ] + Gather.kinds(depth, less) + BlockSum.kinds(fullb, BF, less),
+        compiler_params=pltpu.CompilerParams(
+            dimension_semantics=("arbitrary",), collective_id=3, has_side_effects=True, vmem_limit_bytes=VMEM_LIMIT
+        ),
+        name="middle",
+    )(mid, dy, w1_own, b0, w2, vec, hb)
+
+
+def enter_kernel(shards, width, steps, *refs):
+    tok_ref, wq, wk, wv, wo, w1, w2, small = refs[:8]
+    attn_out, w1_out, w2_out, small_out, vec_out = refs[8:13]
+    results = refs[13:21]
+    attn, tiles_in, local = refs[21:24]
+    sems = refs[24:26]
+    step = pl.program_id(0)
+    p = Place(shards)
+    depth = p.depth
+    rows = wq.shape[0]
+    s, b, c, *early = (
+        Gather(p, full, sems, i)
+        for i, full in enumerate(
+            [tiles_in, w1_out, w2_out] + [attn.at[:, :, i * rows : (i + 1) * rows] for i in range(4)]
+        )
+    )
+    early.insert(0, s)
+
+    def start():
+        mine = p.zed, lax.rem(p.me, 4)
+        copies = [
+            pltpu.make_async_copy(w, out.at[mine], local.at[i])
+            for i, (w, out) in enumerate(((w1, w1_out), (w2, w2_out)))
+        ]
+        for copy in copies:
+            copy.start()
+        attn[mine] = jnp.concatenate([w[...] for w in (wq, wk, wv, wo)], axis=0)
+        tiles_in[mine] = small[...]
+        for copy in copies:
+            copy.wait()
+        p.greet()
+        for g in early + [b, c]:
+            g.own()
+        for g in early:
+            g.column()
+        for g in early:
+            g.plane()
+        b.column()
+        for g in early:
+            g.rest()
+        b.plane()
+        for g in early[:-1]:
+            g.joined()
+        vec = jnp.zeros(vec_out.shape, F32)
+        blank = jnp.zeros((8, vec.shape[1] - 128), F32)
+        for i in range(shards):
+            piece = jnp.concatenate([tiles_in[i // 4, i % 4, :, :128], blank], axis=1)
+            vec = vec + (pltpu.roll(piece, i * rows, 1) if i else piece)
+        vec_out[...] = vec
+        small_out[...] = tiles_in[...]
+
+    def keep():
+        return pltpu.make_async_copy(attn, attn_out, local.at[2])
+
+    def whole_attn():
+        early[-1].joined()
+        keep().start()
+
+    def end():
+        b.joined(), c.joined()
+        for g in early + [b, c]:
+            g.drained()
+        keep().wait()
+
+    pl.when(step == 0)(start)
+    plan = {(0, 1): [whole_attn, c.column], (0, 2): [b.rest], (steps // 2 - 1, 3): [c.plane], (steps - 1, 2): [c.rest], (steps - 1, 3): [end]}
+    view = [attn.at[:, :, i * rows : (i + 1) * rows, :] for i in range(4)]
+    attend_kernel(width, tok_ref, view, vec_out, *results, tick=ticker(plan, step))
+
+
+def enter(shards, tokens, wq, wk, wv, wo, w1, w2, small, heads):
+    rows, d = tokens.shape
+    t = min(ROWS, rows)
+    pairs = d // PAIR
+    blocks = rows // BLOCK
+    big = tiles(t, d)
+    depth = shards // 4
+    lead = (depth, 4)
+    anywhere = pl.BlockSpec(memory_space=pl.ANY)
+    packed = lead + (4 * wq.shape[0], d)
+    full_small = lead + small.shape
+    chunk = w1.shape[1] // depth
+    return pl.pallas_call(
+        lambda *refs: enter_kernel(shards, d // heads, rows // t, *refs),
+        grid=(rows // t,),
+        in_specs=[big] + [whole(w.shape) for w in (wq, wk, wv, wo)] + [whole((w1.shape[0], chunk))] + [whole(w.shape) for w in (w2, small)],
+        out_specs=[
+            anywhere, anywhere, anywhere, whole(full_small), whole((8, d)), big, big, big,
+            pl.BlockSpec((t // BLOCK, pairs, FRAMES, 2 * BLOCK), lambda i: (i, 0, 0, 0)),
+            big, big,
+            whole((pairs, FRAMES, 2 * BLOCK)), big,
+        ],
+        out_shape=[
+            shaped(packed, BF), shaped(lead + (w1.shape[0], chunk), BF), shaped(lead + w2.shape, BF),
+            shaped(full_small, F32), shaped((8, d), F32),
+        ]
+        + [shaped((rows, d), BF)] * 3
+        + [shaped((blocks, pairs, FRAMES, 2 * BLOCK), F32), shaped((rows, d), BF), shaped((rows, d), F32)]
+        + [shaped((pairs, FRAMES, 2 * BLOCK), F32), shaped((rows, d), BF)],
+        scratch_shapes=[
+            pltpu.VMEM(packed, BF), pltpu.VMEM(full_small, F32), pltpu.SemaphoreType.DMA((3,)),
+        ] + Gather.kinds(depth, 7),
+        compiler_params=pltpu.CompilerParams(
+            dimension_semantics=("arbitrary",), collective_id=0, has_side_effects=True, vmem_limit_bytes=VMEM_LIMIT
+        ),
+        name="enter",
+    )(tokens, wq, wk, wv, wo, w1, w2, small)
+
+
+def leave_kernel(shards, width, steps, *refs):
+    mg_ref, q_ref, k_ref, v_ref, p_ref, mix_ref, wo_ref, fullb, fullc = refs[:9]
+    dq_ref, dk_ref, dv_ref, wog_ref, vg_ref, w1_out, w2_out = refs[9:16]
+    acco, mgl_ref = refs[16:18]
+    own = refs[18:]
+    step, p = pl.program_id(0), Place(shards)
+    rows = fullc.shape[2] // 2
+    b = BlockSum(p, fullb, own[:11])
+    c = BlockSum(p, fullc.at[:, :, :rows], own[11:22])
+    e = BlockSum(p, fullc.at[:, :, rows:], own[22:33])
+
+    def finish():
+        wide = w2_out.shape[1] // 2
+        c.finish(writer(w2_out, slice(0, rows), 0, wide))
+        e.finish(writer(w2_out, slice(rows, None), 0, wide))
+        b.finish(writer(w1_out, slice(None), 0, w1_out.shape[1] // 2))
+
+    events = [
+        (0, p.greet), (0, c.first), (0, e.first), (0, b.first), (1, c.second), (2, e.second), (3, b.second),
+        (5, c.third), (6, e.third), (7, b.third), (8, c.fourth), (9, e.fourth), (9, b.fourth), (11, c.fifth),
+        (11, e.fifth), (11, b.fifth),
+    ]
+    points = [(when, where) for when in range(steps) for where in range(3)]
+    plan = {}
+    for at, event in events:
+        plan.setdefault(points[at * len(points) // 12], []).append(event)
+    tick = ticker(plan, step)
+
+    @pl.when(step == 0)
+    def _():
+        acco[...] = jnp.zeros_like(acco)
+        vg_ref[...] = jnp.zeros_like(vg_ref)
+
+    tick(0)
+    branch = mg_ref[...].astype(BF)
+    mgl_ref[...] = nt(branch, square(wo_ref)).astype(BF)
+    acco[...] += tn(mix_ref[...], branch)
+    vg_ref[4:5] += column_sum(branch.astype(F32))
+    tick(1)
+    attention_back(width, mgl_ref, q_ref, k_ref, v_ref, p_ref, dq_ref, dk_ref, dv_ref)
+    vg_ref[2:3] += column_sum(dq_ref[...].astype(F32))
+    vg_ref[3:4] += column_sum(dv_ref[...].astype(F32))
+    tick(2)
+
+    @pl.when(step == steps - 1)
+    def _():
+        wog_ref[...] = acco[...].astype(BF).reshape(wog_ref.shape)
+        finish()
+
+
+def leave(shards, mg, q, k, v, p, mixed, attn, fullb, fullc, heads):
+    rows, d = mg.shape
+    t = min(ROWS, rows)
+    pairs = d // PAIR
+    big = tiles(t, d)
+    half = fullc.shape[:2] + (fullc.shape[2] // 2, fullc.shape[3])
+    w1_out, w2_out = fullb.shape[2:], fullc.shape[2:]
+    wog = (shards // 4, 4, attn.shape[1] // 4, d)
+    return pl.pallas_call(
+        lambda *refs: leave_kernel(shards, d // heads, rows // t, *refs),
+        grid=(rows // t,),
+        in_specs=[
+            big, big, big, big,
+            pl.BlockSpec((t // BLOCK, pairs, FRAMES, 2 * BLOCK), lambda i: (i, 0, 0, 0)),
+            big, weight_specs((attn,))[3], whole(fullb.shape), whole(fullc.shape),
+        ],
+        out_specs=[big, big, big, whole(wog), whole((8, d)), whole(w1_out), whole(w2_out)],
+        out_shape=[shaped((rows, d), BF)] * 3
+        + [shaped(wog, BF), shaped((8, d), F32), shaped(w1_out, F32), shaped(w2_out, F32)],
+        scratch_shapes=[pltpu.VMEM((d, d), F32), pltpu.VMEM((t, d), BF)]
+        + BlockSum.kinds(fullb.shape, BF) + BlockSum.kinds(half, BF) + BlockSum.kinds(half, BF),
+        compiler_params=pltpu.CompilerParams(
+            dimension_semantics=("arbitrary",), collective_id=1, has_side_effects=True, vmem_limit_bytes=VMEM_LIMIT
+        ),
+        name="leave",
+    )(mg, q, k, v, p, mixed, attn, fullb, fullc)
+
+
+def last_kernel(shards, steps, *refs):
+    tok_ref, mg_ref, dq_hbm, dk_hbm, dv_hbm, one_hbm, wq, wk, wv, vec_ref, wog_ref, vgin_ref, hbt_ref, top_ref = refs[:14]
+    gt_ref, attn_out, small_out, top_out = refs[14:18]
+    d_ref, one_ref, full, tile, vg, local = refs[18:24]
+    jobs, little, most = refs[24:35], refs[35:46], refs[46:]
+    step, p = pl.program_id(0), Place(shards)
+    rows = wog_ref.shape[2]
+    wide = attn_out.shape[1] // 2
+    o = BlockSum(p, wog_ref, jobs, 3)
+    s = BlockSum(p, tile, little)
+    t = Largest(p, top_ref, top_out, *most)
+    weight = lambda i: BlockSum(p, full.at[i], jobs, i)
+    fetches = [
+        pltpu.make_async_copy(src, dst, local.at[i])
+        for i, (src, dst) in enumerate(
+            ((dq_hbm, d_ref.at[0]), (dk_hbm, d_ref.at[1]), (dv_hbm, d_ref.at[2]), (one_hbm, one_ref))
+        )
+    ]
+
+    @pl.when(step == 0)
+    def _():
+        for i in (3, 0, 1, 2):
+            fetches[i].start()
+        vg[...] = vgin_ref[...]
+        p.greet()
+        o.first(), t.push(0)
+        fetches[3].wait()
+
+    for i in range(3):
+        pl.when(step == i)(fetches[i].wait)
+
+    @pl.when(step < 3)
+    def _():
+        full[step] = tn(one_ref[...], d_ref[step]).astype(BF).reshape(full.shape[1:])
+        weight(step).first()
+
+    @pl.when(step >= 3)
+    def _():
+        tall = tok_ref.shape[0]
+        at = pl.ds(pl.multiple_of((step - 3) * tall, tall), tall)
+        unit, inverse = normalise(tok_ref[...].astype(F32))
+        grad = nt(d_ref[0, at], square(wq)) + nt(d_ref[1, at], square(wk)) + nt(d_ref[2, at], square(wv))
+        vg[0:1] += column_sum(grad * unit)
+        vg[1:2] += column_sum(grad)
+        gt_ref[...] = (mg_ref[...] + norm_back(grad, unit, inverse, vec_ref[0:1])).astype(BF)
+
+    def end():
+        d = vg.shape[1]
+        value = vg[...]
+        for i in range(shards):
+            piece = pltpu.roll(value, d - i * rows, 1) if i else value
+            tile[i // 4, i % 4, :, :128] = piece[:, :128]
+        tile[:, :, :, 128:] = hbt_ref[...]
+        s.first()
+        weight(2).fourth()
+        s.second()
+        o.fifth(), weight(0).fifth()
+        s.third()
+        weight(1).fifth()
+        s.fourth()
+        weight(2).fifth()
+        s.fifth()
+        for i, job in ((3, o), (0, weight(0)), (1, weight(1)), (2, weight(2))):
+            job.finish(writer(attn_out, slice(i * rows, (i + 1) * rows), 0, wide))
+        s.finish(writer(small_out, slice(None), 0, small_out.shape[1] // 2))
+
+    q, k, v = weight(0), weight(1), weight(2)
+    events = [
+        (0, o.second), (1, q.second), (1, lambda: t.take(0)), (1, lambda: t.push(1)), (2, k.second), (2, o.third),
+        (3, v.second), (3, q.third), (3, lambda: t.take(1)), (3, lambda: t.push(2)), (4, o.fourth), (4, k.third),
+        (4, lambda: t.take(2)), (4, lambda: t.push(3)), (5, v.third), (5, q.fourth), (6, k.fourth), (6, lambda: t.take(3)),
+    ]
+    plan = {}
+    for at, event in events:
+        plan.setdefault((min(at, steps - 1), 0), []).append(event)
+    plan.setdefault((steps - 1, 0), []).append(end)
+    ticker(plan, step)(0)
+
+
+def last(shards, tokens, mg, dq, dk, dv, one, attn, vec, wog, vgin, hbt, top):
+    rows, d = tokens.shape
+    t = min(ROWS, rows)
+    depth = shards // 4
+    steps = 3 + rows // t
+    later = pl.BlockSpec((t, d), lambda i: (jnp.maximum(i - 3, 0), 0))
+    anywhere = pl.BlockSpec(memory_space=pl.ANY)
+    small = (depth, 4, 8, 256)
+    return pl.pallas_call(
+        lambda *refs: last_kernel(shards, steps, *refs),
+        grid=(steps,),
+        in_specs=[later, later] + [anywhere] * 4 + weight_specs((attn,))[:3]
+        + [whole(x.shape) for x in (vec, wog, vgin, hbt, top)],
+        out_specs=[later, whole((4 * wog.shape[2], d)), whole((8, 256)), whole((8, 128))],
+        out_shape=[
+            shaped((rows, d), BF), shaped((4 * wog.shape[2], d), F32), shaped((8, 256), F32), shaped((8, 128), F32),
+        ],
+        scratch_shapes=[
+            pltpu.VMEM((3, rows, d), BF), pltpu.VMEM((rows, d), BF), pltpu.VMEM((3,) + wog.shape, BF),
+            pltpu.VMEM(small, F32), pltpu.VMEM((8, d), F32), pltpu.SemaphoreType.DMA((4,)),
+        ] + BlockSum.kinds(wog.shape, BF, 4) + BlockSum.kinds(small, F32) + [
+            pltpu.VMEM((depth + 2, 8, 128), F32), pltpu.VMEM((4, 8, 128), F32),
+            pltpu.SemaphoreType.DMA((depth + 2,)), pltpu.SemaphoreType.DMA((depth + 2,)),
+        ],
+        compiler_params=pltpu.CompilerParams(
+            dimension_semantics=("arbitrary",), collective_id=2, has_side_effects=True, vmem_limit_bytes=VMEM_LIMIT
+        ),
+        name="last",
+    )(tokens, mg, dq, dk, dv, one, attn, attn, attn, vec, wog, vgin, hbt, top)
+
+
+def on_device(shards, reps, *args):
+    (
+        tokens, grad_out, first_gain, first_shift, query_proj, query_bias, key_proj, value_proj, value_bias,
+        output_proj, output_bias, second_gain, second_shift, hidden_proj, hidden_bias, final_proj, final_bias, threshold,
+    ) = args
+    heads = threshold.shape[0]
+    d = tokens.shape[1]
+    hidden = hidden_proj.shape[1]
+    head_dim = d // heads
+    small = (first_gain, first_shift, query_bias, value_bias, output_bias, second_gain, second_shift, final_bias)
+    rows, more = small[0].shape[0], hidden_bias.shape[0] // 8
+    whole_chunks = shards % 4 == 0 and hidden * 4 % (shards * 256) == 0 and hidden * 4 // shards == 4 * final_proj.shape[0]
+    own = whole_chunks and reps == 2 and shards % 4 == 0 and shards > 4 and rows % 16 == 0 and rows <= 128 and more <= 128
+
     def gather(x):
         return lax.all_gather(x, "shard", axis=0, tiled=True)
-
-    heads = threshold.shape[0]
-    wq, wk, wv, wo = (gather(x) for x in (query_proj, key_proj, value_proj, output_proj))
-    small = (first_gain, first_shift, query_bias, value_bias, output_bias, second_gain, second_shift, final_bias)
-    vec = jnp.stack([gather(x) for x in small]).astype(F32)
-    hb = gather(hidden_bias).astype(F32)[None]
-    w1, w2 = gather(hidden_proj), gather(final_proj)
-    q, k, v, p, mixed, middle, top = attend(tokens, wq, wk, wv, wo, vec, heads)
-    head_dim = tokens.shape[1] // heads
-    local = jnp.max(top.reshape(top.shape[0], FRAMES, 2, BLOCK), axis=(1, 3)).reshape(heads)
-    global_max = lax.pmax(local, ("shard", "rep"))
-    layer_output, mg, w1g, w2g, vg2, hbg = mlp(middle, grad_out, w1, w2, vec, hb)
-    grad_tokens, wqg, wkg, wvg, wog, vg1 = back(tokens, mg, q, k, v, p, mixed, wq, wk, wv, wo, vec, heads)
 
     def scatter(x):
         y = lax.psum_scatter(x.astype(BF), "shard", scatter_dimension=0, tiled=True)
         return lax.psum(y, "rep").astype(F32)
 
+    if own:
+        tile = jnp.concatenate(
+            [
+                jnp.pad(jnp.stack(small).astype(F32), ((0, 0), (0, 128 - rows))),
+                jnp.pad(hidden_bias.astype(F32).reshape(8, more), ((0, 0), (0, 128 - more))),
+            ],
+            axis=1,
+        )
+        attn, w1, w2, tile, vec, q, k, v, p, mixed, mid, top, one = enter(
+            shards, tokens, query_proj, key_proj, value_proj, output_proj, hidden_proj, final_proj, tile, heads
+        )
+        tile = tile.reshape(shards, 8, -1)
+        hb = tile[:, :, 128 : 128 + more].reshape(1, hidden)
+        attn, w2 = attn.reshape(shards, -1, d), w2.reshape(shards, -1, d)
+    else:
+        weights = tuple(gather(x) for x in (query_proj, key_proj, value_proj, output_proj))
+        w1, w2 = gather(hidden_proj), gather(final_proj)
+        vec = jnp.stack([gather(x) for x in small]).astype(F32)
+        hb = gather(hidden_bias).astype(F32)[None]
+        q, k, v, p, mixed, mid, top = attend(tokens, weights, vec, heads)
+    local = jnp.max(top.reshape(top.shape[0], FRAMES, 2, BLOCK), axis=(1, 3)).reshape(heads)
+    if own:
+        layer_output, mg, b3g, w2g, w1g, vg2, hbg = middle(shards, mid, grad_out, hidden_proj, w1, w2, vec, hb)
+        dq, dk, dv, wog, vg1, w1l, w2g = leave(
+            shards, mg, q, k, v, p, mixed, attn, b3g, w2g.reshape(shards // 4, 4, -1, d), heads
+        )
+        hbt = jnp.pad(hbg.reshape(shards // 4, 4, 8, more), ((0, 0), (0, 0), (0, 0), (0, 128 - more)))
+        grad_tokens, attn, tile, top = last(
+            shards, tokens, mg, dq, dk, dv, one, attn, vec, wog, jnp.concatenate([vg1[:5], vg2[:3]]), hbt,
+            jnp.broadcast_to(jnp.pad(local, (0, 128 - heads))[None], (8, 128)),
+        )
+        w1g = jnp.concatenate([w1g, w1l], axis=1)
+    else:
+        layer_output, mg, w1g, w2g, vg2, hbg = mlp(mid, grad_out, w1, w2, vec, hb)
+        grad_tokens, wg, vg1 = back(tokens, mg, q, k, v, p, mixed, weights, vec, heads)
+    if own:
+        wg = tuple(attn[i * rows : (i + 1) * rows] for i in range(4))
+        vg = tuple(tile[i, :rows] for i in range(8))
+        hbg = tile[:, 128 : 128 + more].reshape(-1)
+        global_max = top[0, :heads]
+    else:
+        vg = jnp.concatenate([vg1[:5], vg2[:3]])
+        global_max = lax.pmax(local, ("shard", "rep"))
+        wg = tuple(scatter(x) for x in wg)
+        w1g, w2g = scatter(w1g), scatter(w2g)
+        vg = tuple(scatter(vg[i]) for i in range(8))
+        hbg = scatter(hbg[0])
     factor = jnp.minimum(1.0, threshold / global_max)
     column_scale = jnp.repeat(jnp.sqrt(factor), head_dim)
-    shard_rows = query_bias.shape[0]
-    bias_scale = lax.dynamic_slice_in_dim(column_scale, lax.axis_index("shard") * shard_rows, shard_rows)
+    bias_scale = lax.dynamic_slice_in_dim(column_scale, lax.axis_index("shard") * rows, rows)
     return (
-        layer_output, grad_tokens, scatter(vg1[0]), scatter(vg1[1]), scatter(wqg), scatter(vg1[2]), scatter(wkg),
-        scatter(wvg), scatter(vg1[3]), scatter(wog), scatter(vg1[4]), scatter(vg2[0]), scatter(vg2[1]), scatter(w1g),
-        scatter(hbg[0]), scatter(w2g), scatter(vg2[2]), global_max, factor,
+        layer_output, grad_tokens, vg[0], vg[1], wg[0], vg[2], wg[1], wg[2], vg[3], wg[3], vg[4], vg[5], vg[6],
+        w1g, hbg, w2g, vg[7], global_max, factor,
         query_proj.astype(F32) * column_scale[None, :], query_bias.astype(F32) * bias_scale,
         key_proj.astype(F32) * column_scale[None, :],
     )
@@ -407,6 +1235,7 @@
         P("shard"),
         P("shard", None),
     )
+    shards, reps = mesh.shape["shard"], mesh.shape["rep"]
     return jax.shard_map(
-        on_device, mesh=mesh, in_specs=in_specs, out_specs=out_specs, check_vma=False
+        functools.partial(on_device, shards, reps), mesh=mesh, in_specs=in_specs, out_specs=out_specs, check_vma=False
     )

time: 1440 us -> 297 us (0.21)
  waiting for transfers between devices: 1030 us -> 0 us
  blocking collectives: 196 us -> 0 us
  Pallas kernels: 170 us -> 273 us
  between operations: 16.8 us -> 0.8 us
    reduce_scatter x6 -> x0, waiting for transfers between devices: 747 us -> none  [scatter(): y = lax.psum_scatter(x.astype(BF), 'shard', scatter_dimension=0, tiled=True)]
    all_gather x6 -> x0, waiting for transfers between devices: 275 us -> none  [gather(): return lax.all_gather(x, 'shard', axis=0, tiled=True)]
    unnamed x2 -> x0, blocking collectives: 154 us -> none
    pallas_call x3 -> x4, Pallas kernels: 170 us -> 273 us  [the longest x1 96.6 us: middle(): pl.pallas_call(lambda *refs: middle_kernel(shards, tall, *refs), grid=(de...]
    pmax x1 -> x0, blocking collectives: 39.4 us -> none  [on_device(): global_max = lax.pmax(local, ('shard', 'rep'))]
    convert_element_type x17 -> x0, other arithmetic: 15.2 us -> none  [the longest x15 14.5 us: scatter(): return lax.psum(y, 'rep').astype(F32)]
  transfers between devices with their start and end apart: 13 -> 0, of which waited for: 11 -> 0; matrix products, arithmetic and copies ran while one was open for 1% -> 0% of each run, Pallas kernels for 2% -> 0%
where the time goes in v4:
time: 297 us; the launch traced here: 296 us
  Pallas kernels  273 us (92%)
  local copies, waits for them, and re-layouts  13.5 us (5%)
  other arithmetic  9.35 us (3%)
    pallas_call x1, Pallas kernels, middle(): pl.pallas_call(lambda *refs: middle_kernel(shards, tall, *refs), grid=(de...  96.6 us
    pallas_call x1, Pallas kernels, enter(): pl.pallas_call(lambda *refs: enter_kernel(shards, d // heads, rows // t,...  79.4 us
    pallas_call x1, Pallas kernels, leave(): pl.pallas_call(lambda *refs: leave_kernel(shards, d // heads, rows // t,...  51.1 us
    pallas_call x1, Pallas kernels, last(): pl.pallas_call(lambda *refs: last_kernel(shards, steps, *refs), grid=(ste...  45.6 us

profile of v4, /device:TPU:0, one launch (start us, length us, event | category | flops | bytes accessed | tf_op | source)
XLA Modules:
  0.0 296.4 jit_solution(4959955722227732166)
XLA Ops:
  0.7 0.8 stack.35
  1.5 0.7 reshape.77
  2.2 0.6 fusion.3.refs_7_
  2.8 79.4 %enter.1 = (bf16[4,4,192,768]{3,2,1,0:T(8,128)(2,1)}, bf16[4,4,48,768]{3,2,1,0:T(8,128)(2,1)}, bf16[4,4,192,768]{3,2,1,0:T(8,128)(2,1)}, f32[4,4,8,256]{3,2,1,0:...) custom-call(bf16[2048,768]{1,0:T(8,128)(2,1)} %refs_0_.3, ...), custom_call_target="tpu_custom_call" | custom-call | tf_op jit(solution)/shard_map/enter/pallas_call | solution.py:899
  82.2 0.9 reduce_max.10
  83.3 0.6 broadcast_in_dim.4.refs_13_
  83.9 0.8 slice.68
  84.8 0.7 reshape.80.refs_6_
  85.5 96.6 %middle.1 = (bf16[2048,768]{1,0:T(8,128)(2,1)}, f32[2048,768]{1,0:T(8,128)}, bf16[4,4,48,768]{3,2,1,0:T(8,128)(2,1)}, bf16[16,192,768]{2,1,0:T(8,128)(2,1)}, f32...) custom-call(f32[2048,768]{1,0:T(8,128)} %get-tuple-element.53.refs_0_, bf16[2048,768]{1,0:T(8,128)(2,1)} %refs_1_.3, ...), custom_call_target="tpu_custom_call" | custom-call | tf_op jit(solution)/shard_map/middle/pallas_call | solution.py:789
  182.1 51.1 %leave.1 = (bf16[2048,768]{1,0:T(8,128)(2,1)}, bf16[2048,768]{1,0:T(8,128)(2,1)}, bf16[2048,768]{1,0:T(8,128)(2,1)}, bf16[4,4,48,768]{3,2,1,0:T(8,128)(2,1)}, f3...) custom-call(f32[2048,768]{1,0:T(8,128)} %get-tuple-element.59.refs_0_.refs_1_, ...), custom_call_target="tpu_custom_call" | custom-call | tf_op jit(solution)/shard_map/leave/pallas_call | solution.py:984
  233.7 0.7 reduce.5
  234.4 1.4 pad_maximum_fusion.1.refs_11_
  235.9 0.6 pad.20.refs_12_
  236.6 45.6 %last.1 = (bf16[2048,768]{1,0:T(8,128)(2,1)}, f32[192,768]{1,0:T(8,128)}, f32[8,256]{1,0:T(8,128)}, f32[8,128]{1,0:T(8,128)}) custom-call(bf16[2048,768]{1,0:T(8,128)(2,1)} %refs_0_.3, f32[2048,768]{1,0:T(8,128)} %get-tuple-element.59.refs_0_.refs_1_, bf16[2048,768]{1,0:T(8,128)(2,1)} %get-tuple-element.68.refs_2_, ...), custom_call_target="tpu_custom_call" | custom-call | tf_op jit(solution)/shard_map/last/pallas_call | solution.py:1091
  282.2 1.2 fusion.4
  283.4 0.7 slice.65
  284.1 1.5 slice_bitcast_fusion.1
  285.6 0.6 reshape.85
  287.0 1.9 pad_maximum_fusion
  288.9 2.1 convert_multiply_fusion
  290.9 1.7 copy.43
  292.6 1.4 copy-done.1
  293.9 1.7 copy.44
  295.6 0.8 copy.45
  (29 shorter events, 1.5 us)
Async XLA Ops:
  182.1 51.7 %copy-start.6 = (f32[1,3072]{1,0:T(1,128)S(1)}, f32[1,3072]{1,0:T(1,128)}, u32[]{:S(2)}) copy-start(f32[1,3072]{1,0:T(1,128)} %get-tuple-element.75) | copy-start | bytes 36868
  182.1 52.3 %copy-start.7 = (f32[8,768]{1,0:T(8,128)S(1)}, f32[8,768]{1,0:T(8,128)}, u32[]{:S(2)}) copy-start(f32[8,768]{1,0:T(8,128)} %get-tuple-element.74) | copy-start | bytes 73732
  236.5 45.7 %copy-start.9 = (f32[12]{0:T(128)S(1)}, f32[12]{0:T(128)}, u32[]{:S(2)}) copy-start(f32[12]{0:T(128)} %param.35) | copy-start | bytes 148
  236.5 49.9 %copy-start.8 = (bf16[48]{0:T(256)(128)(2,1)S(1)}, bf16[48]{0:T(256)(128)(2,1)}, u32[]{:S(2)}) copy-start(bf16[48]{0:T(256)(128)(2,1)} %param.23) | copy-start | bytes 292
  236.5 50.5 %copy-start.5 = (f32[48,768]{1,0:T(8,128)S(1)}, f32[48,768]{1,0:T(8,128)}, u32[]{:S(2)}) copy-start(f32[48,768]{1,0:T(8,128)} %get-tuple-element.81) | copy-start | bytes 442372
  236.5 52.3 %copy-start.3 = (bf16[48,768]{1,0:T(8,128)(2,1)S(1)}, bf16[48,768]{1,0:T(8,128)(2,1)}, u32[]{:S(2)}) copy-start(bf16[48,768]{1,0:T(8,128)(2,1)} %refs_1_.2) | copy-start | bytes 221188
  236.5 52.3 %copy-start.4 = (bf16[48,768]{1,0:T(8,128)(2,1)S(1)}, bf16[48,768]{1,0:T(8,128)(2,1)}, u32[]{:S(2)}) copy-start(bf16[48,768]{1,0:T(8,128)(2,1)} %refs_2_.2) | copy-start | bytes 221188
  236.6 54.4 %copy-start = (bf16[2048,768]{1,0:T(8,128)(2,1)S(1)}, bf16[2048,768]{1,0:T(8,128)(2,1)}, u32[]{:S(2)}) copy-start(bf16[2048,768]{1,0:T(8,128)(2,1)} %get-tuple-element.127) | copy-start | bytes 9437188
  290.9 3.0 %copy-start.1 = (bf16[2048,768]{1,0:T(8,128)(2,1)S(1)}, bf16[2048,768]{1,0:T(8,128)(2,1)}, u32[]{:S(2)}) copy-start(bf16[2048,768]{1,0:T(8,128)(2,1)} %get-tuple-element.128) | copy-start | bytes 9437188
  293.9 1.7 copy-start.2

commit v5 on v4

--- a/solution.py
+++ b/solution.py
@@ -476,6 +476,49 @@
     return tick
 
 
+class Direct:
+    def kinds(shards):
+        return [
+            pltpu.VMEM((shards, 8, 128), F32), pltpu.VMEM((2 * shards, 8, 128), F32),
+            pltpu.SemaphoreType.DMA((2 * shards,)), pltpu.SemaphoreType.DMA((2 * shards,)),
+        ]
+
+    def __init__(self, place, scratch):
+        self.tiles, self.got, self.send, self.recv = scratch
+        self.count = 2 * place.shards
+        self.at = 2 * place.me + place.core
+        self.me = place.me
+
+    def greet(self):
+        barrier = pltpu.get_barrier_semaphore()
+        for k in range(1, self.count):
+            other = lax.rem(self.at + k, self.count)
+            pl.semaphore_signal(barrier, inc=1, device_id=(other // 2, lax.rem(other, 2)), device_id_type=MESH)
+        pl.semaphore_wait(barrier, self.count - 1)
+
+    def copy(self, k, slot):
+        other = lax.rem(self.at + k, self.count)
+        return pltpu.make_async_remote_copy(
+            src_ref=self.tiles.at[other // 2], dst_ref=self.got.at[slot], send_sem=self.send.at[k],
+            recv_sem=self.recv.at[slot], device_id=(other // 2, lax.rem(other, 2)), device_id_type=MESH,
+        )
+
+    def push(self):
+        for k in range(1, self.count):
+            self.copy(k, self.at).start()
+
+    def sum(self):
+        self.got[self.at] = self.tiles[self.me]
+        for k in range(1, self.count):
+            self.copy(k, lax.rem(self.at + k, self.count)).wait_recv()
+        value = self.got[0]
+        for i in range(1, self.count):
+            value = value + self.got[i]
+        for k in range(1, self.count):
+            self.copy(k, self.at).wait_send()
+        return value
+
+
 class Largest:
     def __init__(self, place, own, out, got, kept, send, recv):
         self.p, self.own, self.out, self.got, self.kept, self.send, self.recv = place, own, out, got, kept, send, recv
@@ -606,6 +649,80 @@
             self.copy(slot).wait_send()
 
 
+class OwnerSum(BlockSum):
+    def kinds(full, dtype, depth, sets=1):
+        _, _, rows, cols = full
+        one = (rows, cols // 2)
+        many = lambda *lead: pltpu.VMEM((sets,) + lead + one, dtype)
+        return [
+            many(1, 4), many(2, 1), many(2, 1), many(1), many(1), many(), pltpu.VMEM((depth - 1,) + one, dtype),
+            pltpu.VMEM(one, F32), pltpu.VMEM(one, F32),
+            pltpu.SemaphoreType.DMA((sets, 4 + depth)), pltpu.SemaphoreType.DMA((sets, 4 + depth)),
+        ]
+
+    def __init__(self, place, full, scratch, at, target):
+        self.p, self.full = place, full
+        self.got_one, self.send_two, self.got_two, self.send_three, self.got_three, self.send_four = (
+            ref.at[at] for ref in scratch[:6]
+        )
+        self.got_four, self.total, self.joined = scratch[6:9]
+        self.send, self.recv = (ref.at[at] for ref in scratch[9:])
+        self.dtype = scratch[0].dtype
+        self.cols, self.others = half_of(full, place.core), half_of(full, 1 - place.core)
+        self.away = lax.rem(target - place.zed + place.depth, place.depth)
+        self.target = target
+
+    def line(self, away):
+        p = self.p
+        return pltpu.make_async_remote_copy(
+            src_ref=self.send_four, dst_ref=self.got_four.at[away - 1], send_sem=self.send.at[3 + away],
+            recv_sem=self.recv.at[3 + away], device_id=(p.block(self.target, p.near, p.far), p.core), device_id_type=MESH,
+        )
+
+    def fourth(self):
+        p = self.p
+        self.copy(1).wait_recv()
+        self.copy(3).wait_recv()
+        self.copy(0).wait_send()
+        value = self.pair(p.near, p.far)[0] + self.got_two[0, 0].astype(F32) + self.got_three[0].astype(F32)
+
+        @pl.when(self.away == 0)
+        def _():
+            self.total[...] = value
+
+        @pl.when(self.away > 0)
+        def _():
+            self.send_four[...] = value.astype(self.dtype)
+            self.line(self.away).start()
+
+    def fifth(self):
+        @pl.when(self.away == 0)
+        def _():
+            value = self.total[...]
+            for away in range(1, self.p.depth):
+                self.line(away).wait_recv()
+                value = value + self.got_four[away - 1].astype(F32)
+            self.total[...] = value
+            self.copy(3 + self.p.depth).start()
+
+    def finish(self, write):
+        last = self.copy(3 + self.p.depth)
+
+        @pl.when(self.away == 0)
+        def _():
+            last.wait_recv()
+            write(self.p.core, self.total[...])
+            write(1 - self.p.core, self.joined[...])
+            last.wait_send()
+
+        @pl.when(self.away > 0)
+        def _():
+            self.line(self.away).wait_send()
+
+        for slot in range(1, 4):
+            self.copy(slot).wait_send()
+
+
 def writer(ref, rows, first, width):
     def write(core, value):
         ref[rows, pl.ds(pl.multiple_of(first + core * width, width), width)] = value
@@ -615,9 +732,9 @@
 
 def middle_kernel(shards, tall, *refs):
     mid_hbm, dy_ref, own_ref, b0_hbm, w2_ref, vec_ref, hb_ref = refs[:7]
-    out_hbm, mg_hbm, bl_hbm, w2g_ref, w1g_ref, vg_ref, hbg_ref = refs[7:14]
-    inp_ref, act_ref, grad_ref, res_ref, two_ref, stage, w1_ref, fullb, local = refs[14:23]
-    sems, sums = refs[23:25], refs[25:]
+    act_hbm, mg_hbm, bl_hbm, cl_hbm, w2g_ref, w1g_ref, vg_ref, hbg_ref = refs[7:15]
+    inp_ref, act_ref, grad_ref, two_ref, stage, w1_ref, fullb, fullc, local = refs[15:24]
+    sems, sums = refs[24:26], refs[26:]
     j, p = pl.program_id(0), Place(shards)
     depth = p.depth
     chunk = w2_ref.shape[1] * 4
@@ -629,22 +746,23 @@
         Gather(p, w1_ref, sems, k - 1, k * chunk, chunk) for k in range(1, depth)
     ]
     def blocks(k):
-        return BlockSum(p, fullb.at[lax.rem(k, 2)], sums, k)
+        return (
+            OwnerSum(p, fullc.at[lax.rem(k, 2)], sums[11:], k, k),
+            BlockSum(p, fullb.at[lax.rem(k, 2)], sums[:11], k),
+        )
+
+    def each(k, stage, *args):
+        for job in blocks(k):
+            getattr(job, stage)(*args)
 
     def rows_of(t):
         return pl.ds(pl.multiple_of(t * tall, tall), tall)
 
-    def fetch(t):
-        return pltpu.make_async_copy(mid_hbm.at[rows_of(t)], res_ref.at[rows_of(t)], local.at[t])
-
     def again(t):
         return pltpu.make_async_copy(mid_hbm.at[rows_of(t)], stage.at[t % 2], local.at[t])
 
     def results(t):
-        return (
-            pltpu.make_async_copy(act_ref.at[rows_of(t)], out_hbm.at[rows_of(t)], local.at[turns + t]),
-            pltpu.make_async_copy(two_ref.at[rows_of(t)], mg_hbm.at[rows_of(t)], local.at[2 * turns + t]),
-        )
+        return pltpu.make_async_copy(two_ref.at[rows_of(t)], mg_hbm.at[rows_of(t)], local.at[2 * turns + t])
 
     def first_chunk():
         return pltpu.make_async_copy(b0_hbm, w1_ref.at[:, :, :, pl.ds(0, chunk)], local.at[3 * turns])
@@ -652,24 +770,20 @@
     @pl.when(j == 0)
     def _():
         first_chunk().start()
-        for t in range(turns):
-            fetch(t).start()
+        again(0).start()
         w1_ref[p.zed, lax.rem(p.me, 4), :, pl.ds(chunk, (depth - 1) * chunk)] = own_ref[:, pl.ds(chunk, (depth - 1) * chunk)]
         p.greet()
         for w in weights:
             w.own()
         for t in range(turns):
-            fetch(t).wait()
-        first_chunk().wait()
-
-        def body(t, carry):
+            if t + 1 < turns:
+                again(t + 1).start()
+            again(t).wait()
             rows = rows_of(t)
-            unit, _ = normalise(res_ref[rows, :])
+            unit, _ = normalise(stage[t % 2])
             inp_ref[rows, :] = (unit * gain + shift).astype(BF)
             two_ref[rows, :] = jnp.zeros((tall, two_ref.shape[1]), F32)
-            return carry
-
-        lax.fori_loop(0, turns, body, 0)
+        first_chunk().wait()
 
     cols = pl.ds(pl.multiple_of(j * chunk, chunk), chunk)
 
@@ -687,7 +801,6 @@
         grad = (act_grad * slope).astype(BF)
         act_ref[rows, :] = act
         grad_ref[rows, :] = grad
-        res_ref[rows, :] += nn(act, w2)
         two_ref[rows, :] += nt(grad, w1)
         hbg_ref[...] += column_sum(grad.astype(F32))
 
@@ -719,35 +832,44 @@
 
         @pl.when(j > 0)
         def _():
-            pl.when(t == 0)(blocks(j - 1).second)
-            pl.when(t == 2)(blocks(j - 1).third)
-
-            @pl.when(j > 1)
-            def _():
-                pl.when(t == 1)(blocks(j - 2).fifth)
+            pl.when(t == 0)(functools.partial(each, j - 1, "second"))
+            pl.when(t == 3)(functools.partial(each, j - 1, "third"))
 
         return carry
 
     hbg_ref[...] = jnp.zeros_like(hbg_ref)
     lax.fori_loop(0, turns, chunk_rows, 0)
+    store = pltpu.make_async_copy(act_ref, act_hbm.at[:, cols], local.at[turns])
+    store.start()
     for k, w in enumerate(weights):
         pl.when(j == k)(w.joined)
 
-    w2g_ref[...] = tn(act_ref[...], dy_ref[...]).astype(BF).reshape(w2g_ref.shape)
+    fullc[lax.rem(j, 2)] = tn(act_ref[...], dy_ref[...]).astype(BF).reshape(fullc.shape[1:])
     fullb[lax.rem(j, 2)] = tn(inp_ref[...], grad_ref[...]).astype(BF).reshape(fullb.shape[1:])
 
+    store.wait()
+
     @pl.when(j < depth - 1)
     def _():
-        blocks(j).first()
+        each(j, "first")
+
+    @pl.when(j > 1)
+    def _():
+        each(j - 2, "fifth")
 
     @pl.when(j > 0)
     def _():
-        blocks(j - 1).fourth()
+        each(j - 1, "fourth")
 
     @pl.when(j == depth - 1)
     def _():
-        last = pltpu.make_async_copy(fullb.at[(depth - 1) % 2], bl_hbm, local.at[3 * turns])
-        last.start()
+        lasts = (
+            pltpu.make_async_copy(fullb.at[(depth - 1) % 2], bl_hbm, local.at[3 * turns]),
+            pltpu.make_async_copy(fullc.at[(depth - 1) % 2], cl_hbm, local.at[3 * turns + 1]),
+        )
+        for copy in lasts:
+            copy.start()
+        w2g_ref[...] = jnp.zeros_like(w2g_ref)
         again(0).start()
         vg_ref[...] = jnp.zeros_like(vg_ref)
         for t in range(turns):
@@ -760,19 +882,19 @@
             vg_ref[0:1] += column_sum(two * unit)
             vg_ref[1:2] += column_sum(two)
             vg_ref[2:3] += column_sum(up)
-            act_ref[rows, :] = (res_ref[rows, :] + vec_ref[7:8]).astype(BF)
             two_ref[rows, :] = up + norm_back(two, unit, inverse, gain)
-            for copy in results(t):
-                copy.start()
-        blocks(depth - 2).fifth()
+            results(t).start()
+        each(depth - 2, "fifth")
         for t in range(turns):
-            for copy in results(t):
-                copy.wait()
-        last.wait()
+            results(t).wait()
+        for copy in lasts:
+            copy.wait()
         for w in weights:
             w.drained()
         for k in range(depth - 1):
-            blocks(k).finish(writer(w1g_ref, slice(None), k * chunk, chunk // 2))
+            c, b = blocks(k)
+            c.finish(writer(w2g_ref, slice(None), 0, w2g_ref.shape[1] // 2))
+            b.finish(writer(w1g_ref, slice(None), k * chunk, chunk // 2))
 
 
 def middle(shards, mid, dy, w1_own, b0, w2, vec, hb):
@@ -786,6 +908,7 @@
     anywhere = pl.BlockSpec(memory_space=pl.ANY)
     fullb = (depth, 4, w1_own.shape[0], chunk)
     w1g = (w1_own.shape[0], less * chunk)
+    fullc = (1, 4) + w2.shape[1:]
     return pl.pallas_call(
         lambda *refs: middle_kernel(shards, tall, *refs),
         grid=(depth,),
@@ -794,19 +917,20 @@
             pl.BlockSpec((4,) + w2.shape[1:], lambda j: (j, 0, 0)), whole(vec.shape), pl.BlockSpec((1, chunk), lambda j: (0, j)),
         ],
         out_specs=[
-            anywhere, anywhere, anywhere, pl.BlockSpec((4,) + w2.shape[1:], lambda j: (j, 0, 0)), whole(w1g), whole((8, d)),
+            anywhere, anywhere, anywhere, anywhere, whole(w2.shape[1:]), whole(w1g), whole((8, d)),
             pl.BlockSpec((1, chunk), lambda j: (0, j)),
         ],
         out_shape=[
-            shaped((rows, d), BF), shaped((rows, d), F32), shaped(fullb, BF), shaped(w2.shape, BF), shaped(w1g, F32),
+            shaped((rows, hidden), BF), shaped((rows, d), F32), shaped(fullb, BF), shaped(fullc, BF), shaped(w2.shape[1:], F32),
+            shaped(w1g, F32),
             shaped((8, d), F32), shaped((1, hidden), F32),
         ],
         scratch_shapes=[
             pltpu.VMEM((rows, d), BF), pltpu.VMEM((rows, chunk), BF), pltpu.VMEM((rows, chunk), BF),
-            pltpu.VMEM((rows, d), F32), pltpu.VMEM((rows, d), F32), pltpu.VMEM((2, tall, d), F32),
+            pltpu.VMEM((rows, d), F32), pltpu.VMEM((2, tall, d), F32),
             pltpu.VMEM((depth, 4) + w1_own.shape, BF), pltpu.VMEM((2,) + fullb, BF),
-            pltpu.SemaphoreType.DMA((3 * turns + 1,)),
-        ] + Gather.kinds(depth, less) + BlockSum.kinds(fullb, BF, less),
+            pltpu.VMEM((2,) + fullc, BF), pltpu.SemaphoreType.DMA((3 * turns + 2,)),
+        ] + Gather.kinds(depth, less) + BlockSum.kinds(fullb, BF, less) + OwnerSum.kinds(fullc, BF, depth, less),
         compiler_params=pltpu.CompilerParams(
             dimension_semantics=("arbitrary",), collective_id=3, has_side_effects=True, vmem_limit_bytes=VMEM_LIMIT
         ),
@@ -924,26 +1048,26 @@
 
 
 def leave_kernel(shards, width, steps, *refs):
-    mg_ref, q_ref, k_ref, v_ref, p_ref, mix_ref, wo_ref, fullb, fullc = refs[:9]
-    dq_ref, dk_ref, dv_ref, wog_ref, vg_ref, w1_out, w2_out = refs[9:16]
-    acco, mgl_ref = refs[16:18]
-    own = refs[18:]
+    mg_ref, q_ref, k_ref, v_ref, p_ref, mix_ref, wo_ref, fullb, fullc, w1_in, w2_in = refs[:11]
+    dq_ref, dk_ref, dv_ref, wog_ref, vg_ref, w1_out, w2_out = refs[11:18]
+    acco, mgl_ref = refs[18:20]
+    own = refs[20:]
     step, p = pl.program_id(0), Place(shards)
-    rows = fullc.shape[2] // 2
     b = BlockSum(p, fullb, own[:11])
-    c = BlockSum(p, fullc.at[:, :, :rows], own[11:22])
-    e = BlockSum(p, fullc.at[:, :, rows:], own[22:33])
+    c = OwnerSum(p, fullc, own[11:22], 0, p.depth - 1)
+    wide = fullb.shape[3]
+
+    def others():
+        w1_out[:, : (p.depth - 1) * wide] = w1_in[...]
+        w2_out[...] = w2_in[...]
 
     def finish():
-        wide = w2_out.shape[1] // 2
-        c.finish(writer(w2_out, slice(0, rows), 0, wide))
-        e.finish(writer(w2_out, slice(rows, None), 0, wide))
-        b.finish(writer(w1_out, slice(None), 0, w1_out.shape[1] // 2))
+        c.finish(writer(w2_out, slice(None), 0, w2_out.shape[1] // 2))
+        b.finish(writer(w1_out, slice(None), (p.depth - 1) * wide, wide // 2))
 
     events = [
-        (0, p.greet), (0, c.first), (0, e.first), (0, b.first), (1, c.second), (2, e.second), (3, b.second),
-        (5, c.third), (6, e.third), (7, b.third), (8, c.fourth), (9, e.fourth), (9, b.fourth), (11, c.fifth),
-        (11, e.fifth), (11, b.fifth),
+        (0, p.greet), (0, c.first), (0, b.first), (1, others), (2, c.second), (2, b.second), (5, c.third), (5, b.third),
+        (8, c.fourth), (8, b.fourth), (11, c.fifth), (11, b.fifth),
     ]
     points = [(when, where) for when in range(steps) for where in range(3)]
     plan = {}
@@ -973,13 +1097,12 @@
         finish()
 
 
-def leave(shards, mg, q, k, v, p, mixed, attn, fullb, fullc, heads):
+def leave(shards, mg, q, k, v, p, mixed, attn, fullb, fullc, w1g, w2g, heads):
     rows, d = mg.shape
     t = min(ROWS, rows)
     pairs = d // PAIR
     big = tiles(t, d)
-    half = fullc.shape[:2] + (fullc.shape[2] // 2, fullc.shape[3])
-    w1_out, w2_out = fullb.shape[2:], fullc.shape[2:]
+    w1_out, w2_out = (w1g.shape[0], shards // 4 * fullb.shape[3]), w2g.shape
     wog = (shards // 4, 4, attn.shape[1] // 4, d)
     return pl.pallas_call(
         lambda *refs: leave_kernel(shards, d // heads, rows // t, *refs),
@@ -987,47 +1110,76 @@
         in_specs=[
             big, big, big, big,
             pl.BlockSpec((t // BLOCK, pairs, FRAMES, 2 * BLOCK), lambda i: (i, 0, 0, 0)),
-            big, weight_specs((attn,))[3], whole(fullb.shape), whole(fullc.shape),
-        ],
+            big, weight_specs((attn,))[3],
+        ] + [whole(x.shape) for x in (fullb, fullc, w1g, w2g)],
         out_specs=[big, big, big, whole(wog), whole((8, d)), whole(w1_out), whole(w2_out)],
         out_shape=[shaped((rows, d), BF)] * 3
         + [shaped(wog, BF), shaped((8, d), F32), shaped(w1_out, F32), shaped(w2_out, F32)],
         scratch_shapes=[pltpu.VMEM((d, d), F32), pltpu.VMEM((t, d), BF)]
-        + BlockSum.kinds(fullb.shape, BF) + BlockSum.kinds(half, BF) + BlockSum.kinds(half, BF),
+        + BlockSum.kinds(fullb.shape, BF) + OwnerSum.kinds(fullc.shape, BF, shards // 4),
         compiler_params=pltpu.CompilerParams(
             dimension_semantics=("arbitrary",), collective_id=1, has_side_effects=True, vmem_limit_bytes=VMEM_LIMIT
         ),
         name="leave",
-    )(mg, q, k, v, p, mixed, attn, fullb, fullc)
+    )(mg, q, k, v, p, mixed, attn, fullb, fullc, w1g, w2g)
 
 
 def last_kernel(shards, steps, *refs):
-    tok_ref, mg_ref, dq_hbm, dk_hbm, dv_hbm, one_hbm, wq, wk, wv, vec_ref, wog_ref, vgin_ref, hbt_ref, top_ref = refs[:14]
-    gt_ref, attn_out, small_out, top_out = refs[14:18]
-    d_ref, one_ref, full, tile, vg, local = refs[18:24]
-    jobs, little, most = refs[24:35], refs[35:46], refs[46:]
+    tok_ref, mg_ref, dq_hbm, dk_hbm, dv_hbm, one_hbm, wq, wk, wv, vec_ref, wog_ref, vgin_ref, hbt_ref, top_ref, mid_ref, act_ref, w2_hbm = refs[:17]
+    gt_ref, lo_ref, attn_out, small_out, top_out = refs[17:22]
+    d_ref, one_ref, full, tile, vg, w2_ref, local = refs[22:29]
+    jobs, little, most, straight = refs[29:40], refs[40:51], refs[51:55], refs[55:]
+    turns = (steps - 3) // 2
     step, p = pl.program_id(0), Place(shards)
     rows = wog_ref.shape[2]
+    d = vg.shape[1]
     wide = attn_out.shape[1] // 2
     o = BlockSum(p, wog_ref, jobs, 3)
     s = BlockSum(p, tile, little)
     t = Largest(p, top_ref, top_out, *most)
+    late = Direct(p, straight)
     weight = lambda i: BlockSum(p, full.at[i], jobs, i)
+    q, k, v = weight(0), weight(1), weight(2)
+    many = functools.partial
+    events = [
+        (1, o.second), (1, s.second), (2, q.second), (3, many(t.take, 0)), (3, many(t.push, 1)), (3, s.third), (4, o.third),
+        (5, k.second), (5, many(t.take, 1)), (5, many(t.push, 2)), (5, s.fourth), (7, v.second), (7, q.third),
+        (8, o.fourth), (9, many(t.take, 2)), (9, many(t.push, 3)), (9, s.fifth), (9, k.third), (11, q.fourth),
+        (11, v.third), (13, o.fifth), (13, k.fourth), (13, many(t.take, 3)), (15, v.fourth), (15, q.fifth), (18, k.fifth),
+        (20, v.fifth),
+    ]
+    plan = {}
+    for at, event in events:
+        at = min(at, 2 * steps - 1)
+        plan.setdefault((at // 2, at % 2), []).append(event)
+    tick = ticker(plan, step)
     fetches = [
         pltpu.make_async_copy(src, dst, local.at[i])
         for i, (src, dst) in enumerate(
-            ((dq_hbm, d_ref.at[0]), (dk_hbm, d_ref.at[1]), (dv_hbm, d_ref.at[2]), (one_hbm, one_ref))
+            ((dq_hbm, d_ref.at[0]), (dk_hbm, d_ref.at[1]), (dv_hbm, d_ref.at[2]), (one_hbm, one_ref), (w2_hbm, w2_ref))
         )
     ]
 
+    def spread(value, put):
+        for i in range(shards):
+            put(i, (pltpu.roll(value, d - i * rows, 1) if i else value)[:, :128])
+
     @pl.when(step == 0)
     def _():
-        for i in (3, 0, 1, 2):
+        for i in (3, 0, 1, 2, 4):
             fetches[i].start()
-        vg[...] = vgin_ref[...]
-        p.greet()
-        o.first(), t.push(0)
+        vg[...] = jnp.zeros_like(vg)
+
+        def put(i, piece):
+            tile[i // 4, i % 4, :, :128] = piece
+
+        spread(vgin_ref[...], put)
+        tile[:, :, :, 128:] = hbt_ref[...]
+        late.greet()
+        o.first(), s.first(), t.push(0)
         fetches[3].wait()
+
+    tick(0)
 
     for i in range(3):
         pl.when(step == i)(fetches[i].wait)
@@ -1037,7 +1189,14 @@
         full[step] = tn(one_ref[...], d_ref[step]).astype(BF).reshape(full.shape[1:])
         weight(step).first()
 
-    @pl.when(step >= 3)
+    pl.when(step == 3 + turns)(fetches[4].wait)
+
+    @pl.when(step >= 3 + turns)
+    def _():
+        w2 = square(w2_ref)
+        lo_ref[...] = (mid_ref[...] + (nn(act_ref[...], w2) + vec_ref[7:8])).astype(BF)
+
+    @pl.when((step >= 3) & (step < 3 + turns))
     def _():
         tall = tok_ref.shape[0]
         at = pl.ds(pl.multiple_of((step - 3) * tall, tall), tall)
@@ -1047,68 +1206,55 @@
         vg[1:2] += column_sum(grad)
         gt_ref[...] = (mg_ref[...] + norm_back(grad, unit, inverse, vec_ref[0:1])).astype(BF)
 
-    def end():
-        d = vg.shape[1]
-        value = vg[...]
-        for i in range(shards):
-            piece = pltpu.roll(value, d - i * rows, 1) if i else value
-            tile[i // 4, i % 4, :, :128] = piece[:, :128]
-        tile[:, :, :, 128:] = hbt_ref[...]
-        s.first()
-        weight(2).fourth()
-        s.second()
-        o.fifth(), weight(0).fifth()
-        s.third()
-        weight(1).fifth()
-        s.fourth()
-        weight(2).fifth()
-        s.fifth()
-        for i, job in ((3, o), (0, weight(0)), (1, weight(1)), (2, weight(2))):
+    @pl.when(step == 2 + turns)
+    def _():
+        def put(i, piece):
+            late.tiles[i] = piece
+
+        spread(vg[...], put)
+        late.push()
+
+    tick(1)
+
+    @pl.when(step == steps - 1)
+    def _():
+        s.finish(writer(small_out, slice(None), 0, small_out.shape[1] // 2))
+        small_out[0:2, :128] = late.sum()[0:2]
+        for i, job in ((3, o), (0, q), (1, k), (2, v)):
             job.finish(writer(attn_out, slice(i * rows, (i + 1) * rows), 0, wide))
-        s.finish(writer(small_out, slice(None), 0, small_out.shape[1] // 2))
-
-    q, k, v = weight(0), weight(1), weight(2)
-    events = [
-        (0, o.second), (1, q.second), (1, lambda: t.take(0)), (1, lambda: t.push(1)), (2, k.second), (2, o.third),
-        (3, v.second), (3, q.third), (3, lambda: t.take(1)), (3, lambda: t.push(2)), (4, o.fourth), (4, k.third),
-        (4, lambda: t.take(2)), (4, lambda: t.push(3)), (5, v.third), (5, q.fourth), (6, k.fourth), (6, lambda: t.take(3)),
-    ]
-    plan = {}
-    for at, event in events:
-        plan.setdefault((min(at, steps - 1), 0), []).append(event)
-    plan.setdefault((steps - 1, 0), []).append(end)
-    ticker(plan, step)(0)
-
-
-def last(shards, tokens, mg, dq, dk, dv, one, attn, vec, wog, vgin, hbt, top):
+
+
+def last(shards, tokens, mg, dq, dk, dv, one, attn, vec, wog, vgin, hbt, top, mid, act, w2):
     rows, d = tokens.shape
     t = min(ROWS, rows)
     depth = shards // 4
-    steps = 3 + rows // t
-    later = pl.BlockSpec((t, d), lambda i: (jnp.maximum(i - 3, 0), 0))
+    turns = rows // t
+    steps = 3 + 2 * turns
+    later = pl.BlockSpec((t, d), lambda i: (jnp.clip(i - 3, 0, turns - 1), 0))
+    latest = lambda width: pl.BlockSpec((t, width), lambda i: (jnp.maximum(i - 3 - turns, 0), 0))
     anywhere = pl.BlockSpec(memory_space=pl.ANY)
     small = (depth, 4, 8, 256)
     return pl.pallas_call(
         lambda *refs: last_kernel(shards, steps, *refs),
         grid=(steps,),
         in_specs=[later, later] + [anywhere] * 4 + weight_specs((attn,))[:3]
-        + [whole(x.shape) for x in (vec, wog, vgin, hbt, top)],
-        out_specs=[later, whole((4 * wog.shape[2], d)), whole((8, 256)), whole((8, 128))],
+        + [whole(x.shape) for x in (vec, wog, vgin, hbt, top)] + [latest(d), latest(act.shape[1]), anywhere],
+        out_specs=[later, latest(d), whole((4 * wog.shape[2], d)), whole((8, 256)), whole((8, 128))],
         out_shape=[
-            shaped((rows, d), BF), shaped((4 * wog.shape[2], d), F32), shaped((8, 256), F32), shaped((8, 128), F32),
+            shaped((rows, d), BF), shaped((rows, d), BF), shaped((4 * wog.shape[2], d), F32), shaped((8, 256), F32), shaped((8, 128), F32),
         ],
         scratch_shapes=[
             pltpu.VMEM((3, rows, d), BF), pltpu.VMEM((rows, d), BF), pltpu.VMEM((3,) + wog.shape, BF),
-            pltpu.VMEM(small, F32), pltpu.VMEM((8, d), F32), pltpu.SemaphoreType.DMA((4,)),
+            pltpu.VMEM(small, F32), pltpu.VMEM((8, d), F32), pltpu.VMEM(w2.shape, BF), pltpu.SemaphoreType.DMA((5,)),
         ] + BlockSum.kinds(wog.shape, BF, 4) + BlockSum.kinds(small, F32) + [
             pltpu.VMEM((depth + 2, 8, 128), F32), pltpu.VMEM((4, 8, 128), F32),
             pltpu.SemaphoreType.DMA((depth + 2,)), pltpu.SemaphoreType.DMA((depth + 2,)),
-        ],
+        ] + Direct.kinds(shards),
         compiler_params=pltpu.CompilerParams(
             dimension_semantics=("arbitrary",), collective_id=2, has_side_effects=True, vmem_limit_bytes=VMEM_LIMIT
         ),
         name="last",
-    )(tokens, mg, dq, dk, dv, one, attn, attn, attn, vec, wog, vgin, hbt, top)
+    )(tokens, mg, dq, dk, dv, one, attn, attn, attn, vec, wog, vgin, hbt, top, mid, act, w2)
 
 
 def on_device(shards, reps, *args):
@@ -1154,16 +1300,16 @@
         q, k, v, p, mixed, mid, top = attend(tokens, weights, vec, heads)
     local = jnp.max(top.reshape(top.shape[0], FRAMES, 2, BLOCK), axis=(1, 3)).reshape(heads)
     if own:
-        layer_output, mg, b3g, w2g, w1g, vg2, hbg = middle(shards, mid, grad_out, hidden_proj, w1, w2, vec, hb)
-        dq, dk, dv, wog, vg1, w1l, w2g = leave(
-            shards, mg, q, k, v, p, mixed, attn, b3g, w2g.reshape(shards // 4, 4, -1, d), heads
+        act, mg, b3g, c3g, w2g, w1g, vg2, hbg = middle(shards, mid, grad_out, hidden_proj, w1, w2, vec, hb)
+        dq, dk, dv, wog, vg1, w1g, w2g = leave(
+            shards, mg, q, k, v, p, mixed, attn, b3g, c3g, w1g, w2g, heads
         )
         hbt = jnp.pad(hbg.reshape(shards // 4, 4, 8, more), ((0, 0), (0, 0), (0, 0), (0, 128 - more)))
-        grad_tokens, attn, tile, top = last(
+        grad_tokens, layer_output, attn, tile, top = last(
             shards, tokens, mg, dq, dk, dv, one, attn, vec, wog, jnp.concatenate([vg1[:5], vg2[:3]]), hbt,
             jnp.broadcast_to(jnp.pad(local, (0, 128 - heads))[None], (8, 128)),
+            mid, act, w2,
         )
-        w1g = jnp.concatenate([w1g, w1l], axis=1)
     else:
         layer_output, mg, w1g, w2g, vg2, hbg = mlp(mid, grad_out, w1, w2, vec, hb)
         grad_tokens, wg, vg1 = back(tokens, mg, q, k, v, p, mixed, weights, vec, heads)

time: 297 us -> 289 us (0.973)
  Pallas kernels: 273 us -> 265 us
    pallas_call x1, Pallas kernels: 45.6 us -> 56.2 us  [last(): pl.pallas_call(lambda *refs: last_kernel(shards, steps, *refs), grid=(ste...]
    pallas_call x1, Pallas kernels: 96.6 us -> 87.2 us  [middle(): pl.pallas_call(lambda *refs: middle_kernel(shards, tall, *refs), grid=(de...]
    pallas_call x1, Pallas kernels: 51.1 us -> 42.4 us  [leave(): pl.pallas_call(lambda *refs: leave_kernel(shards, d // heads, rows // t,...]
    unnamed x23 -> x22, local copies, waits for them, and re-layouts: 5.54 us -> 7.23 us
where the time goes in v5:
time: 289 us
  Pallas kernels  265 us (92%)
  local copies, waits for them, and re-layouts  15.2 us (5%)
  other arithmetic  7.47 us (3%)
    pallas_call x1, Pallas kernels, middle(): pl.pallas_call(lambda *refs: middle_kernel(shards, tall, *refs), grid=(de...  87.2 us
    pallas_call x1, Pallas kernels, enter(): pl.pallas_call(lambda *refs: enter_kernel(shards, d // heads, rows // t,...  79.3 us
    pallas_call x1, Pallas kernels, last(): pl.pallas_call(lambda *refs: last_kernel(shards, steps, *refs), grid=(ste...  56.2 us
    pallas_call x1, Pallas kernels, leave(): pl.pallas_call(lambda *refs: leave_kernel(shards, d // heads, rows // t,...  42.4 us
    unnamed x22, local copies, waits for them, and re-layouts  7.23 us

profile of v5, /device:TPU:0, one launch (start us, length us, event | category | flops | bytes accessed | tf_op | source)
XLA Modules:
  0.0 288.6 jit_solution(9991165167306638307)
XLA Ops:
  0.7 0.8 stack.35
  1.5 0.7 reshape.74
  2.2 0.6 fusion.3.refs_7_
  2.8 79.3 %enter.1 = (bf16[4,4,192,768]{3,2,1,0:T(8,128)(2,1)}, bf16[4,4,48,768]{3,2,1,0:T(8,128)(2,1)}, bf16[4,4,192,768]{3,2,1,0:T(8,128)(2,1)}, f32[4,4,8,256]{3,2,1,0:...) custom-call(bf16[2048,768]{1,0:T(8,128)(2,1)} %refs_0_.3, ...), custom_call_target="tpu_custom_call" | custom-call | tf_op jit(solution)/shard_map/enter/pallas_call | solution.py:1023
  82.1 0.9 reduce_max.10
  83.2 0.6 broadcast_in_dim.4.refs_13_
  83.8 0.8 slice.68
  84.7 0.7 reshape.77.refs_6_
  85.4 87.2 %middle.1 = (bf16[2048,3072]{1,0:T(8,128)(2,1)}, f32[2048,768]{1,0:T(8,128)}, bf16[4,4,48,768]{3,2,1,0:T(8,128)(2,1)}, bf16[1,4,192,768]{3,2,1,0:T(8,128)(2,1)},...) custom-call(f32[2048,768]{1,0:T(8,128)} %get-tuple-element.55.refs_0_.refs_14_, ...), custom_call_target="tpu_custom_call" | custom-call | tf_op jit(solution)/shard_map/middle/pallas_call | solution.py:912
  172.6 42.4 %leave.1 = (bf16[2048,768]{1,0:T(8,128)(2,1)}, bf16[2048,768]{1,0:T(8,128)(2,1)}, bf16[2048,768]{1,0:T(8,128)(2,1)}, bf16[4,4,48,768]{3,2,1,0:T(8,128)(2,1)}, f3...) custom-call(f32[2048,768]{1,0:T(8,128)} %get-tuple-element.60.refs_0_.refs_1_, ...), custom_call_target="tpu_custom_call" | custom-call | tf_op jit(solution)/shard_map/leave/pallas_call | solution.py:1107
  215.5 0.7 reduce.5
  216.2 1.4 pad_maximum_fusion.refs_11_
  217.7 0.6 pad.20.refs_12_
  218.3 56.2 %last.1 = (bf16[2048,768]{1,0:T(8,128)(2,1)}, bf16[2048,768]{1,0:T(8,128)(2,1)}, f32[192,768]{1,0:T(8,128)}, f32[8,256]{1,0:T(8,128)}, f32[8,128]{1,0:T(8,128)}) custom-call(bf16[2048,768]{1,0:T(8,128)(2,1)} %refs_0_.3, f32[2048,768]{1,0:T(8,128)} %get-tuple-element.60.refs_0_.refs_1_, bf16[2048,768]{1,0:T(8,128)(2,1)} %get-tuple-element.71.refs_2_, ...), custom_call_target="tpu_custom_call" | custom-call | tf_op jit(solution)/shard_map/last/pallas_call | solution.py:1237
  274.5 1.2 fusion.4
  275.7 0.7 slice.65
  276.4 1.5 slice_bitcast_fusion.1
  277.9 0.6 reshape.81
  278.7 0.6 dynamic-slice_multiply_fusion
  279.3 2.1 convert_multiply_fusion
  281.3 3.9 %copy.44 = bf16[2048,768]{1,0:T(8,128)(2,1)} copy(bf16[2048,768]{1,0:T(8,128)(2,1)} %get-tuple-element.131) | data formatting | bytes 6291456
  285.3 1.7 copy.45
  286.9 0.8 copy.46
  287.7 0.8 copy.47
  (27 shorter events, 1.0 us)
Async XLA Ops:
  172.6 43.0 %copy-start.5 = (f32[1,3072]{1,0:T(1,128)S(1)}, f32[1,3072]{1,0:T(1,128)}, u32[]{:S(2)}) copy-start(f32[1,3072]{1,0:T(1,128)} %get-tuple-element.78) | copy-start | bytes 36868
  172.6 43.7 %copy-start.6 = (f32[8,768]{1,0:T(8,128)S(1)}, f32[8,768]{1,0:T(8,128)}, u32[]{:S(2)}) copy-start(f32[8,768]{1,0:T(8,128)} %get-tuple-element.77) | copy-start | bytes 73732
  218.3 56.2 %copy-start.8 = (f32[12]{0:T(128)S(1)}, f32[12]{0:T(128)}, u32[]{:S(2)}) copy-start(f32[12]{0:T(128)} %param.35) | copy-start | bytes 148
  218.3 60.4 %copy-start.7 = (bf16[48]{0:T(256)(128)(2,1)S(1)}, bf16[48]{0:T(256)(128)(2,1)}, u32[]{:S(2)}) copy-start(bf16[48]{0:T(256)(128)(2,1)} %param.23) | copy-start | bytes 292
  218.3 60.9 %copy-start.3 = (bf16[48,768]{1,0:T(8,128)(2,1)S(1)}, bf16[48,768]{1,0:T(8,128)(2,1)}, u32[]{:S(2)}) copy-start(bf16[48,768]{1,0:T(8,128)(2,1)} %refs_1_.2) | copy-start | bytes 221188
  218.3 60.9 %copy-start.4 = (bf16[48,768]{1,0:T(8,128)(2,1)S(1)}, bf16[48,768]{1,0:T(8,128)(2,1)}, u32[]{:S(2)}) copy-start(bf16[48,768]{1,0:T(8,128)(2,1)} %refs_2_.2) | copy-start | bytes 221188
  281.3 3.9 %copy-start = (bf16[2048,768]{1,0:T(8,128)(2,1)S(1)}, bf16[2048,768]{1,0:T(8,128)(2,1)}, u32[]{:S(2)}) copy-start(bf16[2048,768]{1,0:T(8,128)(2,1)} %get-tuple-element.132) | copy-start | bytes 9437188
  285.3 1.7 copy-start.2
  285.3 2.5 copy-start.1

commit v6 on v5

--- a/solution.py
+++ b/solution.py
@@ -122,7 +122,7 @@
             mix_ref[rows, cols] = mixed.astype(BF)
         return carry
 
-    lax.fori_loop(0, tok_ref.shape[0] // BLOCK, body, 0)
+    lax.fori_loop(0, tok_ref.shape[0] // BLOCK, body, 0, unroll=2)
     tick(2)
     mid_ref[...] = tok_ref[...].astype(F32) + (nn(mix_ref[...], square(w_refs[3])) + vec_ref[4:5])
     tick(3)
@@ -205,7 +205,7 @@
             dq_ref[rows, cols] = (tn(stack(wide), split(two_k, first, second)) * scale).astype(BF)
         return carry
 
-    lax.fori_loop(0, q_ref.shape[0] // BLOCK, body, 0)
+    lax.fori_loop(0, q_ref.shape[0] // BLOCK, body, 0, unroll=4)
 
 
 def back_kernel(
@@ -879,9 +879,9 @@
             again(t).wait()
             unit, inverse = normalise(stage[t % 2])
             two, up = two_ref[rows, :], dy_ref[rows, :].astype(F32)
-            vg_ref[0:1] += column_sum(two * unit)
-            vg_ref[1:2] += column_sum(two)
-            vg_ref[2:3] += column_sum(up)
+            vg_ref[5:6] += column_sum(two * unit)
+            vg_ref[6:7] += column_sum(two)
+            vg_ref[7:8] += column_sum(up)
             two_ref[rows, :] = up + norm_back(two, unit, inverse, gain)
             results(t).start()
         each(depth - 2, "fifth")
@@ -940,10 +940,11 @@
 
 def enter_kernel(shards, width, steps, *refs):
     tok_ref, wq, wk, wv, wo, w1, w2, small = refs[:8]
-    attn_out, w1_out, w2_out, small_out, vec_out = refs[8:13]
-    results = refs[13:21]
-    attn, tiles_in, local = refs[21:24]
-    sems = refs[24:26]
+    attn_out, w1_out, w2_out, hb_out, vec_out = refs[8:13]
+    results, top_out, one_out = refs[13:19], refs[19], refs[20]
+    attn, tiles_in, tops, local = refs[21:25]
+    sems = refs[25:27]
+    hidden_rows = hb_out.shape[1] // shards
     step = pl.program_id(0)
     p = Place(shards)
     depth = p.depth
@@ -987,7 +988,13 @@
             piece = jnp.concatenate([tiles_in[i // 4, i % 4, :, :128], blank], axis=1)
             vec = vec + (pltpu.roll(piece, i * rows, 1) if i else piece)
         vec_out[...] = vec
-        small_out[...] = tiles_in[...]
+        empty = jnp.zeros((8, 2 * hidden_rows - 256), F32)
+        for i in range(0, shards, 2):
+            even, odd = (
+                jnp.concatenate([tiles_in[n // 4, n % 4, :, 256:], empty], axis=1) for n in (i, i + 1)
+            )
+            both = even + pltpu.roll(odd, hidden_rows, 1)
+            hb_out[:, i * hidden_rows : (i + 2) * hidden_rows] = both[0:1]
 
     def keep():
         return pltpu.make_async_copy(attn, attn_out, local.at[2])
@@ -997,6 +1004,14 @@
         keep().start()
 
     def end():
+        lane = lax.broadcasted_iota(jnp.int32, (8, 128), 1)
+        tile = jnp.zeros((8, 128), F32)
+        for pair in range(tops.shape[0]):
+            best = jnp.max(tops[pair], axis=0, keepdims=True)
+            for i in range(2):
+                one = jnp.max(best[:, i * BLOCK : (i + 1) * BLOCK], axis=1, keepdims=True)
+                tile = jnp.where(lane == 2 * pair + i, one, tile)
+        top_out[...] = tile
         b.joined(), c.joined()
         for g in early + [b, c]:
             g.drained()
@@ -1005,7 +1020,7 @@
     pl.when(step == 0)(start)
     plan = {(0, 1): [whole_attn, c.column], (0, 2): [b.rest], (steps // 2 - 1, 3): [c.plane], (steps - 1, 2): [c.rest], (steps - 1, 3): [end]}
     view = [attn.at[:, :, i * rows : (i + 1) * rows, :] for i in range(4)]
-    attend_kernel(width, tok_ref, view, vec_out, *results, tick=ticker(plan, step))
+    attend_kernel(width, tok_ref, view, vec_out, *results, tops, one_out, tick=ticker(plan, step))
 
 
 def enter(shards, tokens, wq, wk, wv, wo, w1, w2, small, heads):
@@ -1025,20 +1040,21 @@
         grid=(rows // t,),
         in_specs=[big] + [whole(w.shape) for w in (wq, wk, wv, wo)] + [whole((w1.shape[0], chunk))] + [whole(w.shape) for w in (w2, small)],
         out_specs=[
-            anywhere, anywhere, anywhere, whole(full_small), whole((8, d)), big, big, big,
+            anywhere, anywhere, anywhere, whole((1, w1.shape[1])), whole((8, d)), big, big, big,
             pl.BlockSpec((t // BLOCK, pairs, FRAMES, 2 * BLOCK), lambda i: (i, 0, 0, 0)),
             big, big,
-            whole((pairs, FRAMES, 2 * BLOCK)), big,
+            whole((8, 128)), big,
         ],
         out_shape=[
             shaped(packed, BF), shaped(lead + (w1.shape[0], chunk), BF), shaped(lead + w2.shape, BF),
-            shaped(full_small, F32), shaped((8, d), F32),
+            shaped((1, w1.shape[1]), F32), shaped((8, d), F32),
         ]
         + [shaped((rows, d), BF)] * 3
         + [shaped((blocks, pairs, FRAMES, 2 * BLOCK), F32), shaped((rows, d), BF), shaped((rows, d), F32)]
-        + [shaped((pairs, FRAMES, 2 * BLOCK), F32), shaped((rows, d), BF)],
+        + [shaped((8, 128), F32), shaped((rows, d), BF)],
         scratch_shapes=[
-            pltpu.VMEM(packed, BF), pltpu.VMEM(full_small, F32), pltpu.SemaphoreType.DMA((3,)),
+            pltpu.VMEM(packed, BF), pltpu.VMEM(full_small, F32), pltpu.VMEM((pairs, FRAMES, 2 * BLOCK), F32),
+            pltpu.SemaphoreType.DMA((3,)),
         ] + Gather.kinds(depth, 7),
         compiler_params=pltpu.CompilerParams(
             dimension_semantics=("arbitrary",), collective_id=0, has_side_effects=True, vmem_limit_bytes=VMEM_LIMIT
@@ -1125,10 +1141,11 @@
 
 
 def last_kernel(shards, steps, *refs):
-    tok_ref, mg_ref, dq_hbm, dk_hbm, dv_hbm, one_hbm, wq, wk, wv, vec_ref, wog_ref, vgin_ref, hbt_ref, top_ref, mid_ref, act_ref, w2_hbm = refs[:17]
-    gt_ref, lo_ref, attn_out, small_out, top_out = refs[17:22]
-    d_ref, one_ref, full, tile, vg, w2_ref, local = refs[22:29]
-    jobs, little, most, straight = refs[29:40], refs[40:51], refs[51:55], refs[55:]
+    tok_ref, mg_ref, dq_hbm, dk_hbm, dv_hbm, one_hbm, wq, wk, wv, vec_ref, wog_ref, vga_ref, vgb_ref, hbg_ref, top_ref, mid_ref, act_ref, w2_hbm = refs[:18]
+    gt_ref, lo_ref, attn_out, small_out, top_out = refs[18:23]
+    d_ref, one_ref, full, tile, vg, w2_ref, local = refs[23:30]
+    jobs, little, most, straight = refs[30:41], refs[41:52], refs[52:56], refs[56:]
+    hidden_rows = hbg_ref.shape[1] // shards
     turns = (steps - 3) // 2
     step, p = pl.program_id(0), Place(shards)
     rows = wog_ref.shape[2]
@@ -1173,8 +1190,14 @@
         def put(i, piece):
             tile[i // 4, i % 4, :, :128] = piece
 
-        spread(vgin_ref[...], put)
-        tile[:, :, :, 128:] = hbt_ref[...]
+        spread(vga_ref[...] + vgb_ref[...], put)
+        tile[:, :, :, 128:256] = jnp.zeros(tile.shape[:3] + (128,), F32)
+        for i in range(0, shards, 2):
+            both = jnp.broadcast_to(
+                hbg_ref[:, i * hidden_rows : (i + 2) * hidden_rows], (8, 2 * hidden_rows)
+            )
+            tile[i // 4, i % 4, :, 256:] = both[:, :256]
+            tile[i // 4, i % 4 + 1, :, 256:] = pltpu.roll(both, hidden_rows, 1)[:, :256]
         late.greet()
         o.first(), s.first(), t.push(0)
         fetches[3].wait()
@@ -1224,7 +1247,7 @@
             job.finish(writer(attn_out, slice(i * rows, (i + 1) * rows), 0, wide))
 
 
-def last(shards, tokens, mg, dq, dk, dv, one, attn, vec, wog, vgin, hbt, top, mid, act, w2):
+def last(shards, tokens, mg, dq, dk, dv, one, attn, vec, wog, vga, vgb, hbg, top, mid, act, w2):
     rows, d = tokens.shape
     t = min(ROWS, rows)
     depth = shards // 4
@@ -1233,15 +1256,15 @@
     later = pl.BlockSpec((t, d), lambda i: (jnp.clip(i - 3, 0, turns - 1), 0))
     latest = lambda width: pl.BlockSpec((t, width), lambda i: (jnp.maximum(i - 3 - turns, 0), 0))
     anywhere = pl.BlockSpec(memory_space=pl.ANY)
-    small = (depth, 4, 8, 256)
+    small = (depth, 4, 8, 512)
     return pl.pallas_call(
         lambda *refs: last_kernel(shards, steps, *refs),
         grid=(steps,),
         in_specs=[later, later] + [anywhere] * 4 + weight_specs((attn,))[:3]
-        + [whole(x.shape) for x in (vec, wog, vgin, hbt, top)] + [latest(d), latest(act.shape[1]), anywhere],
-        out_specs=[later, latest(d), whole((4 * wog.shape[2], d)), whole((8, 256)), whole((8, 128))],
+        + [whole(x.shape) for x in (vec, wog, vga, vgb, hbg, top)] + [latest(d), latest(act.shape[1]), anywhere],
+        out_specs=[later, latest(d), whole((4 * wog.shape[2], d)), whole((8, 512)), whole((8, 128))],
         out_shape=[
-            shaped((rows, d), BF), shaped((rows, d), BF), shaped((4 * wog.shape[2], d), F32), shaped((8, 256), F32), shaped((8, 128), F32),
+            shaped((rows, d), BF), shaped((rows, d), BF), shaped((4 * wog.shape[2], d), F32), shaped((8, 512), F32), shaped((8, 128), F32),
         ],
         scratch_shapes=[
             pltpu.VMEM((3, rows, d), BF), pltpu.VMEM((rows, d), BF), pltpu.VMEM((3,) + wog.shape, BF),
@@ -1254,7 +1277,7 @@
             dimension_semantics=("arbitrary",), collective_id=2, has_side_effects=True, vmem_limit_bytes=VMEM_LIMIT
         ),
         name="last",
-    )(tokens, mg, dq, dk, dv, one, attn, attn, attn, vec, wog, vgin, hbt, top, mid, act, w2)
+    )(tokens, mg, dq, dk, dv, one, attn, attn, attn, vec, wog, vga, vgb, hbg, top, mid, act, w2)
 
 
 def on_device(shards, reps, *args):
@@ -1267,9 +1290,9 @@
     hidden = hidden_proj.shape[1]
     head_dim = d // heads
     small = (first_gain, first_shift, query_bias, value_bias, output_bias, second_gain, second_shift, final_bias)
-    rows, more = small[0].shape[0], hidden_bias.shape[0] // 8
+    rows, more = small[0].shape[0], hidden_bias.shape[0]
     whole_chunks = shards % 4 == 0 and hidden * 4 % (shards * 256) == 0 and hidden * 4 // shards == 4 * final_proj.shape[0]
-    own = whole_chunks and reps == 2 and shards % 4 == 0 and shards > 4 and rows % 16 == 0 and rows <= 128 and more <= 128
+    own = whole_chunks and reps == 2 and shards % 4 == 0 and shards > 4 and rows % 16 == 0 and rows <= 128 and more <= 256 and more % 64 == 0 and more > 128
 
     def gather(x):
         return lax.all_gather(x, "shard", axis=0, tiled=True)
@@ -1281,16 +1304,14 @@
     if own:
         tile = jnp.concatenate(
             [
-                jnp.pad(jnp.stack(small).astype(F32), ((0, 0), (0, 128 - rows))),
-                jnp.pad(hidden_bias.astype(F32).reshape(8, more), ((0, 0), (0, 128 - more))),
+                jnp.pad(jnp.stack(small).astype(F32), ((0, 0), (0, 256 - rows))),
+                jnp.pad(hidden_bias.astype(F32)[None], ((0, 7), (0, 256 - more))),
             ],
             axis=1,
         )
-        attn, w1, w2, tile, vec, q, k, v, p, mixed, mid, top, one = enter(
+        attn, w1, w2, hb, vec, q, k, v, p, mixed, mid, top, one = enter(
             shards, tokens, query_proj, key_proj, value_proj, output_proj, hidden_proj, final_proj, tile, heads
         )
-        tile = tile.reshape(shards, 8, -1)
-        hb = tile[:, :, 128 : 128 + more].reshape(1, hidden)
         attn, w2 = attn.reshape(shards, -1, d), w2.reshape(shards, -1, d)
     else:
         weights = tuple(gather(x) for x in (query_proj, key_proj, value_proj, output_proj))
@@ -1298,17 +1319,13 @@
         vec = jnp.stack([gather(x) for x in small]).astype(F32)
         hb = gather(hidden_bias).astype(F32)[None]
         q, k, v, p, mixed, mid, top = attend(tokens, weights, vec, heads)
-    local = jnp.max(top.reshape(top.shape[0], FRAMES, 2, BLOCK), axis=(1, 3)).reshape(heads)
     if own:
         act, mg, b3g, c3g, w2g, w1g, vg2, hbg = middle(shards, mid, grad_out, hidden_proj, w1, w2, vec, hb)
         dq, dk, dv, wog, vg1, w1g, w2g = leave(
             shards, mg, q, k, v, p, mixed, attn, b3g, c3g, w1g, w2g, heads
         )
-        hbt = jnp.pad(hbg.reshape(shards // 4, 4, 8, more), ((0, 0), (0, 0), (0, 0), (0, 128 - more)))
         grad_tokens, layer_output, attn, tile, top = last(
-            shards, tokens, mg, dq, dk, dv, one, attn, vec, wog, jnp.concatenate([vg1[:5], vg2[:3]]), hbt,
-            jnp.broadcast_to(jnp.pad(local, (0, 128 - heads))[None], (8, 128)),
-            mid, act, w2,
+            shards, tokens, mg, dq, dk, dv, one, attn, vec, wog, vg1, vg2, hbg, top, mid, act, w2
         )
     else:
         layer_output, mg, w1g, w2g, vg2, hbg = mlp(mid, grad_out, w1, w2, vec, hb)
@@ -1316,10 +1333,11 @@
     if own:
         wg = tuple(attn[i * rows : (i + 1) * rows] for i in range(4))
         vg = tuple(tile[i, :rows] for i in range(8))
-        hbg = tile[:, 128 : 128 + more].reshape(-1)
+        hbg = tile[0, 256 : 256 + more]
         global_max = top[0, :heads]
     else:
         vg = jnp.concatenate([vg1[:5], vg2[:3]])
+        local = jnp.max(top.reshape(top.shape[0], FRAMES, 2, BLOCK), axis=(1, 3)).reshape(heads)
         global_max = lax.pmax(local, ("shard", "rep"))
         wg = tuple(scatter(x) for x in wg)
         w1g, w2g = scatter(w1g), scatter(w2g)

time: 289 us -> 278 us (0.962)
  Pallas kernels: 265 us -> 261 us
  local copies, waits for them, and re-layouts: 15.2 us -> 11.6 us
  other arithmetic: 7.47 us -> 4.45 us
    pallas_call x1, Pallas kernels: 42.4 us -> 39.5 us  [leave(): pl.pallas_call(lambda *refs: leave_kernel(shards, d // heads, rows // t,...]
    unnamed x22 -> x18, local copies, waits for them, and re-layouts: 7.23 us -> 7.23 us
where the time goes in v6:
time: 278 us
  Pallas kernels  261 us (94%)
  local copies, waits for them, and re-layouts  11.6 us (4%)
  other arithmetic  4.45 us (2%)
    pallas_call x1, Pallas kernels, middle(): pl.pallas_call(lambda *refs: middle_kernel(shards, tall, *refs), grid=(de...  87.1 us
    pallas_call x1, Pallas kernels, enter(): pl.pallas_call(lambda *refs: enter_kernel(shards, d // heads, rows // t,...  77.5 us
    pallas_call x1, Pallas kernels, last(): pl.pallas_call(lambda *refs: last_kernel(shards, steps, *refs), grid=(ste...  56.9 us
    pallas_call x1, Pallas kernels, leave(): pl.pallas_call(lambda *refs: leave_kernel(shards, d // heads, rows // t,...  39.5 us
    unnamed x18, local copies, waits for them, and re-layouts  7.23 us

profile of v6, /device:TPU:0, one launch (start us, length us, event | category | flops | bytes accessed | tf_op | source)
XLA Modules:
  0.0 277.9 jit_solution(9340755868414256948)
XLA Ops:
  0.7 0.8 stack.35
  1.5 0.7 broadcast_in_dim.7
  2.1 0.6 fusion.3.refs_7_
  2.7 77.5 %enter.1 = (bf16[4,4,192,768]{3,2,1,0:T(8,128)(2,1)}, bf16[4,4,48,768]{3,2,1,0:T(8,128)(2,1)}, bf16[4,4,192,768]{3,2,1,0:T(8,128)(2,1)}, f32[1,3072]{1,0:T(1,128...) custom-call(bf16[2048,768]{1,0:T(8,128)(2,1)} %refs_0_.3, ...), custom_call_target="tpu_custom_call" | custom-call | tf_op jit(solution)/shard_map/enter/pallas_call | solution.py:1038
  80.2 87.1 %middle.1 = (bf16[2048,3072]{1,0:T(8,128)(2,1)}, f32[2048,768]{1,0:T(8,128)}, bf16[4,4,48,768]{3,2,1,0:T(8,128)(2,1)}, bf16[1,4,192,768]{3,2,1,0:T(8,128)(2,1)},...) custom-call(f32[2048,768]{1,0:T(8,128)} %get-tuple-element.55.refs_0_.refs_15_, ...), custom_call_target="tpu_custom_call" | custom-call | tf_op jit(solution)/shard_map/middle/pallas_call | solution.py:912
  167.4 39.5 %leave.1 = (bf16[2048,768]{1,0:T(8,128)(2,1)}, bf16[2048,768]{1,0:T(8,128)(2,1)}, bf16[2048,768]{1,0:T(8,128)(2,1)}, bf16[4,4,48,768]{3,2,1,0:T(8,128)(2,1)}, f3...) custom-call(f32[2048,768]{1,0:T(8,128)} %get-tuple-element.60.refs_0_.refs_1_, ...), custom_call_target="tpu_custom_call" | custom-call | tf_op jit(solution)/shard_map/leave/pallas_call | solution.py:1123
  206.9 0.0 copy-start.6
  206.9 0.0 copy-start.3
  206.9 0.0 copy-start.4
  206.9 0.0 copy-start.5
  206.9 56.9 %last.1 = (bf16[2048,768]{1,0:T(8,128)(2,1)}, bf16[2048,768]{1,0:T(8,128)(2,1)}, f32[192,768]{1,0:T(8,128)}, f32[8,512]{1,0:T(8,128)}, f32[8,128]{1,0:T(8,128)}) custom-call(bf16[2048,768]{1,0:T(8,128)(2,1)} %refs_0_.3, f32[2048,768]{1,0:T(8,128)} %get-tuple-element.60.refs_0_.refs_1_, bf16[2048,768]{1,0:T(8,128)(2,1)} %get-tuple-element.71.refs_2_, ...), custom_call_target="tpu_custom_call" | custom-call | tf_op jit(solution)/shard_map/last/pallas_call | solution.py:1260
  263.9 0.0 copy-done.6
  263.9 1.2 fusion.4
  265.1 0.1 broadcast_in_dim.8
  265.2 0.1 mul.22
  265.2 0.0 copy-done.4
  265.3 2.1 convert_multiply_fusion
  267.3 0.6 dynamic-slice_multiply_fusion
  267.9 1.5 slice_bitcast_fusion.1
  269.4 1.3 slice.53
  270.7 3.9 %copy.44 = bf16[2048,768]{1,0:T(8,128)(2,1)} copy(bf16[2048,768]{1,0:T(8,128)(2,1)} %get-tuple-element.131) | data formatting | bytes 6291456
  274.6 1.7 copy.45
  276.2 0.8 copy.46
  277.1 0.8 copy.47
  (8 shorter events, 0.0 us)
Async XLA Ops:
  206.9 57.0 %copy-start.6 = (f32[12]{0:T(128)S(1)}, f32[12]{0:T(128)}, u32[]{:S(2)}) copy-start(f32[12]{0:T(128)} %param.35) | copy-start | bytes 148
  206.9 58.3 %copy-start.3 = (bf16[48,768]{1,0:T(8,128)(2,1)S(1)}, bf16[48,768]{1,0:T(8,128)(2,1)}, u32[]{:S(2)}) copy-start(bf16[48,768]{1,0:T(8,128)(2,1)} %refs_1_.2) | copy-start | bytes 221188
  206.9 58.3 %copy-start.4 = (bf16[48,768]{1,0:T(8,128)(2,1)S(1)}, bf16[48,768]{1,0:T(8,128)(2,1)}, u32[]{:S(2)}) copy-start(bf16[48,768]{1,0:T(8,128)(2,1)} %refs_2_.2) | copy-start | bytes 221188
  206.9 60.4 %copy-start.5 = (bf16[48]{0:T(256)(128)(2,1)S(1)}, bf16[48]{0:T(256)(128)(2,1)}, u32[]{:S(2)}) copy-start(bf16[48]{0:T(256)(128)(2,1)} %param.23) | copy-start | bytes 292
  270.7 3.9 %copy-start = (bf16[2048,768]{1,0:T(8,128)(2,1)S(1)}, bf16[2048,768]{1,0:T(8,128)(2,1)}, u32[]{:S(2)}) copy-start(bf16[2048,768]{1,0:T(8,128)(2,1)} %get-tuple-element.132) | copy-start | bytes 9437188
  274.6 1.7 copy-start.2
  274.6 2.5 copy-start.1

commit v7 on v6

--- a/solution.py
+++ b/solution.py
@@ -982,6 +982,7 @@
         b.plane()
         for g in early[:-1]:
             g.joined()
+        c.column()
         vec = jnp.zeros(vec_out.shape, F32)
         blank = jnp.zeros((8, vec.shape[1] - 128), F32)
         for i in range(shards):
@@ -1018,7 +1019,7 @@
         keep().wait()
 
     pl.when(step == 0)(start)
-    plan = {(0, 1): [whole_attn, c.column], (0, 2): [b.rest], (steps // 2 - 1, 3): [c.plane], (steps - 1, 2): [c.rest], (steps - 1, 3): [end]}
+    plan = {(0, 1): [whole_attn], (0, 2): [b.rest], (min(1, steps - 1), 2): [c.plane], (steps - 1, 1): [c.rest], (steps - 1, 3): [end]}
     view = [attn.at[:, :, i * rows : (i + 1) * rows, :] for i in range(4)]
     attend_kernel(width, tok_ref, view, vec_out, *results, tops, one_out, tick=ticker(plan, step))
 

time: 278 us -> 275 us (0.989)
  Pallas kernels: 261 us -> 258 us
    pallas_call x1, Pallas kernels: 77.5 us -> 74.2 us  [enter(): pl.pallas_call(lambda *refs: enter_kernel(shards, d // heads, rows // t,...]
where the time goes in v7:
time: 275 us
  Pallas kernels  258 us (94%)
  local copies, waits for them, and re-layouts  11.6 us (4%)
  other arithmetic  4.45 us (2%)
    pallas_call x1, Pallas kernels, middle(): pl.pallas_call(lambda *refs: middle_kernel(shards, tall, *refs), grid=(de...  88.5 us
    pallas_call x1, Pallas kernels, enter(): pl.pallas_call(lambda *refs: enter_kernel(shards, d // heads, rows // t,...  74.2 us
    pallas_call x1, Pallas kernels, last(): pl.pallas_call(lambda *refs: last_kernel(shards, steps, *refs), grid=(ste...  57.2 us
    pallas_call x1, Pallas kernels, leave(): pl.pallas_call(lambda *refs: leave_kernel(shards, d // heads, rows // t,...  38.2 us
    unnamed x18, local copies, waits for them, and re-layouts  7.23 us

profile of v7, /device:TPU:0, one launch (start us, length us, event | category | flops | bytes accessed | tf_op | source)
XLA Modules:
  0.0 274.9 jit_solution(6651312345506346)
XLA Ops:
  0.7 0.8 stack.35
  1.5 0.7 broadcast_in_dim.7
  2.1 0.6 fusion.3.refs_7_
  2.7 74.2 %enter.1 = (bf16[4,4,192,768]{3,2,1,0:T(8,128)(2,1)}, bf16[4,4,48,768]{3,2,1,0:T(8,128)(2,1)}, bf16[4,4,192,768]{3,2,1,0:T(8,128)(2,1)}, f32[1,3072]{1,0:T(1,128...) custom-call(bf16[2048,768]{1,0:T(8,128)(2,1)} %refs_0_.3, ...), custom_call_target="tpu_custom_call" | custom-call | tf_op jit(solution)/shard_map/enter/pallas_call | solution.py:1039
  77.0 88.5 %middle.1 = (bf16[2048,3072]{1,0:T(8,128)(2,1)}, f32[2048,768]{1,0:T(8,128)}, bf16[4,4,48,768]{3,2,1,0:T(8,128)(2,1)}, bf16[1,4,192,768]{3,2,1,0:T(8,128)(2,1)},...) custom-call(f32[2048,768]{1,0:T(8,128)} %get-tuple-element.55.refs_0_.refs_15_, ...), custom_call_target="tpu_custom_call" | custom-call | tf_op jit(solution)/shard_map/middle/pallas_call | solution.py:912
  165.5 38.2 %leave.1 = (bf16[2048,768]{1,0:T(8,128)(2,1)}, bf16[2048,768]{1,0:T(8,128)(2,1)}, bf16[2048,768]{1,0:T(8,128)(2,1)}, bf16[4,4,48,768]{3,2,1,0:T(8,128)(2,1)}, f3...) custom-call(f32[2048,768]{1,0:T(8,128)} %get-tuple-element.60.refs_0_.refs_1_, ...), custom_call_target="tpu_custom_call" | custom-call | tf_op jit(solution)/shard_map/leave/pallas_call | solution.py:1124
  203.6 0.0 copy-start.6
  203.6 0.0 copy-start.3
  203.6 0.0 copy-start.4
  203.7 0.0 copy-start.5
  203.7 57.2 %last.1 = (bf16[2048,768]{1,0:T(8,128)(2,1)}, bf16[2048,768]{1,0:T(8,128)(2,1)}, f32[192,768]{1,0:T(8,128)}, f32[8,512]{1,0:T(8,128)}, f32[8,128]{1,0:T(8,128)}) custom-call(bf16[2048,768]{1,0:T(8,128)(2,1)} %refs_0_.3, f32[2048,768]{1,0:T(8,128)} %get-tuple-element.60.refs_0_.refs_1_, bf16[2048,768]{1,0:T(8,128)(2,1)} %get-tuple-element.71.refs_2_, ...), custom_call_target="tpu_custom_call" | custom-call | tf_op jit(solution)/shard_map/last/pallas_call | solution.py:1261
  260.9 1.2 fusion.4
  262.1 0.1 broadcast_in_dim.8
  262.2 0.1 mul.22
  262.3 0.0 copy-done.3
  262.3 2.1 convert_multiply_fusion
  264.3 0.6 dynamic-slice_multiply_fusion
  264.9 1.5 slice_bitcast_fusion.1
  266.4 1.3 slice.53
  267.7 3.9 %copy.44 = bf16[2048,768]{1,0:T(8,128)(2,1)} copy(bf16[2048,768]{1,0:T(8,128)(2,1)} %get-tuple-element.131) | data formatting | bytes 6291456
  271.6 1.7 copy.45
  273.3 0.8 copy.46
  274.1 0.0 copy-done.1
  274.1 0.8 copy.47
  (8 shorter events, 0.0 us)
Async XLA Ops:
  203.6 57.3 %copy-start.6 = (f32[12]{0:T(128)S(1)}, f32[12]{0:T(128)}, u32[]{:S(2)}) copy-start(f32[12]{0:T(128)} %param.35) | copy-start | bytes 148
  203.6 58.6 %copy-start.3 = (bf16[48,768]{1,0:T(8,128)(2,1)S(1)}, bf16[48,768]{1,0:T(8,128)(2,1)}, u32[]{:S(2)}) copy-start(bf16[48,768]{1,0:T(8,128)(2,1)} %refs_1_.2) | copy-start | bytes 221188
  203.6 58.6 %copy-start.4 = (bf16[48,768]{1,0:T(8,128)(2,1)S(1)}, bf16[48,768]{1,0:T(8,128)(2,1)}, u32[]{:S(2)}) copy-start(bf16[48,768]{1,0:T(8,128)(2,1)} %refs_2_.2) | copy-start | bytes 221188
  203.7 60.7 %copy-start.5 = (bf16[48]{0:T(256)(128)(2,1)S(1)}, bf16[48]{0:T(256)(128)(2,1)}, u32[]{:S(2)}) copy-start(bf16[48]{0:T(256)(128)(2,1)} %param.23) | copy-start | bytes 292
  267.7 3.9 %copy-start = (bf16[2048,768]{1,0:T(8,128)(2,1)S(1)}, bf16[2048,768]{1,0:T(8,128)(2,1)}, u32[]{:S(2)}) copy-start(bf16[2048,768]{1,0:T(8,128)(2,1)} %get-tuple-element.132) | copy-start | bytes 9437188
  271.6 1.7 copy-start.2
  271.6 2.5 copy-start.1
